TPU v7x, 32 devices: a whole 2x2x4 slice. The times are simulated.
32 devices in a mesh: dp: 16 (over z, y, x), seq: 2 (over core).
Axes of the slice: x: 2, y: 2, z: 4, core: 2. Of those that a mesh axis runs over, the one named last changes fastest.
Arguments:
- tokens: bfloat16 [32768, 512], P(('dp', 'seq')), may hold values from -6 to 6
- route: int32 [512], P(('dp', 'seq')), may hold values from 0 to 511, as said below
- lengths: int32 [16, 6], P('dp'), may hold values from 1 to 1024, 2048 in all within a row
- query_weight: bfloat16 [512, 512], replicated, may hold values from -0.25 to 0.25
- query_bias: bfloat16 [512], replicated, may hold values from -3 to 3
- key_weight: bfloat16 [512, 512], replicated, may hold values from -0.25 to 0.25
- value_weight: bfloat16 [512, 512], replicated, may hold values from -0.25 to 0.25
- value_bias: bfloat16 [512], replicated, may hold values from -3 to 3
- output_weight: bfloat16 [512, 512], replicated, may hold values from -2 to 2
- output_bias: bfloat16 [512], replicated, may hold values from -3 to 3
- first_gain: bfloat16 [512], replicated, may hold values from 0.5 to 1.5
- first_shift: bfloat16 [512], replicated, may hold values from -3 to 3
- up_weight: bfloat16 [512, 2048], replicated, may hold values from -0.25 to 0.25
- up_bias: bfloat16 [2048], replicated, may hold values from -3 to 3
- down_weight: bfloat16 [2048, 512], replicated, may hold values from -0.1875 to 0.1875
- down_bias: bfloat16 [512], replicated, may hold values from -3 to 3
- second_gain: bfloat16 [512], replicated, may hold values from 0.5 to 1.5
- second_shift: bfloat16 [512], replicated, may hold values from -3 to 3
- cotangent: bfloat16 [32768, 512], P(('dp', 'seq')), may hold values from -6 to 6
Outputs:
- layer_out: bfloat16 [32768, 512], P(('dp', 'seq'))
- token_grad: bfloat16 [32768, 512], P(('dp', 'seq'))
- query_weight_gradient: float32 [512, 512], replicated
- query_bias_gradient: float32 [512], replicated
- key_weight_gradient: float32 [512, 512], replicated
- value_weight_gradient: float32 [512, 512], replicated
- value_bias_gradient: float32 [512], replicated
- output_weight_gradient: float32 [512, 512], replicated
- output_bias_gradient: float32 [512], replicated
- first_gain_gradient: float32 [512], replicated
- first_shift_gradient: float32 [512], replicated
- up_weight_gradient: float32 [512, 2048], replicated
- up_bias_gradient: float32 [2048], replicated
- down_weight_gradient: float32 [2048, 512], replicated
- down_bias_gradient: float32 [512], replicated
- second_gain_gradient: float32 [512], replicated
- second_shift_gradient: float32 [512], replicated
Inputs may be any that keep to these rules, and one draw needn't show every extreme that they name: route is a permutation of the piece numbers. The device with index b of dp+seq (b = dp index * 2 + seq index) holds entries b * 16 to (b + 1) * 16 - 1, and packed piece t lies on the device with that index t // 16. Each device's 16 entries name 16 different groups, one piece for each, always on the device of the same seq index, so each device receives exactly one piece from every group. Each group's 6 lengths add up to 2048; in every group the longest is exactly 1024.
All inputs are finite; a program needn't handle non-finite values.
Results may differ from a plain program's by a relative error of at most 0.014.
The roundings to bfloat16 on the way count: a program that leaves them out, or rounds other values in their place, can miss the bound.
Values may be sent and summed in bfloat16 or wider, within the bound.
A program may use at most 256 MiB of HBM per device.

v0:
```python
import jax
import jax.numpy as jnp
from jax import lax
from jax.sharding import PartitionSpec as P

D = 512
HEADS = 8
HEAD = 64


def norm_rows(value, gain, shift):
    center = value - jnp.mean(value, axis=-1, keepdims=True)
    spread = jnp.mean(center * center, axis=-1, keepdims=True)
    return center * lax.rsqrt(spread + 1e-05) * gain + shift


def gelu_exact(value):
    return jax.nn.gelu(value, approximate=False)


def product(left, right):
    return jnp.dot(left, right, preferred_element_type=jnp.float32)


def product_left(left, right):
    return lax.dot_general(
        left, right, (((0,), (0,)), ((), ())), preferred_element_type=jnp.float32
    )


def product_right(left, right):
    return lax.dot_general(
        left, right, (((1,), (1,)), ((), ())), preferred_element_type=jnp.float32
    )


def column_sums(value):
    return jnp.sum(value.astype(jnp.float32), axis=0)


def block_scores(query_block, segment_block, key_heads, key_segment, scale):
    raw = (
        jnp.einsum("qhd,khd->hqk", query_block, key_heads, preferred_element_type=jnp.float32)
        * scale
    )
    same = segment_block[:, None] == key_segment[None, :]
    return jnp.where(same[None], raw, -jnp.inf)


def body(
    tokens,
    route,
    lengths,
    query_weight,
    query_bias,
    key_weight,
    value_weight,
    value_bias,
    output_weight,
    output_bias,
    first_gain,
    first_shift,
    up_weight,
    up_bias,
    down_weight,
    down_bias,
    second_gain,
    second_shift,
    cotangent,
):
    groups = lax.axis_size("dp")
    rows = tokens.shape[0]
    piece = rows // groups
    span = rows * lax.axis_size("seq")
    scale = HEAD ** (-0.5)
    target = route // groups // lax.axis_size("seq")
    place = route % groups
    outgoing = (
        jnp.zeros((groups, piece, D), jnp.bfloat16).at[target].set(tokens.reshape(groups, piece, D))
    )
    slots_out = jnp.zeros((groups,), jnp.int32).at[target].set(place)
    incoming, slots_in = (
        lax.all_to_all(outgoing, "dp", split_axis=0, concat_axis=0, tiled=True),
        lax.all_to_all(slots_out, "dp", split_axis=0, concat_axis=0, tiled=True),
    )
    inputs = jnp.zeros_like(incoming).at[slots_in].set(incoming).reshape(rows, D)
    bounds = jnp.cumsum(lengths[0])
    positions = jnp.arange(span, dtype=jnp.int32)
    key_segment = jnp.sum((bounds[None, :] <= positions[:, None]).astype(jnp.int32), axis=1)
    query_segment = lax.dynamic_slice_in_dim(key_segment, lax.axis_index("seq") * rows, rows)
    queries = (product(inputs, query_weight) + query_bias).astype(jnp.bfloat16)
    keys_own = product(inputs, key_weight).astype(jnp.bfloat16)
    values_own = (product(inputs, value_weight) + value_bias).astype(jnp.bfloat16)
    keyset, valueset = (
        lax.all_gather(keys_own, "seq", axis=0, tiled=True),
        lax.all_gather(values_own, "seq", axis=0, tiled=True),
    )
    block = min(512, rows)
    count_blocks = rows // block
    query_heads = queries.reshape(count_blocks, block, HEADS, HEAD)
    segment_blocks = query_segment.reshape(count_blocks, block)
    key_heads = keyset.reshape(span, HEADS, HEAD)
    value_heads = valueset.reshape(span, HEADS, HEAD)

    def attend_forward(pair):
        query_block, segment_block = pair
        scores = block_scores(query_block, segment_block, key_heads, key_segment, scale)
        top = jnp.max(scores, axis=-1, keepdims=True)
        expo = jnp.exp(scores - top)
        total = jnp.sum(expo, axis=-1, keepdims=True)
        weights_low = (expo / total).astype(jnp.bfloat16)
        mixed_block = jnp.einsum(
            "hqk,khd->qhd", weights_low, value_heads, preferred_element_type=jnp.float32
        )
        return (mixed_block, top + jnp.log(total))

    mixed_blocks, logsum = lax.map(attend_forward, (query_heads, segment_blocks))
    mixed = mixed_blocks.reshape(rows, D).astype(jnp.bfloat16)
    branch = product(mixed, output_weight) + output_bias
    residual = inputs.astype(jnp.float32) + branch
    first, first_back = jax.vjp(
        norm_rows, residual, first_gain.astype(jnp.float32), first_shift.astype(jnp.float32)
    )
    first_low = first.astype(jnp.bfloat16)
    hidden = product(first_low, up_weight) + up_bias
    active = gelu_exact(hidden).astype(jnp.bfloat16)
    update = product(active, down_weight) + down_bias
    layer_out, second_back = jax.vjp(
        norm_rows, first + update, second_gain.astype(jnp.float32), second_shift.astype(jnp.float32)
    )
    grad_second, grad_second_gain, grad_second_shift = second_back(cotangent.astype(jnp.float32))
    grad_update = grad_second.astype(jnp.bfloat16)
    again = product(first_low, up_weight) + up_bias
    active_again, gelu_back = jax.vjp(gelu_exact, again)
    active_low = active_again.astype(jnp.bfloat16)
    grad_down = product_left(active_low, grad_update)
    grad_down_bias = column_sums(grad_update)
    (grad_active,) = gelu_back(product_right(grad_update, down_weight))
    grad_hidden = grad_active.astype(jnp.bfloat16)
    grad_up = product_left(first_low, grad_hidden)
    grad_up_bias = column_sums(grad_hidden)
    grad_first = grad_second + product_right(grad_hidden, up_weight)
    grad_residual, grad_first_gain, grad_first_shift = first_back(grad_first)
    grad_branch = grad_residual.astype(jnp.bfloat16)
    grad_output = product_left(mixed, grad_branch)
    grad_output_bias = column_sums(grad_branch)
    grad_mixed = product_right(grad_branch, output_weight).astype(jnp.bfloat16)
    grad_mixed_heads = grad_mixed.reshape(count_blocks, block, HEADS, HEAD)

    def attend_back(carry, inputs_block):
        grad_key_sum, grad_value_sum = carry
        query_block, segment_block, grad_block, logsum_block = inputs_block
        scores = block_scores(query_block, segment_block, key_heads, key_segment, scale)
        weights = jnp.exp(scores - logsum_block)
        weights_low = weights.astype(jnp.bfloat16)
        grad_weights = jnp.einsum(
            "qhd,khd->hqk", grad_block, value_heads, preferred_element_type=jnp.float32
        )
        inner = jnp.sum(grad_weights * weights, axis=-1, keepdims=True)
        grad_scores = (weights * (grad_weights - inner)).astype(jnp.bfloat16)
        grad_value_sum = grad_value_sum + jnp.einsum(
            "hqk,qhd->khd", weights_low, grad_block, preferred_element_type=jnp.float32
        )
        grad_key_sum = (
            grad_key_sum
            + jnp.einsum(
                "hqk,qhd->khd", grad_scores, query_block, preferred_element_type=jnp.float32
            )
            * scale
        )
        grad_query = (
            jnp.einsum("hqk,khd->qhd", grad_scores, key_heads, preferred_element_type=jnp.float32)
            * scale
        )
        return ((grad_key_sum, grad_value_sum), grad_query)

    empty = jnp.zeros((span, HEADS, HEAD), jnp.float32)
    (key_part, value_part), grad_query_blocks = lax.scan(
        attend_back, (empty, empty), (query_heads, segment_blocks, grad_mixed_heads, logsum)
    )
    grad_keys, grad_values = (
        lax.psum_scatter(
            key_part.reshape(span, D).astype(jnp.bfloat16), "seq", scatter_dimension=0, tiled=True
        ).astype(jnp.float32),
        lax.psum_scatter(
            value_part.reshape(span, D).astype(jnp.bfloat16), "seq", scatter_dimension=0, tiled=True
        ).astype(jnp.float32),
    )
    grad_keys = grad_keys.astype(jnp.bfloat16)
    grad_values = grad_values.astype(jnp.bfloat16)
    grad_queries = grad_query_blocks.reshape(rows, D).astype(jnp.bfloat16)
    grad_query_weight = product_left(inputs, grad_queries)
    grad_query_bias = column_sums(grad_queries)
    grad_key_weight = product_left(inputs, grad_keys)
    grad_value_weight = product_left(inputs, grad_values)
    grad_value_bias = column_sums(grad_values)
    grad_inputs = (
        grad_residual
        + product_right(grad_queries, query_weight)
        + product_right(grad_keys, key_weight)
        + product_right(grad_values, value_weight)
    )
    back_rows = grad_inputs.astype(jnp.bfloat16).reshape(groups, piece, D)[slots_in]
    returned = lax.all_to_all(back_rows, "dp", split_axis=0, concat_axis=0, tiled=True)
    token_grad = returned[target].reshape(rows, D)
    local = (
        grad_query_weight,
        grad_query_bias,
        grad_key_weight,
        grad_value_weight,
        grad_value_bias,
        grad_output,
        grad_output_bias,
        grad_first_gain,
        grad_first_shift,
        grad_up,
        grad_up_bias,
        grad_down,
        grad_down_bias,
        grad_second_gain,
        grad_second_shift,
    )
    summed = lax.psum(
        (
            local[0],
            local[1],
            local[2],
            local[3],
            local[4],
            local[5],
            local[6],
            local[7],
            local[8],
            local[9],
            local[10],
            local[11],
            local[12],
            local[13],
            local[14],
        ),
        ("dp", "seq"),
    )
    return (layer_out.astype(jnp.bfloat16), token_grad) + tuple(summed)


def solution(mesh):
    placed = (
        P(("dp", "seq"), None),
        P(("dp", "seq")),
        P("dp", None),
        P(),
        P(),
        P(),
        P(),
        P(),
        P(),
        P(),
        P(),
        P(),
        P(),
        P(),
        P(),
        P(),
        P(),
        P(),
        P(("dp", "seq"), None),
    )
    return jax.shard_map(
        body,
        mesh=mesh,
        in_specs=placed,
        out_specs=(
            P(("dp", "seq"), None),
            P(("dp", "seq"), None),
            P(),
            P(),
            P(),
            P(),
            P(),
            P(),
            P(),
            P(),
            P(),
            P(),
            P(),
            P(),
            P(),
            P(),
            P(),
        ),
        check_vma=False,
    )
```

profile of v0, /device:TPU:0, one launch (start us, length us, event | category | flops | bytes accessed | tf_op | source)
XLA Modules:
  0.0 752.6 jit_solution(1640573698236095677)
XLA Ops:
  9.4 8.3 %all-to-all-start = ((s32[16,1,1]{2,1,0:T(1,128)}), s32[16,1,1]{2,1,0:T(1,128)S(1)}, u32[]{:S(2)}, u32[]{:S(2)}) async-start(s32[16,1,1]{2,1,0:T(1,128)} %copy.72), calls=%async_computation | async-start | bytes 16384 | tf_op jit(solution)/shard_map/all_to_all | solution.py:84
  24.9 4.1 all-to-all-start.1
  29.6 23.3 %all-to-all-done.1 = bf16[16,64,512]{2,1,0:T(8,128)(2,1)S(1)} async-done(((bf16[16,64,512]{2,1,0:T(8,128)(2,1)}), bf16[16,64,512]{2,1,0:T(8,128)(2,1)S(1)}, u32[]{:S(2)}, u32[]{:S(2)}) %all-to-all-start.1) | async-done | bytes 1048608 | tf_op jit(solution)/shard_map/all_to_all | solution.py:83
  70.2 4.1 reshape.333
  90.1 92.4 %while.27 = (s32[]{:T(128)}, bf16[2,512,8,64]{1,3,2,0:T(8,128)(2,1)}, f32[2,8,512,1]{2,1,3,0:T(8,128)S(1)}, s32[2,512]{1,0:T(2,128)S(1)}, s32[2048]{0:T(1024)S(1...) while((s32[]{:T(128)}, ...), condition=%wide.region_8.9_spmd, body=%wide.region_5.8_spmd.sunk | while | flops 2249191424 | bytes 110770288 | solution.py:117
  90.7 15.0 %fusion.120 = (f32[8,512]{1,0:T(8,128)S(1)}, f32[8,512,2048]{2,1,0:T(8,128)}) fusion(pred[512,2048]{1,0:T(8,128)(4,1)S(1)} %broadcast_compare_fusion.4, bf16[2048,8,64]{0,2,1:T(8,128)(2,1)} %get-tuple-element.487, bf16[2,512,8,64]{1,3,2,0:T(8,128)(2,1)} %get-tuple-element.486, s32[]{:T(128)S(6)} %copy.96), kind=kOutput, calls=%fused_computation.8.clone.1 | convolution fusion | flops 1098903552 | bytes 37240836 | tf_op jit(solution)/shard_map/while/body/eval_jaxpr/qhd,khd->hqk/dot_general | solution.py:43
  105.7 15.0 %fusion.121 = f32[8,512]{1,0:T(8,128)S(1)} fusion(f32[8,512,2048]{2,1,0:T(8,128)} %get-tuple-element.448, f32[8,512]{1,0:T(8,128)S(1)} %get-tuple-element.449, pred[512,2048]{1,0:T(8,128)(4,1)S(1)} %broadcast_compare_fusion.4), kind=kLoop, calls=%fused_computation.9.clone.1 | loop fusion | flops 33550336 | bytes 34635776 | tf_op jit(solution)/shard_map/while/body/eval_jaxpr/reduce_sum | solution.py:110
  120.7 15.5 %fusion.122 = bf16[2,512,8,64]{1,3,2,0:T(8,128)(2,1)} fusion(bf16[2,512,8,64]{1,3,2,0:T(8,128)(2,1)} %get-tuple-element.473, s32[]{:T(128)S(6)} %copy.96, bf16[2048,8,64]{0,2,1:T(8,128)(2,1)} %get-tuple-element.488, f32[8,512,2048]{2,1,0:T(8,128)} %get-tuple-element.448, f32[8,512]{1,0:T(8,128)S(1)} %fusion.121, ...), kind=kOutput, calls=%fused_computation.13.clone.1 | convolution fusion | flops 1115684864 | bytes 37781508 | tf_op jit(solution)/shard_map/while/body/eval_jaxpr/hqk,khd->qhd/dot_general | solution.py:112
  136.9 15.0 %fusion.120 = (f32[8,512]{1,0:T(8,128)S(1)}, f32[8,512,2048]{2,1,0:T(8,128)}) fusion(pred[512,2048]{1,0:T(8,128)(4,1)S(1)} %broadcast_compare_fusion.4, bf16[2048,8,64]{0,2,1:T(8,128)(2,1)} %get-tuple-element.487, bf16[2,512,8,64]{1,3,2,0:T(8,128)(2,1)} %get-tuple-element.486, s32[]{:T(128)S(6)} %copy.96), kind=kOutput, calls=%fused_computation.8.clone.1 | convolution fusion | flops 1098903552 | bytes 37240836 | tf_op jit(solution)/shard_map/while/body/eval_jaxpr/qhd,khd->hqk/dot_general | solution.py:43
  151.9 15.0 %fusion.121 = f32[8,512]{1,0:T(8,128)S(1)} fusion(f32[8,512,2048]{2,1,0:T(8,128)} %get-tuple-element.448, f32[8,512]{1,0:T(8,128)S(1)} %get-tuple-element.449, pred[512,2048]{1,0:T(8,128)(4,1)S(1)} %broadcast_compare_fusion.4), kind=kLoop, calls=%fused_computation.9.clone.1 | loop fusion | flops 33550336 | bytes 34635776 | tf_op jit(solution)/shard_map/while/body/eval_jaxpr/reduce_sum | solution.py:110
  166.9 15.5 %fusion.122 = bf16[2,512,8,64]{1,3,2,0:T(8,128)(2,1)} fusion(bf16[2,512,8,64]{1,3,2,0:T(8,128)(2,1)} %get-tuple-element.473, s32[]{:T(128)S(6)} %copy.96, bf16[2048,8,64]{0,2,1:T(8,128)(2,1)} %get-tuple-element.488, f32[8,512,2048]{2,1,0:T(8,128)} %get-tuple-element.448, f32[8,512]{1,0:T(8,128)S(1)} %fusion.121, ...), kind=kOutput, calls=%fused_computation.13.clone.1 | convolution fusion | flops 1115684864 | bytes 37781508 | tf_op jit(solution)/shard_map/while/body/eval_jaxpr/hqk,khd->qhd/dot_general | solution.py:112
  186.6 22.4 %multiply_convert_fusion.1 = (bf16[1024,2048]{1,0:T(8,128)(2,1)S(1)}, f32[1024,2048]{1,0:T(8,128)S(1)}, f32[1024,2048]{1,0:T(8,128)}) fusion(f32[2048]{0:T(1024)S(1)} %copy-done.40, bf16[512,2048]{1,0:T(8,128)(2,1)S(1)} %copy-done, f32[1024,512]{1,0:T(8,128)S(1)} %get-tuple-element.332, f32[512]{0:T(512)S(1)} %copy-done.35, f32[512]{0:T(512)S(1)} %copy-done.33, ...), kind=kOutput, calls=%fused_computation.52 | convolution fusion | flops 2288517120 | bytes 25186304 | tf_op jit(solution)/shard_map/dot_general | solution.py:22
  216.5 8.5 %convert_reduce_fusion = (f32[2048]{0:T(1024)}, bf16[1024,2048]{1,0:T(8,128)(2,1)S(1)}) fusion(f32[1024,2048]{1,0:T(8,128)S(1)} %get-tuple-element.323, bf16[1024,512]{1,0:T(8,128)(2,1)S(1)} %get-tuple-element.315, bf16[2048,512]{1,0:T(8,128)(2,1)S(1)} %copy-done.62, f32[1024,2048]{1,0:T(8,128)} %get-tuple-element.333, f32[2048]{0:T(1024)S(1)} %copy-done.40), kind=kOutput, calls=%fused_computation.50 | convolution fusion | flops 2183133184 | bytes 24133632 | tf_op jit(solution)/shard_map/dot_general | solution.py:32
  238.8 200.8 %while.28 = (s32[]{:T(128)}, f32[2048,8,64]{0,2,1:T(8,128)}, f32[2048,8,64]{0,2,1:T(8,128)}, bf16[2,512,8,64]{1,3,2,0:T(8,128)(2,1)}, bf16[2,512,8,64]{1,3,2,0:T...) while((s32[]{:T(128)}, f32[2048,8,64]{0,2,1:T(8,128)}, ...), condition=%wide.region_19.20_spmd.clone, body=%wide.region_17.19_spmd.clone.sunk | while | flops 5450756096 | bytes 347175104 | solution.py:178
  239.7 16.1 %subtract_exponential_fusion.3 = f32[8,512,2048]{2,1,0:T(8,128)} fusion(bf16[2048,8,64]{0,2,1:T(8,128)(2,1)S(1)} %get-tuple-element.523, f32[8,512]{1,0:T(8,128)S(1)} %dynamic-slice_bitcast_fusion.2, pred[512,2048]{1,0:T(8,128)(4,1)S(1)} %broadcast_compare_fusion.5, bf16[2,512,8,64]{1,3,2,0:T(8,128)(2,1)} %get-tuple-element.520, s32[]{:T(128)S(6)} %copy.106), kind=kOutput, calls=%fused_computation.24.clone.1 | convolution fusion | flops 1098907648 | bytes 37240836 | tf_op jit(solution)/shard_map/while/body/eval_jaxpr/qhd,khd->hqk/dot_general | solution.py:43
  255.8 15.8 %bitcast_add_fusion.5 = f32[2048,8,64]{0,2,1:T(8,128)} fusion(f32[2048,8,64]{0,2,1:T(8,128)} %get-tuple-element.505, f32[8,512,2048]{2,1,0:T(8,128)} %subtract_exponential_fusion.3, pred[]{:T(512)S(6)} %compare.8, bf16[2,512,8,64]{1,3,2,0:T(8,128)(2,1)} %get-tuple-element.525, s32[]{:T(128)S(6)} %copy.106), kind=kOutput, calls=%fused_computation.27.clone.1 | convolution fusion | flops 1084227584 | bytes 42467332 | tf_op jit(solution)/shard_map/while/body/eval_jaxpr/hqk,qhd->khd/dot_general | solution.py:161
  271.5 22.1 %multiply_reduce_fusion.6 = (f32[8,512]{1,0:T(8,128)S(1)}, f32[8,512,2048]{2,1,0:T(8,128)}) fusion(f32[8,512,2048]{2,1,0:T(8,128)} %subtract_exponential_fusion.3, bf16[2048,8,64]{0,2,1:T(8,128)(2,1)} %get-tuple-element.526, bf16[2,512,8,64]{1,3,2,0:T(8,128)(2,1)} %get-tuple-element.525, s32[]{:T(128)S(6)} %copy.106), kind=kOutput, calls=%fused_computation.23.clone.1 | convolution fusion | flops 1090514944 | bytes 69746688 | tf_op jit(solution)/shard_map/while/body/eval_jaxpr/qhd,khd->hqk/dot_general | solution.py:156
  293.6 27.5 %multiply_convert_fusion.3 = bf16[8,512,2048]{2,1,0:T(8,128)(2,1)} fusion(f32[8,512,2048]{2,1,0:T(8,128)} %subtract_exponential_fusion.3, f32[8,512,2048]{2,1,0:T(8,128)} %get-tuple-element.461, f32[8,512]{1,0:T(8,128)S(1)} %get-tuple-element.462), kind=kLoop, calls=%fused_computation.22.clone.1 | loop fusion | flops 25165824 | bytes 83902464 | tf_op jit(solution)/shard_map/while/body/eval_jaxpr/convert_element_type | solution.py:160
  321.0 9.7 %fusion.132 = bf16[2,512,8,64]{1,3,2,0:T(8,128)(2,1)} fusion(bf16[2,512,8,64]{1,3,2,0:T(8,128)(2,1)} %get-tuple-element.506, s32[]{:T(128)S(6)} %copy.106, bf16[8,512,2048]{2,1,0:T(8,128)(2,1)} %multiply_convert_fusion.3, bf16[2048,8,64]{0,2,1:T(8,128)(2,1)S(1)} %get-tuple-element.523), kind=kOutput, calls=%fused_computation.32.clone.1 | convolution fusion | flops 1074003968 | bytes 19922948 | tf_op jit(solution)/shard_map/while/body/eval_jaxpr/hqk,khd->qhd/dot_general | solution.py:172
  331.8 6.2 bitcast_add_fusion.4
  338.6 16.1 %subtract_exponential_fusion.3 = f32[8,512,2048]{2,1,0:T(8,128)} fusion(bf16[2048,8,64]{0,2,1:T(8,128)(2,1)S(1)} %get-tuple-element.523, f32[8,512]{1,0:T(8,128)S(1)} %dynamic-slice_bitcast_fusion.2, pred[512,2048]{1,0:T(8,128)(4,1)S(1)} %broadcast_compare_fusion.5, bf16[2,512,8,64]{1,3,2,0:T(8,128)(2,1)} %get-tuple-element.520, s32[]{:T(128)S(6)} %copy.106), kind=kOutput, calls=%fused_computation.24.clone.1 | convolution fusion | flops 1098907648 | bytes 37240836 | tf_op jit(solution)/shard_map/while/body/eval_jaxpr/qhd,khd->hqk/dot_general | solution.py:43
  354.7 17.0 %bitcast_add_fusion.5 = f32[2048,8,64]{0,2,1:T(8,128)} fusion(f32[2048,8,64]{0,2,1:T(8,128)} %get-tuple-element.505, f32[8,512,2048]{2,1,0:T(8,128)} %subtract_exponential_fusion.3, pred[]{:T(512)S(6)} %compare.8, bf16[2,512,8,64]{1,3,2,0:T(8,128)(2,1)} %get-tuple-element.525, s32[]{:T(128)S(6)} %copy.106), kind=kOutput, calls=%fused_computation.27.clone.1 | convolution fusion | flops 1084227584 | bytes 42467332 | tf_op jit(solution)/shard_map/while/body/eval_jaxpr/hqk,qhd->khd/dot_general | solution.py:161
  371.7 22.1 %multiply_reduce_fusion.6 = (f32[8,512]{1,0:T(8,128)S(1)}, f32[8,512,2048]{2,1,0:T(8,128)}) fusion(f32[8,512,2048]{2,1,0:T(8,128)} %subtract_exponential_fusion.3, bf16[2048,8,64]{0,2,1:T(8,128)(2,1)} %get-tuple-element.526, bf16[2,512,8,64]{1,3,2,0:T(8,128)(2,1)} %get-tuple-element.525, s32[]{:T(128)S(6)} %copy.106), kind=kOutput, calls=%fused_computation.23.clone.1 | convolution fusion | flops 1090514944 | bytes 69746688 | tf_op jit(solution)/shard_map/while/body/eval_jaxpr/qhd,khd->hqk/dot_general | solution.py:156
  393.7 27.5 %multiply_convert_fusion.3 = bf16[8,512,2048]{2,1,0:T(8,128)(2,1)} fusion(f32[8,512,2048]{2,1,0:T(8,128)} %subtract_exponential_fusion.3, f32[8,512,2048]{2,1,0:T(8,128)} %get-tuple-element.461, f32[8,512]{1,0:T(8,128)S(1)} %get-tuple-element.462), kind=kLoop, calls=%fused_computation.22.clone.1 | loop fusion | flops 25165824 | bytes 83902464 | tf_op jit(solution)/shard_map/while/body/eval_jaxpr/convert_element_type | solution.py:160
  421.2 9.7 %fusion.132 = bf16[2,512,8,64]{1,3,2,0:T(8,128)(2,1)} fusion(bf16[2,512,8,64]{1,3,2,0:T(8,128)(2,1)} %get-tuple-element.506, s32[]{:T(128)S(6)} %copy.106, bf16[8,512,2048]{2,1,0:T(8,128)(2,1)} %multiply_convert_fusion.3, bf16[2048,8,64]{0,2,1:T(8,128)(2,1)S(1)} %get-tuple-element.523), kind=kOutput, calls=%fused_computation.32.clone.1 | convolution fusion | flops 1074003968 | bytes 19922948 | tf_op jit(solution)/shard_map/while/body/eval_jaxpr/hqk,khd->qhd/dot_general | solution.py:172
  431.9 7.5 bitcast_add_fusion.4
  448.9 4.0 fusion.60
  454.8 4.5 fusion.61
  459.3 4.7 fusion.46
  481.1 6.9 all-to-all-start.2
  488.6 58.2 %all-reduce = (f32[512]{0:T(512)}, f32[512]{0:T(512)}, f32[512]{0:T(512)}, f32[512]{0:T(512)}, f32[512]{0:T(512)}, /*index=5*/f32[2048]{0:T(1024)}, f32[512]{0:T(512)}, f32[512]{0:T(512)}, f32[512]{0:T(512)}) all-reduce(f32[512]{0:T(512)S(1)} %reduce_sum.224, ...), channel_id=1, replica_groups=mesh['dp'=16,'seq'=2] {'dp','seq'}, use_global_device_ids=true, to_apply=%region_24.25 | all-reduce | flops 6144 | bytes 49152 | tf_op jit(solution)/shard_map/psum | solution.py:223
  548.3 185.1 %all-reduce.4.cloned.1.call-done = (f32[512,512]{1,0:T(8,128)}, f32[512,512]{1,0:T(8,128)}, f32[512,512]{1,0:T(8,128)}, f32[512,512]{1,0:T(8,128)}, f32[512,2048]{1,0:T(8,128)}, /*index=5*/f32[2048,512]{1,0:T(8,128)}) async-done(((f32[512,512]{1,0:T(8,128)}, f32[512,512]{1,0:T(8,128)}, f32[512,512]{1,0:T(8,128)}, f32[512,512]{1,0:T(8,128)}, f32[512,2048]{1,0:T(8,128)}, /*index=5*/f32[2048,512]{1,0:T(8,128)}), ...) | async-done | bytes 12582928 | tf_op jit(solution)/shard_map/psum | solution.py:223
  (243 shorter events, 115.2 us)
Async XLA Ops:
  7.2 179.4 %copy-start = (bf16[512,2048]{1,0:T(8,128)(2,1)S(1)}, bf16[512,2048]{1,0:T(8,128)(2,1)}, u32[]{:S(2)}) copy-start(bf16[512,2048]{1,0:T(8,128)(2,1)} %param.35) | copy-start | bytes 6291460
  7.2 21.9 %copy-start.54 = (bf16[512]{0:T(512)(128)(2,1)S(1)}, bf16[512]{0:T(512)(128)(2,1)}, u32[]{:S(2)}) copy-start(bf16[512]{0:T(512)(128)(2,1)} %param.30) | copy-start | bytes 3076
  8.0 16.9 %copy-start.50 = (s32[16]{0:T(128)}, s32[16]{0:T(128)S(1)}, u32[]{:S(2)}) copy-start(s32[16]{0:T(128)S(1)} %get-tuple-element.330) | copy-start | bytes 196
  9.4 15.6 %all-to-all-start = ((s32[16,1,1]{2,1,0:T(1,128)}), s32[16,1,1]{2,1,0:T(1,128)S(1)}, u32[]{:S(2)}, u32[]{:S(2)}) async-start(s32[16,1,1]{2,1,0:T(1,128)} %copy.72), calls=%async_computation | async-start | bytes 16384 | tf_op jit(solution)/shard_map/all_to_all | solution.py:84
  24.9 27.9 %all-to-all-start.1 = ((bf16[16,64,512]{2,1,0:T(8,128)(2,1)}), bf16[16,64,512]{2,1,0:T(8,128)(2,1)S(1)}, u32[]{:S(2)}, u32[]{:S(2)}) async-start(bf16[16,64,512]{2,1,0:T(8,128)(2,1)} %scatter_fusion), calls=%async_computation.1 | async-start | bytes 2097152 | tf_op jit(solution)/shard_map/all_to_all | solution.py:83
  29.1 48.5 %all-gather.5.cloned.1.call-start = ((), (), s32[]{:S(2)}) async-start(), calls=%async_computation.6 | async-start | bytes 3145728 | tf_op jit(solution)/shard_map/all_gather | solution.py:96
  29.5 30.6 %copy-start.52 = (s32[16]{0:T(128)}, s32[16]{0:T(128)S(1)}, u32[]{:S(2)}) copy-start(s32[16]{0:T(128)S(1)} %fusion.43) | copy-start | bytes 196
  57.0 8.6 %copy-start.60 = (bf16[512]{0:T(512)(128)(2,1)S(1)}, bf16[512]{0:T(512)(128)(2,1)}, u32[]{:S(2)}) copy-start(bf16[512]{0:T(512)(128)(2,1)} %param.38) | copy-start | bytes 3076
  57.0 9.2 %copy-start.61 = (bf16[512]{0:T(512)(128)(2,1)S(1)}, bf16[512]{0:T(512)(128)(2,1)}, u32[]{:S(2)}) copy-start(bf16[512]{0:T(512)(128)(2,1)} %param.40) | copy-start | bytes 3076
  57.0 9.9 %copy-start.45 = (bf16[2048]{0:T(1024)(128)(2,1)S(1)}, bf16[2048]{0:T(1024)(128)(2,1)}, u32[]{:S(2)}) copy-start(bf16[2048]{0:T(1024)(128)(2,1)} %param.36) | copy-start | bytes 12292
  60.1 24.9 %all-gather.3.cloned.1.call-start = ((), (), s32[]{:S(2)}) async-start(), calls=%async_computation.5 | async-start | bytes 3145728 | tf_op jit(solution)/shard_map/all_gather | solution.py:95
  62.9 401.0 %reduce-scatter.3.cloned.1.call-start = ((), (), s32[]{:S(2)}) async-start(), calls=%async_computation.7 | async-start | bytes 3145728 | tf_op jit(solution)/shard_map/reduce_scatter | solution.py:182
  186.1 42.4 %copy-start.4 = (f32[1024,512]{1,0:T(8,128)}, f32[1024,512]{1,0:T(8,128)S(1)}, u32[]{:S(2)}) copy-start(f32[1024,512]{1,0:T(8,128)S(1)} %get-tuple-element.332) | copy-start | bytes 6291460
  186.1 42.4 %copy-start.27 = (f32[1024]{0:T(1024)}, f32[1024]{0:T(1024)S(1)}, u32[]{:S(2)}) copy-start(f32[1024]{0:T(1024)S(1)} %broadcast_multiply_fusion.1) | copy-start | bytes 12292
  186.6 42.0 %copy-start.29 = (f32[1024]{0:T(1024)}, f32[1024]{0:T(1024)S(1)}, u32[]{:S(2)}) copy-start(f32[1024]{0:T(1024)S(1)} %fusion.41) | copy-start | bytes 12292
  186.6 22.4 %copy-start.48 = (f32[512]{0:T(512)S(1)}, f32[512]{0:T(512)}, u32[]{:S(2)}) copy-start(f32[512]{0:T(512)} %convert_element_type.141) | copy-start | bytes 6148
  186.6 22.4 %copy-start.62 = (bf16[2048,512]{1,0:T(8,128)(2,1)S(1)}, bf16[2048,512]{1,0:T(8,128)(2,1)}, u32[]{:S(2)}) copy-start(bf16[2048,512]{1,0:T(8,128)(2,1)} %param.37) | copy-start | bytes 6291460
  216.5 8.5 %copy-start.21 = (bf16[1024,512]{1,0:T(8,128)(2,1)}, bf16[1024,512]{1,0:T(8,128)(2,1)S(1)}, u32[]{:S(2)}) copy-start(bf16[1024,512]{1,0:T(8,128)(2,1)S(1)} %get-tuple-element.315) | copy-start | bytes 3145732
  321.0 10.7 %copy-start.2 = (bf16[8,512,2048]{2,1,0:T(8,128)(2,1)S(1)}, bf16[8,512,2048]{2,1,0:T(8,128)(2,1)}, u32[]{:S(2)}) copy-start(bf16[8,512,2048]{2,1,0:T(8,128)(2,1)} %multiply_convert_fusion.3) | copy-start | bytes 50331652 | tf_op jit(solution)/shard_map/while
  421.2 10.7 %copy-start.2 = (bf16[8,512,2048]{2,1,0:T(8,128)(2,1)S(1)}, bf16[8,512,2048]{2,1,0:T(8,128)(2,1)}, u32[]{:S(2)}) copy-start(bf16[8,512,2048]{2,1,0:T(8,128)(2,1)} %multiply_convert_fusion.3) | copy-start | bytes 50331652 | tf_op jit(solution)/shard_map/while
  443.5 24.0 %reduce-scatter.5.cloned.1.call-start = ((), (), s32[]{:S(2)}) async-start(), calls=%async_computation.8 | async-start | bytes 3145728 | tf_op jit(solution)/shard_map/reduce_scatter | solution.py:185
  447.5 285.9 %all-reduce.4.cloned.1.call-start = ((), (), s32[]{:S(2)}) async-start(), calls=%async_computation.9 | async-start | bytes 25165824 | tf_op jit(solution)/shard_map/psum | solution.py:223
  478.1 9.9 %copy-start.51 = (s32[16]{0:T(128)S(1)}, s32[16]{0:T(128)}, u32[]{:S(2)}) copy-start(s32[16]{0:T(128)} %copy-done.50) | copy-start | bytes 196
  478.1 10.2 %copy-start.19 = (bf16[1024,512]{0,1:T(8,128)(2,1)S(1)}, bf16[1024,512]{0,1:T(8,128)(2,1)}, u32[]{:S(2)}) copy-start(bf16[1024,512]{0,1:T(8,128)(2,1)} %reduce-scatter.5.cloned.1.call-done) | copy-start | bytes 3145732
  478.1 10.4 %copy-start.39 = (f32[2048]{0:T(1024)S(1)}, f32[2048]{0:T(1024)}, u32[]{:S(2)}) copy-start(f32[2048]{0:T(1024)} %get-tuple-element.337) | copy-start | bytes 24580
  478.1 10.4 %copy-start.41 = (f32[512]{0:T(512)S(1)}, f32[512]{0:T(512)}, u32[]{:S(2)}) copy-start(f32[512]{0:T(512)} %get-tuple-element.257) | copy-start | bytes 6148
  478.1 10.4 %copy-start.42 = (f32[512]{0:T(512)S(1)}, f32[512]{0:T(512)}, u32[]{:S(2)}) copy-start(f32[512]{0:T(512)} %get-tuple-element.260) | copy-start | bytes 6148
  478.1 10.4 %copy-start.43 = (f32[512]{0:T(512)S(1)}, f32[512]{0:T(512)}, u32[]{:S(2)}) copy-start(f32[512]{0:T(512)} %get-tuple-element.314) | copy-start | bytes 6148
  478.1 10.4 %copy-start.44 = (f32[512]{0:T(512)S(1)}, f32[512]{0:T(512)}, u32[]{:S(2)}) copy-start(f32[512]{0:T(512)} %get-tuple-element.316) | copy-start | bytes 6148
  478.2 10.4 %copy-start.46 = (f32[512]{0:T(512)S(1)}, f32[512]{0:T(512)}, u32[]{:S(2)}) copy-start(f32[512]{0:T(512)} %get-tuple-element.255) | copy-start | bytes 6148
  478.2 10.4 %copy-start.47 = (f32[512]{0:T(512)S(1)}, f32[512]{0:T(512)}, u32[]{:S(2)}) copy-start(f32[512]{0:T(512)} %get-tuple-element.259) | copy-start | bytes 6148
  481.1 65.7 %all-to-all-start.2 = ((bf16[16,64,512]{2,1,0:T(8,128)(2,1)}), bf16[16,64,512]{2,1,0:T(8,128)(2,1)S(1)}, u32[]{:S(2)}, u32[]{:S(2)}) async-start(bf16[16,64,512]{2,1,0:T(8,128)(2,1)} %gather_fusion), calls=%async_computation.4 | async-start | bytes 2097152 | tf_op jit(solution)/shard_map/all_to_all | solution.py:204
  (44 other events, 183.2 us)
Sparse Core Ops, SparseCore 0:
  60.2 10.8 all-gather.4
  73.3 11.7 all-gather.2
  443.6 10.7 reduce-scatter.2
  456.6 10.8 reduce-scatter.4
  474.9 258.4 all-reduce.3
where the time goes:
time: 758 us; the launch traced here: 753 us
  matrix products  279 us (37%)
  waiting for transfers between devices  215 us (28%)
  other arithmetic  108 us (14%)
  blocking collectives  58.2 us (8%)
  local copies, waits for them, and re-layouts  57.7 us (8%)
  starting transfers between devices  19.6 us (3%)
  between operations  14.9 us (2%)
    psum x1, waiting for transfers between devices, body(): lax.psum((local[0], local[1], local[2], local[3], local[4], local[5], loc...  185 us
    dot_general x4, matrix products, block_scores(): jnp.einsum('qhd,khd->hqk', query_block, key_heads, preferred_element_type...  62.2 us
    psum x1, blocking collectives, body(): lax.psum((local[0], local[1], local[2], local[3], local[4], local[5], loc...  58.2 us
    convert_element_type x2, other arithmetic, attend_back(): grad_scores = (weights * (grad_weights - inner)).astype(jnp.bfloat16)  54.9 us
    dot_general x2, matrix products, attend_back(): jnp.einsum('qhd,khd->hqk', grad_block, value_heads, preferred_element_typ...  44.1 us
    dot_general x6, matrix products, product(): return jnp.dot(left, right, preferred_element_type=jnp.float32)  34.6 us
    dot_general x2, matrix products, attend_back(): jnp.einsum('hqk,qhd->khd', weights_low, grad_block, preferred_element_typ...  32.7 us
    dot_general x2, matrix products, attend_forward(): jnp.einsum('hqk,khd->qhd', weights_low, value_heads, preferred_element_ty...  31.1 us
  transfers between devices with their start and end apart: 8, of which 5 were waited for; matrix products, arithmetic and copies ran while one was open for 8% of the time, Pallas kernels for 0%

commit v1 on v0

v1 whole, which is shorter than its diff:
```python
import functools

import jax
import jax.numpy as jnp
from jax import lax
from jax.experimental import pallas as pl
from jax.experimental.pallas import tpu as pltpu
from jax.sharding import PartitionSpec as P

D = 512
HEADS = 8
HEAD = 64
HL = HEADS // 2
C = HL * HEAD
PAIR = 128
NEG = -1e30
BQ = 256
BK = 256
F32 = jnp.float32
BF16 = jnp.bfloat16
MESH = pl.DeviceIdType.MESH
VMEM = pltpu.VMEM
SMEM = pltpu.SMEM


def norm_rows(value, gain, shift):
    center = value - jnp.mean(value, axis=-1, keepdims=True)
    spread = jnp.mean(center * center, axis=-1, keepdims=True)
    return center * lax.rsqrt(spread + 1e-05) * gain + shift


def gelu_exact(value):
    return jax.nn.gelu(value, approximate=False)


def product(left, right):
    return jnp.dot(left, right, preferred_element_type=F32)


def product_left(left, right):
    return lax.dot_general(left, right, (((0,), (0,)), ((), ())), preferred_element_type=F32)


def product_right(left, right):
    return lax.dot_general(left, right, (((1,), (1,)), ((), ())), preferred_element_type=F32)


def column_sums(value):
    return jnp.sum(value.astype(F32), axis=0)


def swap_kernel(x_ref, o_ref, send, recv, local):
    dp, me = lax.axis_index("dp"), lax.axis_index("seq")
    other = 1 - me
    barrier = pltpu.get_barrier_semaphore()
    pl.semaphore_signal(barrier, inc=1, device_id=(dp, other), device_id_type=MESH)
    pl.semaphore_wait(barrier, 1)
    whole = len(x_ref.shape) == 2
    copy = pltpu.make_async_remote_copy(
        src_ref=x_ref if whole else x_ref.at[other],
        dst_ref=o_ref.at[me],
        send_sem=send,
        recv_sem=recv,
        device_id=(dp, other),
        device_id_type=MESH,
    )
    copy.start()
    own = pltpu.make_async_copy(x_ref if whole else x_ref.at[me], o_ref.at[me], local)
    own.start()
    own.wait()
    copy.wait()


def swap(x, collective_id):
    shape = x.shape if x.ndim == 3 else (2,) + x.shape
    return pl.pallas_call(
        swap_kernel,
        out_shape=jax.ShapeDtypeStruct(shape, x.dtype),
        in_specs=[pl.BlockSpec(memory_space=VMEM)],
        out_specs=pl.BlockSpec(memory_space=VMEM),
        scratch_shapes=[pltpu.SemaphoreType.DMA] * 3,
        compiler_params=pltpu.CompilerParams(collective_id=collective_id, has_side_effects=True),
    )(x)


def table_starts(bounds_ref, position):
    start = jnp.zeros_like(position)
    end = None
    for j in range(bounds_ref.shape[0]):
        b = bounds_ref[j]
        start = jnp.where(b <= position, b, start)
    for j in range(bounds_ref.shape[0] - 1, -1, -1):
        b = bounds_ref[j]
        end = jnp.where(b > position, b, end if end is not None else b)
    return start, end


def head_masks():
    lane = lax.broadcasted_iota(jnp.int32, (1, PAIR), 1)
    low = (lane < HEAD).astype(F32).astype(BF16)
    return low, (lane >= HEAD).astype(F32).astype(BF16)


def block_range(bounds_ref, i):
    start, _ = table_starts(bounds_ref, i * BQ)
    _, end = table_starts(bounds_ref, i * BQ + BQ - 1)
    return start // BK, (end + BK - 1) // BK


def tile_mask(bounds_ref, i):
    pos = i * BQ + lax.broadcasted_iota(jnp.int32, (1, BQ), 1)
    return table_starts(bounds_ref, pos)


def forward_kernel(
    bounds_ref, me_ref, x_ref, wq_ref, wk_ref, wv_ref, bq_ref, bv_ref,
    q_ref, k_ref, v_ref, mixed_ref, out_ref, lse_ref,
    vt_ref, acc_ref,
):
    span = x_ref.shape[0]
    blocks = span // BQ

    def project(i, _):
        rows = pl.ds(pl.multiple_of(i * BQ, BQ), BQ)
        x = x_ref[rows, :]
        q = (product(x, wq_ref[...]) + bq_ref[...].astype(F32)).astype(BF16)
        q_ref[rows, :] = (q.astype(F32) * (HEAD**-0.5)).astype(BF16)
        k_ref[rows, :] = product(x, wk_ref[...]).astype(BF16)
        v = (product(x, wv_ref[...]) + bv_ref[...].astype(F32)).astype(BF16)
        v_ref[rows, :] = v
        vt_ref[:, rows] = v.T
        return 0

    lax.fori_loop(0, blocks, project, 0)
    masks = head_masks()

    def query_block(i, _):
        rows = pl.ds(pl.multiple_of(i * BQ, BQ), BQ)
        lo, hi = block_range(bounds_ref, i)
        start, end = tile_mask(bounds_ref, i)
        q = q_ref[rows, :]
        heads = [q[:, (h // 2) * PAIR : (h // 2 + 1) * PAIR] * masks[h % 2] for h in range(HL)]
        acc_ref[...] = jnp.zeros_like(acc_ref)

        def key_block(j, carry):
            keys = pl.ds(pl.multiple_of(j * BK, BK), BK)
            kpos = j * BK + lax.broadcasted_iota(jnp.int32, (BK, BQ), 0)
            mask = (kpos >= start) & (kpos < end)
            tops, totals = carry
            new_tops, new_totals = [], []
            for h in range(HL):
                kp = k_ref[keys, (h // 2) * PAIR : (h // 2 + 1) * PAIR]
                s = jnp.where(mask, product_right(kp, heads[h]), NEG)
                top = jnp.maximum(tops[h], jnp.max(s, axis=0, keepdims=True))
                p = jnp.exp(s - top)
                alpha = jnp.exp(tops[h] - top)
                new_totals.append(totals[h] * alpha + jnp.sum(p, axis=0, keepdims=True))
                new_tops.append(top)
                lanes = slice(h * HEAD, (h + 1) * HEAD)
                acc_ref[lanes, :] = acc_ref[lanes, :] * alpha + product(
                    vt_ref[lanes, keys], p.astype(BF16)
                )
            return tuple(new_tops), tuple(new_totals)

        tops = tuple(jnp.full((1, BQ), NEG, F32) for _ in range(HL))
        totals = tuple(jnp.zeros((1, BQ), F32) for _ in range(HL))
        tops, totals = lax.fori_loop(lo, hi, key_block, (tops, totals))
        for h in range(HL):
            lanes = slice(h * HEAD, (h + 1) * HEAD)
            acc_ref[lanes, :] = acc_ref[lanes, :] / totals[h]
            lse_ref[h : h + 1, rows] = tops[h] + jnp.log(totals[h])
        out = acc_ref[...]
        out_ref[:, rows] = out
        mixed_ref[rows, :] = out.T.astype(BF16)
        return 0

    lax.fori_loop(0, blocks, query_block, 0)


def column_block(shape):
    return pl.BlockSpec(shape, lambda i, bounds, me: (0, me[0]))


def whole_block(shape):
    return pl.BlockSpec(shape, lambda i, bounds, me: (0,) * len(shape))


def attend_forward(x_all, bounds, me, wq, wk, wv, bq, bv):
    span = x_all.shape[0]
    rows_shape = jax.ShapeDtypeStruct((span, C), BF16)
    return pl.pallas_call(
        forward_kernel,
        grid_spec=pltpu.PrefetchScalarGridSpec(
            num_scalar_prefetch=2,
            grid=(1,),
            in_specs=[
                whole_block((span, D)),
                column_block((D, C)),
                column_block((D, C)),
                column_block((D, C)),
                column_block((1, C)),
                column_block((1, C)),
            ],
            out_specs=[whole_block((span, C))] * 4 + [whole_block((C, span)), whole_block((8, span))],
            scratch_shapes=[VMEM((C, span), BF16), VMEM((C, BQ), F32)],
        ),
        out_shape=[rows_shape] * 4
        + [jax.ShapeDtypeStruct((C, span), F32), jax.ShapeDtypeStruct((8, span), F32)],
        name="attend_forward",
    )(bounds, me, x_all, wq, wk, wv, bq.reshape(1, D), bv.reshape(1, D))


def backward_kernel(
    bounds_ref, me_ref, x_ref, q_ref, k_ref, v_ref, g_ref, out_ref, lse_ref, wq_ref, wk_ref, wv_ref,
    gw_ref, sums_ref, gx_ref,
    kt_ref, gq_ref, gk_ref, gv_ref, gqt_ref,
):
    span = x_ref.shape[0]
    blocks = span // BQ
    scale = HEAD**-0.5

    def prepare(i, _):
        rows = pl.ds(pl.multiple_of(i * BQ, BQ), BQ)
        kt_ref[:, rows] = k_ref[rows, :].T
        gk_ref[rows, :] = jnp.zeros((BQ, C), F32)
        gv_ref[rows, :] = jnp.zeros((BQ, C), F32)
        return 0

    lax.fori_loop(0, blocks, prepare, 0)
    masks = head_masks()

    def query_block(i, _):
        rows = pl.ds(pl.multiple_of(i * BQ, BQ), BQ)
        lo, hi = block_range(bounds_ref, i)
        start, end = tile_mask(bounds_ref, i)
        q = q_ref[rows, :]
        g = g_ref[rows, :]
        pairs = [slice((h // 2) * PAIR, (h // 2 + 1) * PAIR) for h in range(HL)]
        queries = [q[:, pairs[h]] * masks[h % 2] for h in range(HL)]
        grads = [g[:, pairs[h]] * masks[h % 2] for h in range(HL)]
        weighted = g.astype(F32).T * out_ref[:, rows]
        inner = [
            jnp.sum(weighted[h * HEAD : (h + 1) * HEAD], axis=0, keepdims=True) for h in range(HL)
        ]
        logsum = [lse_ref[h : h + 1, rows] for h in range(HL)]
        gqt_ref[...] = jnp.zeros_like(gqt_ref)

        def key_block(j, _):
            keys = pl.ds(pl.multiple_of(j * BK, BK), BK)
            kpos = j * BK + lax.broadcasted_iota(jnp.int32, (BK, BQ), 0)
            mask = (kpos >= start) & (kpos < end)
            for p in range(HL // 2):
                lanes = slice(p * PAIR, (p + 1) * PAIR)
                kp, vp = k_ref[keys, lanes], v_ref[keys, lanes]
                gk = gk_ref[keys, lanes]
                gv = gv_ref[keys, lanes]
                for h in (2 * p, 2 * p + 1):
                    s = product_right(kp, queries[h])
                    w = jnp.where(mask, jnp.exp(s - logsum[h]), 0.0)
                    gw = product_right(vp, grads[h])
                    gs = (w * (gw - inner[h])).astype(BF16)
                    gv = gv + product(w.astype(BF16), grads[h])
                    gk = gk + product(gs, queries[h])
                    part = slice(h * HEAD, (h + 1) * HEAD)
                    gqt_ref[part, :] += product(kt_ref[part, keys], gs)
                gk_ref[keys, lanes] = gk
                gv_ref[keys, lanes] = gv
            return 0

        lax.fori_loop(lo, hi, key_block, 0)
        gq_ref[rows, :] = (gqt_ref[...].T * scale).astype(BF16)
        return 0

    lax.fori_loop(0, blocks, query_block, 0)

    wide = span // 4

    def tail(i, _):
        rows = pl.ds(pl.multiple_of(i * wide, wide), wide)
        gq, gk, gv = gq_ref[rows, :], gk_ref[rows, :].astype(BF16), gv_ref[rows, :].astype(BF16)
        gx = product_right(gq, wq_ref[...]) + product_right(gk, wk_ref[...])
        gx_ref[rows, :] = (gx + product_right(gv, wv_ref[...])).astype(BF16)
        x = x_ref[rows, :]
        for n, part in enumerate((gq, gk, gv)):
            term = product_left(x, part)
            gw_ref[n] = jnp.where(i == 0, term, gw_ref[n] + term)
        sums = jnp.concatenate(
            [jnp.sum(a.astype(F32), axis=0, keepdims=True) for a in (gq, gv)], axis=1
        )
        sums_ref[...] = jnp.where(i == 0, sums, sums_ref[...] + sums)
        return 0

    lax.fori_loop(0, 4, tail, 0)


def attend_backward(bounds, me, x_all, q, k, v, g, out, lse, wq, wk, wv):
    span = x_all.shape[0]
    rows = whole_block((span, C))
    return pl.pallas_call(
        backward_kernel,
        grid_spec=pltpu.PrefetchScalarGridSpec(
            num_scalar_prefetch=2,
            grid=(1,),
            in_specs=[whole_block((span, D)), rows, rows, rows, rows]
            + [whole_block((C, span)), whole_block((8, span))]
            + [column_block((D, C))] * 3,
            out_specs=[whole_block((3, D, C)), whole_block((1, 2 * C)), whole_block((span, D))],
            scratch_shapes=[
                VMEM((C, span), BF16),
                VMEM((span, C), BF16),
                VMEM((span, C), F32),
                VMEM((span, C), F32),
                VMEM((C, BQ), F32),
            ],
        ),
        out_shape=[
            jax.ShapeDtypeStruct((3, D, C), F32),
            jax.ShapeDtypeStruct((1, 2 * C), F32),
            jax.ShapeDtypeStruct((span, D), BF16),
        ],
        name="attend_backward",
    )(bounds, me, x_all, q, k, v, g, out, lse, wq, wk, wv)


def sum_plan(n):
    weights = []
    w = 1
    while w < n:
        weights.append(w)
        w *= 2
    first = list(weights)
    second = list(weights)
    second[0], second[1] = second[1], second[0]
    return list(zip(first, second))


def rows_add(acc, base, other, size, into):
    step = min(size, 64 if acc.shape[-1] > 1024 else 128)

    def add(i, _):
        here = pl.ds(pl.multiple_of(base + i * step, 16), step)
        there = pl.ds(pl.multiple_of(i * step, step), step)
        into[here, :] = (acc[here, :].astype(F32) + other[there, :].astype(F32)).astype(acc.dtype)
        return 0

    lax.fori_loop(0, size // step, add, 0)


def sum_kernel(n, count, *refs):
    ins = refs[: count + 2]
    outs = refs[count + 2 : 2 * count + 4]
    accs = refs[2 * count + 4 : 3 * count + 5]
    recvs = refs[3 * count + 5 : 4 * count + 6]
    fulls = refs[4 * count + 6 : 5 * count + 7]
    handed, vec_recv, send, recv = refs[5 * count + 7 :]
    shared, own_in, vec_in = ins[:count], ins[count], ins[count + 1]
    dp, me = lax.axis_index("dp"), lax.axis_index("seq")
    plan = sum_plan(n)

    def peer(weights):
        w = weights[0] + me * (weights[1] - weights[0])
        bit = (dp // w) % 2
        return dp + (1 - 2 * bit) * w, bit

    barrier = pltpu.get_barrier_semaphore()
    for a, b in plan:
        w = a
        bit = (dp // w) % 2
        pl.semaphore_signal(
            barrier, inc=1, device_id=(dp + (1 - 2 * bit) * w, me), device_id_type=MESH
        )
    pl.semaphore_signal(barrier, inc=1, device_id=(dp, 1 - me), device_id_type=MESH)
    pl.semaphore_wait(barrier, len(plan) + 1)

    def push(src, dst, chunk, stage, device):
        return pltpu.make_async_remote_copy(
            src_ref=src,
            dst_ref=dst,
            send_sem=send.at[chunk, stage],
            recv_sem=recv.at[chunk, stage],
            device_id=device,
            device_id_type=MESH,
        )

    def chunk_steps(c):
        acc, landing, full = accs[c], recvs[c], fulls[c]
        rows = acc.shape[0]
        paired = c < count
        steps = []
        state = {"base": 0, "size": rows, "copy": None, "offset": 0, "stage": 0, "kept": []}

        def send_half(device, bit):
            half = state["size"] // 2
            keep = state["base"] + bit * half
            give = state["base"] + (1 - bit) * half
            src = acc.at[pl.ds(pl.multiple_of(give, 16), half), :]
            dst = landing.at[pl.ds(state["offset"], half), :]
            copy = push(src, dst, c, state["stage"], device)
            copy.start()
            state["copy"] = (copy, keep, half, state["offset"])
            state["kept"].append((keep, half, device))
            state["stage"] += 1

        def finish_half(into=acc):
            copy, keep, half, offset = state["copy"]
            copy.wait()
            rows_add(acc, keep, landing.at[pl.ds(offset, half), :], half, into)
            state["base"], state["size"], state["offset"] = keep, half, offset + half

        def first():
            if paired:
                send_half((dp, 1 - me), me)
            else:
                device, bit = peer(plan[0])
                send_half((device, me), bit)

        steps.append(first)
        rest = plan if paired else plan[1:]
        for weights in rest:

            def onward(weights=weights):
                finish_half()
                device, bit = peer(weights)
                send_half((device, me), bit)

            steps.append(onward)

        def gather(last):
            def run():
                if not last:
                    finish_half(full)
                    state["back"] = list(reversed(state["kept"]))
                else:
                    state["copy"].wait()
                    state["back"].pop(0)
                keep, half, device = state["back"][0]
                region = full.at[pl.ds(pl.multiple_of(keep, 16), half), :]
                copy = push(region, region, c, state["stage"], device)
                copy.start()
                state["copy"] = copy
                state["stage"] += 1

            return run

        for g in range(len(rest) + 1):
            steps.append(gather(g > 0))
        if not paired:

            def hand_over():
                state["copy"].wait()
                copy = push(full, handed, c, state["stage"], (dp, 1 - me))
                copy.start()
                state["copy"] = copy

            steps.append(hand_over)

        def close():
            state["copy"].wait()
            if paired:
                out = outs[c]
                step = 128 if acc.shape[1] <= 512 else 32

                def widen(i, _):
                    here = pl.ds(pl.multiple_of(i * step, step), step)
                    out[here, :] = full[here, :].astype(F32)
                    return 0

                lax.fori_loop(0, rows // step, widen, 0)
            else:
                out = outs[c]
                third = acc.shape[1] // 3
                for w in range(3):
                    for source, half in ((full, me), (handed, 1 - me)):
                        lanes = pl.ds(pl.multiple_of(half * third, third), third)
                        out[w, :, lanes] = source[0:rows, w * third : (w + 1) * third].astype(F32)

        steps.append(close)
        return steps

    vec_out = outs[count + 1]

    def vec_steps():
        state = {}
        steps = []
        peers = [(dp, 1 - me)]
        for a, _ in plan:
            bit = (dp // a) % 2
            peers.append((dp + (1 - 2 * bit) * a, me))
        for s, device in enumerate(peers):

            def run(s=s, device=device):
                if s == 0:
                    vec_out[...] = vec_in[...]
                else:
                    state["copy"].wait()
                    vec_out[...] += vec_recv[s - 1]
                sent = vec_recv.at[len(peers) + s]
                sent[...] = vec_out[...]
                copy = push(sent, vec_recv.at[s], count + 1, s, device)
                copy.start()
                state["copy"] = copy

            steps.append(run)

        def close():
            state["copy"].wait()
            vec_out[...] += vec_recv[len(peers) - 1]

        steps.append(close)
        return steps

    for c in range(count + 1):
        source = shared[c] if c < count else own_in
        acc = accs[c]
        step = min(64, acc.shape[0])

        def load(i, _, acc=acc, source=source, step=step):
            here = pl.ds(pl.multiple_of(i * step, step), step)
            acc[here, :] = source[here, :].astype(BF16)
            return 0

        lax.fori_loop(0, acc.shape[0] // step, load, 0)

    lines = [chunk_steps(c) for c in range(count + 1)] + [vec_steps()]
    ticks = max(len(line) + at for at, line in enumerate(lines))
    for t in range(ticks):
        for at, line in enumerate(lines):
            if 0 <= t - at < len(line):
                line[t - at]()


def sum_gradients(shared, own, vec, n, collective_id):
    count = len(shared)
    stages = 2 * len(sum_plan(n)) + 3
    accs = [VMEM(a.shape, BF16) for a in shared] + [VMEM(own.shape, BF16)]
    vmem = pl.BlockSpec(memory_space=VMEM)
    return pl.pallas_call(
        functools.partial(sum_kernel, n, count),
        out_shape=[jax.ShapeDtypeStruct(a.shape, F32) for a in shared]
        + [jax.ShapeDtypeStruct((3, own.shape[0], 2 * own.shape[1] // 3), F32)]
        + [jax.ShapeDtypeStruct(vec.shape, F32)],
        in_specs=[vmem] * (count + 2),
        out_specs=[vmem] * (count + 2),
        scratch_shapes=accs
        + accs
        + accs
        + [
            VMEM(own.shape, BF16),
            VMEM((2 * len(sum_plan(n)) + 2,) + vec.shape, F32),
            pltpu.SemaphoreType.DMA((count + 2, stages)),
            pltpu.SemaphoreType.DMA((count + 2, stages)),
        ],
        compiler_params=pltpu.CompilerParams(
            collective_id=collective_id, has_side_effects=True, vmem_limit_bytes=60 << 20
        ),
        name="sum_gradients",
    )(*shared, own, vec)


def body(
    tokens,
    route,
    lengths,
    query_weight,
    query_bias,
    key_weight,
    value_weight,
    value_bias,
    output_weight,
    output_bias,
    first_gain,
    first_shift,
    up_weight,
    up_bias,
    down_weight,
    down_bias,
    second_gain,
    second_shift,
    cotangent,
):
    groups = lax.axis_size("dp")
    rows = tokens.shape[0]
    piece = rows // groups
    span = rows * lax.axis_size("seq")
    seq = lax.axis_index("seq")
    target = route // groups // lax.axis_size("seq")
    place = route % groups
    outgoing = jnp.zeros((groups, piece, D), BF16).at[target].set(tokens.reshape(groups, piece, D))
    slots_out = jnp.zeros((groups,), jnp.int32).at[target].set(place)
    incoming, slots_in = (
        lax.all_to_all(outgoing, "dp", split_axis=0, concat_axis=0, tiled=True),
        lax.all_to_all(slots_out, "dp", split_axis=0, concat_axis=0, tiled=True),
    )
    inputs = jnp.zeros_like(incoming).at[slots_in].set(incoming).reshape(rows, D)
    bounds = jnp.cumsum(lengths[0]).astype(jnp.int32)
    me = seq.reshape(1).astype(jnp.int32)
    x_all = swap(inputs, 0).reshape(span, D)
    q, k, v, mixed_all, attend_out, lse = attend_forward(
        x_all, bounds, me, query_weight, key_weight, value_weight, query_bias, value_bias
    )
    mixed_halves = swap(mixed_all.reshape(2, rows, C), 1)
    mixed = jnp.concatenate([mixed_halves[0], mixed_halves[1]], axis=1)
    branch = product(mixed, output_weight) + output_bias
    residual = inputs.astype(F32) + branch
    first, first_back = jax.vjp(
        norm_rows, residual, first_gain.astype(F32), first_shift.astype(F32)
    )
    first_low = first.astype(BF16)
    hidden = product(first_low, up_weight) + up_bias
    active = gelu_exact(hidden).astype(BF16)
    update = product(active, down_weight) + down_bias
    layer_out, second_back = jax.vjp(
        norm_rows, first + update, second_gain.astype(F32), second_shift.astype(F32)
    )
    grad_second, grad_second_gain, grad_second_shift = second_back(cotangent.astype(F32))
    grad_update = grad_second.astype(BF16)
    again = product(first_low, up_weight) + up_bias
    active_again, gelu_back = jax.vjp(gelu_exact, again)
    active_low = active_again.astype(BF16)
    grad_down = product_left(active_low, grad_update)
    grad_down_bias = column_sums(grad_update)
    (grad_active,) = gelu_back(product_right(grad_update, down_weight))
    grad_hidden = grad_active.astype(BF16)
    grad_up = product_left(first_low, grad_hidden)
    grad_up_bias = column_sums(grad_hidden)
    grad_first = grad_second + product_right(grad_hidden, up_weight)
    grad_residual, grad_first_gain, grad_first_shift = first_back(grad_first)
    grad_branch = grad_residual.astype(BF16)
    grad_output = product_left(mixed, grad_branch)
    grad_output_bias = column_sums(grad_branch)
    grad_mixed = product_right(grad_branch, output_weight).astype(BF16)
    grad_halves = jnp.stack([grad_mixed[:, :C], grad_mixed[:, C:]])
    grad_mixed_all = swap(grad_halves, 2).reshape(span, C)
    grad_columns, column_parts, grad_x = attend_backward(
        bounds, me, x_all, q, k, v, grad_mixed_all, attend_out, lse,
        query_weight, key_weight, value_weight,
    )
    grad_parts = swap(grad_x.reshape(2, rows, D), 3)
    grad_inputs = grad_residual + grad_parts[0].astype(F32) + grad_parts[1].astype(F32)
    back_rows = grad_inputs.astype(BF16).reshape(groups, piece, D)[slots_in]
    returned = lax.all_to_all(back_rows, "dp", split_axis=0, concat_axis=0, tiled=True)
    token_grad = returned[target].reshape(rows, D)

    def own_columns(part):
        return lax.dynamic_update_slice(jnp.zeros((1, D), F32), part, (0, seq * C))

    vec = jnp.concatenate(
        [
            own_columns(column_parts[:, :C]),
            own_columns(column_parts[:, C:]),
            jnp.stack(
                [
                    grad_output_bias,
                    grad_first_gain,
                    grad_first_shift,
                    grad_down_bias,
                    grad_second_gain,
                    grad_second_shift,
                ]
            ),
            grad_up_bias.reshape(-1, D),
            jnp.zeros((4, D), F32),
        ]
    )
    if groups == 16:
        up_sum, down_sum, out_sum, columns, vec = sum_gradients(
            [grad_up, grad_down, grad_output],
            jnp.concatenate([grad_columns[0], grad_columns[1], grad_columns[2]], axis=1),
            vec, groups, 4,
        )
        query_sum, key_sum, value_sum = columns[0], columns[1], columns[2]
    else:
        up_sum, down_sum, out_sum, vec = lax.psum((grad_up, grad_down, grad_output, vec), ("dp", "seq"))
        columns = lax.all_gather(lax.psum(grad_columns, "dp"), "seq", axis=2, tiled=True)
        query_sum, key_sum, value_sum = columns[0], columns[1], columns[2]
    return (
        layer_out.astype(BF16),
        token_grad,
        query_sum,
        vec[0],
        key_sum,
        value_sum,
        vec[1],
        out_sum,
        vec[2],
        vec[3],
        vec[4],
        up_sum,
        vec[8:12].reshape(-1),
        down_sum,
        vec[5],
        vec[6],
        vec[7],
    )


def solution(mesh):
    both, one = P(("dp", "seq"), None), P()
    return jax.shard_map(
        body,
        mesh=mesh,
        in_specs=(both, P(("dp", "seq")), P("dp", None)) + (one,) * 15 + (both,),
        out_specs=(both, both) + (one,) * 15,
        check_vma=False,
    )
```

time: 758 us -> 369 us (0.49)
  matrix products: 279 us -> 50.3 us
  Pallas kernels: 0 us -> 201 us
  waiting for transfers between devices: 215 us -> 24.1 us
  other arithmetic: 108 us -> 13.4 us
  blocking collectives: 58.2 us -> 0 us
  starting transfers between devices: 19.6 us -> 42.3 us
  local copies, waits for them, and re-layouts: 57.7 us -> 35.5 us
  between operations: 14.9 us -> 1.17 us
    dot_general x20 -> x3, matrix products: 238 us -> 25.4 us  [product(): return jnp.dot(left, right, preferred_element_type=F32)]
    pallas_call x0 -> x7, Pallas kernels: none -> 201 us  [the longest x1 95.2 us: sum_gradients(): pl.pallas_call(functools.partial(sum_kernel, n, count), out_shape=[jax.Sh...]
    psum x1 -> x0, waiting for transfers between devices: 185 us -> none  [body(): lax.psum((local[0], local[1], local[2], local[3], local[4], local[5], loc...]
    convert_element_type x10 -> x5, other arithmetic: 65 us -> 2.63 us  [the longest x1 2.61 us: body(): back_rows = grad_inputs.astype(BF16).reshape(groups, piece, D)[slots_in]]
    psum x1 -> x0, blocking collectives: 58.2 us -> none  [body(): lax.psum((local[0], local[1], local[2], local[3], local[4], local[5], loc...]
    reduce_sum x7 -> x2, other arithmetic: 32.4 us -> 0.52 us  [column_sums(): return jnp.sum(value.astype(F32), axis=0)]
    all_to_all x1, starting transfers between devices: 6.91 us -> 29.6 us  [body(): lax.all_to_all(back_rows, 'dp', split_axis=0, concat_axis=0, tiled=True)]
    dot_general x6 -> x3, matrix products: 21.6 us -> 13.3 us  [product_left(): lax.dot_general(left, right, (((0,), (0,)), ((), ())), preferred_element_...]
  transfers between devices with their start and end apart: 8 -> 3, of which waited for: 5 -> 2; matrix products, arithmetic and copies ran while one was open for 8% -> 9% of each run, Pallas kernels for 0% -> 26%
where the time goes in v1:
time: 369 us; the launch traced here: 367 us
  Pallas kernels  201 us (54%)
  matrix products  50.3 us (14%)
  starting transfers between devices  42.3 us (11%)
  local copies, waits for them, and re-layouts  35.5 us (10%)
  waiting for transfers between devices  24.1 us (7%)
  other arithmetic  13.4 us (4%)
    pallas_call x1, Pallas kernels, sum_gradients(): pl.pallas_call(functools.partial(sum_kernel, n, count), out_shape=[jax.Sh...  95.2 us
    pallas_call x1, Pallas kernels, attend_forward(): pl.pallas_call(forward_kernel, grid_spec=pltpu.PrefetchScalarGridSpec(num...  43.8 us
    pallas_call x1, Pallas kernels, attend_backward(): pl.pallas_call(backward_kernel, grid_spec=pltpu.PrefetchScalarGridSpec(nu...  42.5 us
    all_to_all x1, starting transfers between devices, body(): lax.all_to_all(back_rows, 'dp', split_axis=0, concat_axis=0, tiled=True)  29.6 us
    dot_general x3, matrix products, product(): return jnp.dot(left, right, preferred_element_type=F32)  25.4 us
    all_to_all x1, waiting for transfers between devices, body(): lax.all_to_all(outgoing, 'dp', split_axis=0, concat_axis=0, tiled=True)  21.4 us
    pallas_call x4, Pallas kernels, swap(): pl.pallas_call(swap_kernel, out_shape=jax.ShapeDtypeStruct(shape, x.dtype...  19.2 us
    dot_general x3, matrix products, product_left(): lax.dot_general(left, right, (((0,), (0,)), ((), ())), preferred_element_...  13.3 us
  transfers between devices with their start and end apart: 3, of which 2 were waited for; matrix products, arithmetic and copies ran while one was open for 9% of the time, Pallas kernels for 26%

profile of v1, /device:TPU:0, one launch (start us, length us, event | category | flops | bytes accessed | tf_op | source)
XLA Modules:
  0.0 367.5 jit_solution(2015700257537403839)
XLA Ops:
  2.8 8.3 %all-to-all-start = ((s32[16,1,1]{2,1,0:T(1,128)}), s32[16,1,1]{2,1,0:T(1,128)S(1)}, u32[]{:S(2)}, u32[]{:S(2)}) async-start(s32[16,1,1]{2,1,0:T(1,128)} %copy.37), calls=%async_computation | async-start | bytes 16384 | tf_op jit(solution)/shard_map/all_to_all | solution.py:592
  12.3 3.4 scatter_fusion
  15.7 2.7 all-to-all-done
  18.4 4.3 %all-to-all-start.1 = ((bf16[16,64,512]{2,1,0:T(8,128)(2,1)}), bf16[16,64,512]{2,1,0:T(8,128)(2,1)}, u32[]{:S(2)}, u32[]{:S(2)}) async-start(bf16[16,64,512]{2,1,0:T(8,128)(2,1)} %scatter_fusion), calls=%async_computation.1 | async-start | bytes 2097152 | tf_op jit(solution)/shard_map/all_to_all | solution.py:591
  25.1 21.4 %all-to-all-done.1 = bf16[16,64,512]{2,1,0:T(8,128)(2,1)} async-done(((bf16[16,64,512]{2,1,0:T(8,128)(2,1)}), bf16[16,64,512]{2,1,0:T(8,128)(2,1)}, u32[]{:S(2)}, u32[]{:S(2)}) %all-to-all-start.1) | async-done | bytes 1048608 | tf_op jit(solution)/shard_map/all_to_all | solution.py:591
  46.6 2.3 scatter_fusion.1
  49.9 5.2 %shard_map.314 = bf16[2,1024,512]{2,1,0:T(8,128)(2,1)} custom-call(bf16[1024,512]{1,0:T(8,128)(2,1)} %bitcast.75), custom_call_target="tpu_custom_call" | custom-call | tf_op jit(solution)/shard_map/pallas_call | solution.py:76
  55.1 43.8 %attend_forward.1 = (bf16[2048,256]{1,0:T(8,128)(2,1)}, bf16[2048,256]{1,0:T(8,128)(2,1)}, bf16[2048,256]{1,0:T(8,128)(2,1)}, bf16[2048,256]{1,0:T(8,128)(2,1)}, f32[256,2048]{1,0:T(8,128)}, /*index=5*/f32[8,2048]{1,0:T(8,128)}) custom-call(s32[6]{0:T(128)} %bitcast.98, s32[1]{0:T(128)} %bitcast.6.me_ref, bf16[2048,512]{1,0:T(8,128)(2,1)} %bitcast.73, ...), custom_call_target="tpu_custom_call" | custom-call | tf_op jit(solution)/shard_map/attend_forward/pallas_call | solution.py:191
  98.9 4.2 %shard_map.315 = bf16[2,1024,256]{2,1,0:T(8,128)(2,1)} custom-call(bf16[2,1024,256]{2,1,0:T(8,128)(2,1)} %bitcast.82), custom_call_target="tpu_custom_call" | custom-call | tf_op jit(solution)/shard_map/pallas_call | solution.py:76
  105.8 21.9 %multiply_convert_fusion = (bf16[1024,2048]{1,0:T(8,128)(2,1)S(1)}, f32[1024,2048]{1,0:T(8,128)S(1)}, f32[1024,2048]{1,0:T(8,128)}) fusion(f32[2048]{0:T(1024)S(1)} %convert_element_type.79, bf16[512,2048]{1,0:T(8,128)(2,1)S(1)} %copy-done, f32[1024,512]{1,0:T(8,128)S(1)} %get-tuple-element.83, f32[512]{0:T(512)S(1)} %convert_element_type.77, ...), kind=kOutput, calls=%fused_computation.9 | convolution fusion | flops 2288517120 | bytes 25186304 | tf_op jit(solution)/shard_map/dot_general | solution.py:37
  127.7 2.7 fusion.29
  132.6 2.0 fusion.25
  134.9 7.9 %convert_reduce_fusion = (f32[2048]{0:T(1024)S(1)}, bf16[1024,2048]{1,0:T(8,128)(2,1)S(1)}) fusion(f32[1024,2048]{1,0:T(8,128)S(1)} %get-tuple-element.60, bf16[1024,512]{1,0:T(8,128)(2,1)S(1)} %get-tuple-element.52, bf16[2048,512]{1,0:T(8,128)(2,1)S(1)} %copy-done.21, f32[1024,2048]{1,0:T(8,128)} %get-tuple-element.84, f32[2048]{0:T(1024)S(1)} %convert_element_type.79), kind=kOutput, calls=%fused_computation.7 | convolution fusion | flops 2183133184 | bytes 24133632 | tf_op jit(solution)/shard_map/dot_general | solution.py:45
  142.7 3.0 multiply_reduce_fusion
  148.0 1.7 fusion.12.refs_2_
  150.8 4.1 %shard_map.316 = bf16[2,1024,256]{2,1,0:T(8,128)(2,1)} custom-call(bf16[2,1024,256]{2,1,0:T(8,128)(2,1)} %pad_maximum_fusion.2.x_ref), custom_call_target="tpu_custom_call" | custom-call | tf_op jit(solution)/shard_map/pallas_call | solution.py:76
  155.0 42.5 %attend_backward.1 = (f32[3,512,256]{2,1,0:T(8,128)}, f32[1,512]{1,0:T(1,128)}, bf16[2048,512]{1,0:T(8,128)(2,1)}) custom-call(s32[6]{0:T(128)} %bitcast.99, s32[1]{0:T(128)} %bitcast.6.me_ref, bf16[2048,512]{1,0:T(8,128)(2,1)} %bitcast.74, bf16[2048,256]{1,0:T(8,128)(2,1)} %get-tuple-element.32.q_ref, bf16[2048,256]{1,0:T(8,128)(2,1)} %get-tuple-element.33.k_ref, ...), custom_call_target="tpu_custom_call" | custom-call | tf_op jit(solution)/shard_map/attend_backward/pallas_call | solution.py:299
  197.5 5.6 %shard_map.317 = bf16[2,1024,512]{2,1,0:T(8,128)(2,1)} custom-call(bf16[2,1024,512]{2,1,0:T(8,128)(2,1)} %bitcast.79), custom_call_target="tpu_custom_call" | custom-call | tf_op jit(solution)/shard_map/pallas_call | solution.py:76
  203.1 2.6 fusion.10
  205.7 1.6 gather_fusion
  207.3 29.6 %all-to-all-start.2 = ((bf16[16,64,512]{2,1,0:T(8,128)(2,1)}), bf16[16,64,512]{2,1,0:T(8,128)(2,1)S(1)}, u32[]{:S(2)}, u32[]{:S(2)}) async-start(bf16[16,64,512]{2,1,0:T(8,128)(2,1)} %gather_fusion), calls=%async_computation.2 | async-start | bytes 2097152 | tf_op jit(solution)/shard_map/all_to_all | solution.py:641
  236.9 2.5 slice_bitcast_fusion.7
  239.5 2.6 pad_maximum_fusion.refs_3_
  243.4 6.9 %fusion.30.refs_1_ = f32[2048,512]{1,0:T(8,128)} fusion(bf16[1024,2048]{1,0:T(8,128)(2,1)} %copy-done.24, bf16[1024,512]{1,0:T(8,128)(2,1)} %copy-done.10), kind=kOutput, calls=%fused_computation.102 | convolution fusion | flops 2147483648 | bytes 9437184 | tf_op jit(solution)/shard_map/dot_general | solution.py:41
  250.3 4.7 %fusion.20.refs_0_ = f32[512,2048]{1,0:T(8,128)} fusion(bf16[1024,2048]{1,0:T(8,128)(2,1)S(1)} %copy-done.5, f32[1024,512]{1,0:T(8,128)S(1)} %copy-done.2, f32[512]{0:T(512)S(1)} %convert_element_type.77, f32[512]{0:T(512)S(1)} %convert_element_type.76, f32[1024]{0:T(1024)S(1)} %fusion.13, f32[1024]{0:T(1024)S(1)} %broadcast_multiply_fusion.1), kind=kOutput, calls=%fused_computation.95 | convolution fusion | flops 2150105088 | bytes 10498048 | tf_op jit(solution)/shard_map/dot_general | solution.py:41
  255.0 95.2 %sum_gradients.1 = (f32[512,2048]{1,0:T(8,128)}, f32[2048,512]{1,0:T(8,128)}, f32[512,512]{1,0:T(8,128)}, f32[3,512,512]{2,1,0:T(8,128)}, f32[16,512]{1,0:T(8,128)}) custom-call(f32[512,2048]{1,0:T(8,128)} %fusion.20.refs_0_, f32[2048,512]{1,0:T(8,128)} %fusion.30.refs_1_, f32[512,512]{1,0:T(8,128)} %fusion.12.refs_2_, f32[512,768]{1,0:T(8,128)} %pad_maximum_fusion.refs_3_, ...), custom_call_target="tpu_custom_call" | custom-call | tf_op jit(solution)/shard_map/sum_gradients/pallas_call | solution.py:537
  351.5 1.6 fusion.27
  353.2 3.6 slice_bitcast_fusion
  356.8 1.6 gather_fusion.1
  358.3 2.3 copy.46
  360.6 4.8 %copy.47 = f32[512,2048]{1,0:T(8,128)} copy(f32[512,2048]{1,0:T(8,128)} %get-tuple-element.118) | data formatting | bytes 8388608
  365.4 2.0 copy.48
  (98 shorter events, 17.6 us)
Async XLA Ops:
  0.7 105.1 %copy-start = (bf16[512,2048]{1,0:T(8,128)(2,1)S(1)}, bf16[512,2048]{1,0:T(8,128)(2,1)}, u32[]{:S(2)}) copy-start(bf16[512,2048]{1,0:T(8,128)(2,1)} %param.31) | copy-start | bytes 6291460
  2.8 15.6 %all-to-all-start = ((s32[16,1,1]{2,1,0:T(1,128)}), s32[16,1,1]{2,1,0:T(1,128)S(1)}, u32[]{:S(2)}, u32[]{:S(2)}) async-start(s32[16,1,1]{2,1,0:T(1,128)} %copy.37), calls=%async_computation | async-start | bytes 16384 | tf_op jit(solution)/shard_map/all_to_all | solution.py:592
  12.2 10.5 %copy-start.13 = (bf16[512]{0:T(512)(128)(2,1)S(1)}, bf16[512]{0:T(512)(128)(2,1)}, u32[]{:S(2)}) copy-start(bf16[512]{0:T(512)(128)(2,1)} %param.34) | copy-start | bytes 3076
  12.2 10.5 %copy-start.11 = (bf16[2048]{0:T(1024)(128)(2,1)S(1)}, bf16[2048]{0:T(1024)(128)(2,1)}, u32[]{:S(2)}) copy-start(bf16[2048]{0:T(1024)(128)(2,1)} %param.32) | copy-start | bytes 12292
  12.2 10.5 %copy-start.14 = (bf16[512]{0:T(512)(128)(2,1)S(1)}, bf16[512]{0:T(512)(128)(2,1)}, u32[]{:S(2)}) copy-start(bf16[512]{0:T(512)(128)(2,1)} %param.28) | copy-start | bytes 3076
  12.2 10.6 %copy-start.23 = (s32[1,6]{1,0:T(1,128)S(1)}, s32[1,6]{1,0:T(1,128)}, u32[]{:S(2)}) copy-start(s32[1,6]{1,0:T(1,128)} %param.21) | copy-start | bytes 76
  12.2 11.3 %copy-start.15 = (bf16[512]{0:T(512)(128)(2,1)S(1)}, bf16[512]{0:T(512)(128)(2,1)}, u32[]{:S(2)}) copy-start(bf16[512]{0:T(512)(128)(2,1)} %param.23) | copy-start | bytes 3076
  12.2 11.8 %copy-start.16 = (bf16[512]{0:T(512)(128)(2,1)S(1)}, bf16[512]{0:T(512)(128)(2,1)}, u32[]{:S(2)}) copy-start(bf16[512]{0:T(512)(128)(2,1)} %param.26) | copy-start | bytes 3076
  12.3 12.4 %copy-start.17 = (bf16[512]{0:T(512)(128)(2,1)S(1)}, bf16[512]{0:T(512)(128)(2,1)}, u32[]{:S(2)}) copy-start(bf16[512]{0:T(512)(128)(2,1)} %param.30) | copy-start | bytes 3076
  12.3 12.4 %copy-start.18 = (bf16[512]{0:T(512)(128)(2,1)S(1)}, bf16[512]{0:T(512)(128)(2,1)}, u32[]{:S(2)}) copy-start(bf16[512]{0:T(512)(128)(2,1)} %param.29) | copy-start | bytes 3076
  12.3 12.4 %copy-start.19 = (bf16[512]{0:T(512)(128)(2,1)S(1)}, bf16[512]{0:T(512)(128)(2,1)}, u32[]{:S(2)}) copy-start(bf16[512]{0:T(512)(128)(2,1)} %param.35) | copy-start | bytes 3076
  12.3 12.4 %copy-start.20 = (bf16[512]{0:T(512)(128)(2,1)S(1)}, bf16[512]{0:T(512)(128)(2,1)}, u32[]{:S(2)}) copy-start(bf16[512]{0:T(512)(128)(2,1)} %param.36) | copy-start | bytes 3076
  18.4 28.1 %all-to-all-start.1 = ((bf16[16,64,512]{2,1,0:T(8,128)(2,1)}), bf16[16,64,512]{2,1,0:T(8,128)(2,1)}, u32[]{:S(2)}, u32[]{:S(2)}) async-start(bf16[16,64,512]{2,1,0:T(8,128)(2,1)} %scatter_fusion), calls=%async_computation.1 | async-start | bytes 2097152 | tf_op jit(solution)/shard_map/all_to_all | solution.py:591
  48.9 1.0 copy-start.6
  98.9 5.6 %copy-start.7 = (bf16[16,64,512]{2,1,0:T(8,128)(2,1)S(1)}, bf16[16,64,512]{2,1,0:T(8,128)(2,1)}, u32[]{:S(2)}) copy-start(bf16[16,64,512]{2,1,0:T(8,128)(2,1)} %copy-done.6) | copy-start | bytes 3145732
  103.1 1.4 copy-start.22
  105.3 40.5 %copy-start.1 = (f32[1024,512]{1,0:T(8,128)}, f32[1024,512]{1,0:T(8,128)S(1)}, u32[]{:S(2)}) copy-start(f32[1024,512]{1,0:T(8,128)S(1)} %get-tuple-element.83) | copy-start | bytes 6291460
  105.8 21.9 %copy-start.21 = (bf16[2048,512]{1,0:T(8,128)(2,1)S(1)}, bf16[2048,512]{1,0:T(8,128)(2,1)}, u32[]{:S(2)}) copy-start(bf16[2048,512]{1,0:T(8,128)(2,1)} %param.33) | copy-start | bytes 6291460
  127.7 2.7 copy-start.24
  130.4 1.2 copy-start.9
  134.8 7.9 %copy-start.10 = (bf16[1024,512]{1,0:T(8,128)(2,1)}, bf16[1024,512]{1,0:T(8,128)(2,1)S(1)}, u32[]{:S(2)}) copy-start(bf16[1024,512]{1,0:T(8,128)(2,1)S(1)} %get-tuple-element.52) | copy-start | bytes 3145732
  142.7 3.0 copy-start.4
  146.6 1.4 copy-start.3
  207.3 149.5 %all-to-all-start.2 = ((bf16[16,64,512]{2,1,0:T(8,128)(2,1)}), bf16[16,64,512]{2,1,0:T(8,128)(2,1)S(1)}, u32[]{:S(2)}, u32[]{:S(2)}) async-start(bf16[16,64,512]{2,1,0:T(8,128)(2,1)} %gather_fusion), calls=%async_computation.2 | async-start | bytes 2097152 | tf_op jit(solution)/shard_map/all_to_all | solution.py:641
  236.9 2.6 copy-start.12
  243.4 7.0 %copy-start.2 = (f32[1024,512]{1,0:T(8,128)S(1)}, f32[1024,512]{1,0:T(8,128)}, u32[]{:S(2)}) copy-start(f32[1024,512]{1,0:T(8,128)} %copy-done.1) | copy-start | bytes 6291460
  243.4 7.0 %copy-start.5 = (bf16[1024,2048]{1,0:T(8,128)(2,1)S(1)}, bf16[1024,2048]{1,0:T(8,128)(2,1)}, u32[]{:S(2)}) copy-start(bf16[1024,2048]{1,0:T(8,128)(2,1)} %copy-done.4) | copy-start | bytes 12582916
  360.6 4.9 %copy-start.8 = (f32[2048,512]{1,0:T(8,128)S(1)}, f32[2048,512]{1,0:T(8,128)}, u32[]{:S(2)}) copy-start(f32[2048,512]{1,0:T(8,128)} %get-tuple-element.120) | copy-start | bytes 12582916

commit v2 on v1

v2 whole, which is shorter than its diff:
```python
import functools

import jax
import jax.numpy as jnp
from jax import lax
from jax.experimental import pallas as pl
from jax.experimental.pallas import tpu as pltpu
from jax.sharding import PartitionSpec as P

D = 512
HEADS = 8
HEAD = 64
HL = HEADS // 2
C = HL * HEAD
PAIR = 128
NEG = -1e30
LOG2E = 1.4426950408889634
BQ = 256
BK = 256
F32 = jnp.float32
BF16 = jnp.bfloat16
MESH = pl.DeviceIdType.MESH
VMEM = pltpu.VMEM
SMEM = pltpu.SMEM


def norm_rows(value, gain, shift):
    center = value - jnp.mean(value, axis=-1, keepdims=True)
    spread = jnp.mean(center * center, axis=-1, keepdims=True)
    return center * lax.rsqrt(spread + 1e-05) * gain + shift


def gelu_exact(value):
    return jax.nn.gelu(value, approximate=False)


def product(left, right):
    return jnp.dot(left, right, preferred_element_type=F32)


def product_left(left, right):
    return lax.dot_general(left, right, (((0,), (0,)), ((), ())), preferred_element_type=F32)


def product_right(left, right):
    return lax.dot_general(left, right, (((1,), (1,)), ((), ())), preferred_element_type=F32)


def column_sums(value):
    return jnp.sum(value.astype(F32), axis=0)


def swap_kernel(x_ref, o_ref, send, recv, local):
    dp, me = lax.axis_index("dp"), lax.axis_index("seq")
    other = 1 - me
    barrier = pltpu.get_barrier_semaphore()
    pl.semaphore_signal(barrier, inc=1, device_id=(dp, other), device_id_type=MESH)
    pl.semaphore_wait(barrier, 1)
    whole = len(x_ref.shape) == 2
    copy = pltpu.make_async_remote_copy(
        src_ref=x_ref if whole else x_ref.at[other],
        dst_ref=o_ref.at[me],
        send_sem=send,
        recv_sem=recv,
        device_id=(dp, other),
        device_id_type=MESH,
    )
    copy.start()
    own = pltpu.make_async_copy(x_ref if whole else x_ref.at[me], o_ref.at[me], local)
    own.start()
    own.wait()
    copy.wait()


def swap(x, collective_id):
    shape = x.shape if x.ndim == 3 else (2,) + x.shape
    return pl.pallas_call(
        swap_kernel,
        out_shape=jax.ShapeDtypeStruct(shape, x.dtype),
        in_specs=[pl.BlockSpec(memory_space=VMEM)],
        out_specs=pl.BlockSpec(memory_space=VMEM),
        scratch_shapes=[pltpu.SemaphoreType.DMA] * 3,
        compiler_params=pltpu.CompilerParams(collective_id=collective_id, has_side_effects=True),
    )(x)


def table_starts(bounds_ref, position):
    start = jnp.zeros_like(position)
    end = None
    for j in range(bounds_ref.shape[0]):
        b = bounds_ref[j]
        start = jnp.where(b <= position, b, start)
    for j in range(bounds_ref.shape[0] - 1, -1, -1):
        b = bounds_ref[j]
        end = jnp.where(b > position, b, end if end is not None else b)
    return start, end


def head_masks():
    lane = lax.broadcasted_iota(jnp.int32, (1, PAIR), 1)
    low = (lane < HEAD).astype(F32).astype(BF16)
    return low, (lane >= HEAD).astype(F32).astype(BF16)


def block_range(bounds_ref, i):
    start, first_end = table_starts(bounds_ref, i * BQ)
    last_start, end = table_starts(bounds_ref, i * BQ + BQ - 1)
    lo, hi = start // BK, (end + BK - 1) // BK
    a, b = (last_start + BK - 1) // BK, first_end // BK
    some = a < b
    return lo, jnp.where(some, a, hi), jnp.where(some, b, hi), hi


def tile_mask(bounds_ref, i):
    pos = i * BQ + lax.broadcasted_iota(jnp.int32, (1, BQ), 1)
    return table_starts(bounds_ref, pos)


def three_loops(ranges, run, carry):
    lo, a, b, hi = ranges
    carry = lax.fori_loop(lo, a, functools.partial(run, True), carry)
    carry = lax.fori_loop(a, b, functools.partial(run, False), carry)
    return lax.fori_loop(b, hi, functools.partial(run, True), carry)


def by_eight(value, op):
    return op(value.reshape(value.shape[0] // 8, 8, value.shape[1]), axis=0)


def forward_kernel(
    pieces, bounds_ref, me_ref, slot_ref, loaded_ref, wq_ref, wk_ref, wv_ref, bq_ref, bv_ref,
    q_ref, k_ref, v_ref, mixed_ref, out_ref, lse_ref, own_ref,
    vt_ref, acc_ref, s_ref, packed_ref,
):
    span = loaded_ref.shape[0]
    blocks = span // BQ
    x_ref = packed_ref if pieces else loaded_ref
    if pieces:
        piece = span // pieces
        for k in range(pieces):
            row = (k // (pieces // 2)) * (span // 2) + slot_ref[k] * piece
            rows = pl.ds(pl.multiple_of(row, piece), piece)
            packed_ref[rows, :] = loaded_ref[k * piece : (k + 1) * piece, :]
    half = span // 2
    own_ref[...] = x_ref[pl.ds(pl.multiple_of(me_ref[0] * half, half), half), :]

    def project(i, _):
        rows = pl.ds(pl.multiple_of(i * BQ, BQ), BQ)
        x = x_ref[rows, :]
        q = (product(x, wq_ref[...]) + bq_ref[...].astype(F32)).astype(BF16)
        q_ref[rows, :] = (q.astype(F32) * (HEAD**-0.5)).astype(BF16)
        k_ref[rows, :] = product(x, wk_ref[...]).astype(BF16)
        v = (product(x, wv_ref[...]) + bv_ref[...].astype(F32)).astype(BF16)
        v_ref[rows, :] = v
        vt_ref[:, rows] = v.T
        return 0

    lax.fori_loop(0, blocks, project, 0)
    masks = head_masks()

    def query_block(i, _):
        rows = pl.ds(pl.multiple_of(i * BQ, BQ), BQ)
        ranges = block_range(bounds_ref, i)
        start, end = tile_mask(bounds_ref, i)
        q = q_ref[rows, :]
        heads = [q[:, (h // 2) * PAIR : (h // 2 + 1) * PAIR] * masks[h % 2] for h in range(HL)]
        acc_ref[...] = jnp.zeros_like(acc_ref)

        def score_block(masked, j, tops):
            keys = pl.ds(pl.multiple_of(j * BK, BK), BK)
            if masked:
                kpos = j * BK + lax.broadcasted_iota(jnp.int32, (BK, BQ), 0)
                mask = (kpos >= start) & (kpos < end)
            new = []
            for h in range(HL):
                kp = k_ref[keys, (h // 2) * PAIR : (h // 2 + 1) * PAIR]
                s = product_right(kp, heads[h]) * LOG2E
                if masked:
                    s = jnp.where(mask, s, NEG)
                s_ref[h, keys, :] = s
                new.append(jnp.maximum(tops[h], by_eight(s, jnp.max)))
            return tuple(new)

        tops = three_loops(
            ranges, score_block, tuple(jnp.full((8, BQ), NEG, F32) for _ in range(HL))
        )
        tops = [jnp.max(t, axis=0, keepdims=True) for t in tops]

        def mix_block(j, totals):
            keys = pl.ds(pl.multiple_of(j * BK, BK), BK)
            new = []
            for h in range(HL):
                p = jnp.exp2(s_ref[h, keys, :] - tops[h])
                new.append(totals[h] + by_eight(p, jnp.sum))
                lanes = slice(h * HEAD, (h + 1) * HEAD)
                acc_ref[lanes, :] += product(vt_ref[lanes, keys], p.astype(BF16))
            return tuple(new)

        totals = lax.fori_loop(
            ranges[0], ranges[3], mix_block, tuple(jnp.zeros((8, BQ), F32) for _ in range(HL))
        )
        for h in range(HL):
            total = jnp.sum(totals[h], axis=0, keepdims=True)
            lanes = slice(h * HEAD, (h + 1) * HEAD)
            acc_ref[lanes, :] = acc_ref[lanes, :] / total
            lse_ref[h : h + 1, rows] = tops[h] + jnp.log2(total)
        out = acc_ref[...]
        out_ref[:, rows] = out
        mixed_ref[rows, :] = out.T.astype(BF16)
        return 0

    lax.fori_loop(0, blocks, query_block, 0)


def column_block(shape):
    return pl.BlockSpec(shape, lambda i, bounds, me, slots: (0, me[0]))


def whole_block(shape):
    return pl.BlockSpec(shape, lambda i, bounds, me, slots: (0,) * len(shape))


def attend_forward(x_all, pieces, bounds, me, slots, wq, wk, wv, bq, bv):
    span = x_all.shape[0]
    rows_shape = jax.ShapeDtypeStruct((span, C), BF16)
    return pl.pallas_call(
        functools.partial(forward_kernel, pieces),
        grid_spec=pltpu.PrefetchScalarGridSpec(
            num_scalar_prefetch=3,
            grid=(1,),
            in_specs=[
                whole_block((span, D)),
                column_block((D, C)),
                column_block((D, C)),
                column_block((D, C)),
                column_block((1, C)),
                column_block((1, C)),
            ],
            out_specs=[whole_block((span, C))] * 4
            + [whole_block((C, span)), whole_block((8, span)), whole_block((span // 2, D))],
            scratch_shapes=[VMEM((C, span), BF16), VMEM((C, BQ), F32), VMEM((HL, span, BQ), F32), VMEM((span, D), BF16)],
        ),
        out_shape=[rows_shape] * 4
        + [jax.ShapeDtypeStruct((C, span), F32), jax.ShapeDtypeStruct((8, span), F32)]
        + [jax.ShapeDtypeStruct((span // 2, D), BF16)],
        name="attend_forward",
    )(bounds, me, slots, x_all, wq, wk, wv, bq.reshape(1, D), bv.reshape(1, D))


def backward_kernel(
    pieces, bounds_ref, me_ref, slot_ref,
    x_ref, q_ref, k_ref, v_ref, g_ref, out_ref, lse_ref, wq_ref, wk_ref, wv_ref, res_ref,
    gw_ref, sums_ref, ga_ref, gb_ref,
    kt_ref, gq_ref, gk_ref, gv_ref, gqt_ref, qs_ref, gs_ref, w_ref, ds_ref, term_ref,
):
    span = x_ref.shape[0]
    blocks = span // BQ
    scale = HEAD**-0.5

    def prepare(i, _):
        rows = pl.ds(pl.multiple_of(i * BQ, BQ), BQ)
        kt_ref[:, rows] = k_ref[rows, :].T
        gk_ref[rows, :] = jnp.zeros((BQ, C), F32)
        gv_ref[rows, :] = jnp.zeros((BQ, C), F32)
        return 0

    lax.fori_loop(0, blocks, prepare, 0)
    lane = lax.broadcasted_iota(jnp.int32, (1, C), 1) // HEAD
    masks = [(lane == h).astype(F32).astype(BF16) for h in range(HL)]

    def query_block(i, _):
        rows = pl.ds(pl.multiple_of(i * BQ, BQ), BQ)
        ranges = block_range(bounds_ref, i)
        start, end = tile_mask(bounds_ref, i)
        q = q_ref[rows, :]
        g = g_ref[rows, :]
        for h in range(HL):
            part = slice(h * BQ, (h + 1) * BQ)
            qs_ref[part, :] = q * masks[h]
            gs_ref[part, :] = g * masks[h]
        weighted = g.astype(F32).T * out_ref[:, rows]
        inner = [
            jnp.sum(weighted[h * HEAD : (h + 1) * HEAD], axis=0, keepdims=True) for h in range(HL)
        ]
        logsum = [lse_ref[h : h + 1, rows] for h in range(HL)]
        gqt_ref[...] = jnp.zeros_like(gqt_ref)

        def key_block(masked, j, _):
            keys = pl.ds(pl.multiple_of(j * BK, BK), BK)
            if masked:
                kpos = j * BK + lax.broadcasted_iota(jnp.int32, (BK, BQ), 0)
                mask = (kpos >= start) & (kpos < end)
            for h in range(HL):
                part = slice(h * BQ, (h + 1) * BQ)
                pair = slice((h // 2) * PAIR, (h // 2 + 1) * PAIR)
                s = product_right(k_ref[keys, pair], qs_ref[part, pair])
                w = jnp.exp2(s * LOG2E - logsum[h])
                if masked:
                    w = jnp.where(mask, w, 0.0)
                gw = product_right(v_ref[keys, pair], gs_ref[part, pair])
                gs = (w * (gw - inner[h])).astype(BF16)
                w_ref[keys, part] = w.astype(BF16)
                ds_ref[keys, part] = gs
            return 0

        def product_block(j, _):
            keys = pl.ds(pl.multiple_of(j * BK, BK), BK)
            for h in range(HL):
                part = slice(h * BQ, (h + 1) * BQ)
                lanes = slice(h * HEAD, (h + 1) * HEAD)
                gqt_ref[lanes, :] += product(kt_ref[lanes, keys], ds_ref[keys, part])
            gv_ref[keys, :] += product(w_ref[keys, :], gs_ref[...])
            gk_ref[keys, :] += product(ds_ref[keys, :], qs_ref[...])
            return 0

        three_loops(ranges, key_block, 0)
        lax.fori_loop(ranges[0], ranges[3], product_block, 0)
        gq_ref[rows, :] = (gqt_ref[...].T * scale).astype(BF16)
        return 0

    lax.fori_loop(0, blocks, query_block, 0)

    count = 4
    wide = span // count
    half = span // 2

    def load(ref, i):
        if not pieces:
            return ref[pl.ds(pl.multiple_of(i * wide, wide), wide), :].astype(BF16)
        piece = span // pieces
        each = pieces // count
        parts = []
        for k in range(each):
            row = (i // (count // 2)) * half + slot_ref[i * each + k] * piece
            parts.append(ref[pl.ds(pl.multiple_of(row, piece), piece), :].astype(BF16))
        return jnp.concatenate(parts, axis=0)

    def own_rows(i):
        if not pieces:
            return res_ref[pl.ds(pl.multiple_of(i * wide, wide), wide), :]
        piece = span // pieces
        each = pieces // count
        parts = []
        for k in range(each):
            row = slot_ref[me_ref[0] * (pieces // 2) + i * each + k] * piece
            parts.append(res_ref[pl.ds(pl.multiple_of(row, piece), piece), :])
        return jnp.concatenate(parts, axis=0)

    def gradients(i):
        rows = pl.ds(pl.multiple_of(i * wide, wide), wide)
        gq, gk, gv = load(gq_ref, i), load(gk_ref, i), load(gv_ref, i)
        x = x_ref[rows, :]
        for n, part in enumerate((gq, gk, gv)):
            term_ref[n] += product_left(x, part)
        sums_ref[...] += jnp.concatenate(
            [jnp.sum(a.astype(F32), axis=0, keepdims=True) for a in (gq, gv)], axis=1
        )
        gx = product_right(gq, wq_ref[...]) + product_right(gk, wk_ref[...])
        return gx + product_right(gv, wv_ref[...])

    term_ref[...] = jnp.zeros_like(term_ref)
    sums_ref[...] = jnp.zeros_like(sums_ref)
    blocks_each = count // 2

    def own_tail(i, _):
        gx = gradients(me_ref[0] * blocks_each + i)
        ga_ref[pl.ds(pl.multiple_of(i * wide, wide), wide), :] = gx + own_rows(i)
        return 0

    def other_tail(i, _):
        gx = gradients((1 - me_ref[0]) * blocks_each + i)
        gb_ref[pl.ds(pl.multiple_of(i * wide, wide), wide), :] = gx.astype(BF16)
        return 0

    lax.fori_loop(0, blocks_each, own_tail, 0)
    lax.fori_loop(0, blocks_each, other_tail, 0)
    gw_ref[...] = term_ref[...].astype(BF16)


def attend_backward(bounds, me, slots, pieces, x_all, q, k, v, g, out, lse, wq, wk, wv, res):
    span = x_all.shape[0]
    rows = whole_block((span, C))
    return pl.pallas_call(
        functools.partial(backward_kernel, pieces),
        grid_spec=pltpu.PrefetchScalarGridSpec(
            num_scalar_prefetch=3,
            grid=(1,),
            in_specs=[whole_block((span, D)), rows, rows, rows, rows]
            + [whole_block((C, span)), whole_block((8, span))]
            + [column_block((D, C))] * 3
            + [whole_block((span // 2, D))],
            out_specs=[whole_block((3, D, C)), whole_block((1, 2 * C))]
            + [whole_block((span // 2, D))] * 2,
            scratch_shapes=[
                VMEM((C, span), BF16),
                VMEM((span, C), BF16),
                VMEM((span, C), F32),
                VMEM((span, C), F32),
                VMEM((C, BQ), F32),
                VMEM((HL * BQ, C), BF16),
                VMEM((HL * BQ, C), BF16),
                VMEM((span, HL * BQ), BF16),
                VMEM((span, HL * BQ), BF16),
                VMEM((3, D, C), F32),
            ],
        ),
        out_shape=[
            jax.ShapeDtypeStruct((3, D, C), BF16),
            jax.ShapeDtypeStruct((1, 2 * C), F32),
            jax.ShapeDtypeStruct((span // 2, D), F32),
            jax.ShapeDtypeStruct((span // 2, D), BF16),
        ],
        name="attend_backward",
    )(bounds, me, slots, x_all, q, k, v, g, out, lse, wq, wk, wv, res)


def arrange_kernel(groups, route_ref, x_ref, o_ref, slot_ref):
    for k in range(groups):
        packed = route_ref[k]
        group = packed // (2 * groups)
        o_ref[group] = x_ref[k]
        slot_ref[group] = jnp.full(slot_ref.shape[1:], packed % groups, jnp.int32)


def arrange(pieces, route):
    groups, piece, _ = pieces.shape
    return pl.pallas_call(
        functools.partial(arrange_kernel, groups),
        grid_spec=pltpu.PrefetchScalarGridSpec(
            num_scalar_prefetch=1,
            grid=(1,),
            in_specs=[pl.BlockSpec(pieces.shape, lambda i, r: (0, 0, 0))],
            out_specs=[
                pl.BlockSpec(pieces.shape, lambda i, r: (0, 0, 0)),
                pl.BlockSpec((groups, 8, 128), lambda i, r: (0, 0, 0)),
            ],
        ),
        out_shape=[
            jax.ShapeDtypeStruct(pieces.shape, BF16),
            jax.ShapeDtypeStruct((groups, 8, 128), jnp.int32),
        ],
        name="arrange",
    )(route, pieces)


def restore_kernel(groups, route_ref, x_ref, o_ref):
    for k in range(groups):
        o_ref[k] = x_ref[route_ref[k] // (2 * groups)]


def restore(pieces, route):
    spec = pl.BlockSpec(pieces.shape, lambda i, r: (0, 0, 0))
    return pl.pallas_call(
        functools.partial(restore_kernel, pieces.shape[0]),
        grid_spec=pltpu.PrefetchScalarGridSpec(
            num_scalar_prefetch=1, grid=(1,), in_specs=[spec], out_specs=spec
        ),
        out_shape=jax.ShapeDtypeStruct(pieces.shape, BF16),
        name="restore",
    )(route, pieces)


def far_first(n):
    return sorted(range(1, n), key=lambda k: abs(k - n // 2))


def dispatch_kernel(n, x_ref, slot_ref, o_ref, slots_ref, send, recv, ssend, srecv, fsend, frecv):
    dp, me = lax.axis_index("dp"), lax.axis_index("seq")
    partner = (dp, 1 - me)
    barrier = pltpu.get_barrier_semaphore()
    for k in range(1, n):
        pl.semaphore_signal(barrier, inc=1, device_id=((dp + k) % n, me), device_id_type=MESH)
    pl.semaphore_signal(barrier, inc=1, device_id=partner, device_id_type=MESH)
    pl.semaphore_wait(barrier, n)

    def push(src, dst, s, r, device):
        return pltpu.make_async_remote_copy(
            src_ref=src, dst_ref=dst, send_sem=s, recv_sem=r,
            device_id=device, device_id_type=MESH,
        )

    order = far_first(n)
    copies, small = {}, {}
    for k in order:
        p = (dp + k) % n
        copies[k] = push(x_ref.at[p], o_ref.at[me, dp], send.at[k], recv.at[k], (p, me))
        copies[k].start()
        small[k] = push(slot_ref.at[p], slots_ref.at[me, dp], ssend.at[k], srecv.at[k], (p, me))
        small[k].start()
    forwards = [push(x_ref.at[dp], o_ref.at[me, dp], fsend.at[0], frecv.at[0], partner)]
    forwards[0].start()
    o_ref[me, dp] = x_ref[dp]
    slots_ref[me, dp] = slot_ref[dp]
    for k in order:
        s = (dp + n - k) % n
        copies[k].wait_recv()
        forward = push(o_ref.at[me, s], o_ref.at[me, s], fsend.at[k], frecv.at[k], partner)
        forward.start()
        forwards.append(forward)
    for k in order:
        small[k].wait_recv()
    last = push(slots_ref.at[me], slots_ref.at[me], fsend.at[n], frecv.at[n], partner)
    last.start()
    forwards.append(last)
    for k in order:
        copies[k].wait_send()
        small[k].wait_send()
    for forward in forwards:
        forward.wait()


def dispatch(outgoing, slots, collective_id):
    n = outgoing.shape[0]
    vmem = pl.BlockSpec(memory_space=VMEM)
    return pl.pallas_call(
        functools.partial(dispatch_kernel, n),
        out_shape=[
            jax.ShapeDtypeStruct((2,) + outgoing.shape, BF16),
            jax.ShapeDtypeStruct((2,) + slots.shape, jnp.int32),
        ],
        in_specs=[vmem] * 2,
        out_specs=[vmem] * 2,
        scratch_shapes=[pltpu.SemaphoreType.DMA((n,))] * 4 + [pltpu.SemaphoreType.DMA((n + 1,))] * 2,
        compiler_params=pltpu.CompilerParams(collective_id=collective_id, has_side_effects=True),
        name="dispatch",
    )(outgoing, slots)


class Chunk:
    def __init__(self, env, number, source, full, acc, landing, shared):
        self.env, self.number, self.shared = env, number, shared
        self.source, self.full, self.acc, self.landing = source, full, acc, landing
        self.base, self.size, self.offset, self.stage = 0, source.shape[0], 0, 0
        self.from_source, self.kept, self.copies = True, [], []

    def push(self, src, dst, device):
        e = self.env
        copy = pltpu.make_async_remote_copy(
            src_ref=src, dst_ref=dst,
            send_sem=e["send"].at[self.number, self.stage],
            recv_sem=e["recv"].at[self.number, self.stage],
            device_id=device, device_id_type=MESH,
        )
        copy.start()
        self.stage += 1
        self.copies.append(copy)

    def at(self, ref, start, size):
        return ref.at[pl.ds(start if isinstance(start, int) else pl.multiple_of(start, 16), size), :]

    def halve(self, peer):
        device, bit = peer
        half = self.size // 2
        keep, give = self.base + bit * half, self.base + (1 - bit) * half
        src = self.source if self.from_source else self.acc
        self.push(self.at(src, give, half), self.at(self.landing, self.offset, half), device)
        self.kept.append((keep, half, device))

    def finish_half(self):
        for copy in self.copies:
            copy.wait()
        self.copies = []
        keep, half, _ = self.kept[-1]
        src = self.source if self.from_source else self.acc
        step = min(half, 64)
        base, offset = keep, self.offset

        def add(i, _):
            here = pl.ds(pl.multiple_of(base + i * step, 16), step)
            there = pl.ds(pl.multiple_of(offset + i * step, 16), step)
            total = src[here, :].astype(F32) + self.landing[there, :].astype(F32)
            self.acc[here, :] = total.astype(BF16)
            return 0

        lax.fori_loop(0, half // step, add, 0)
        self.base, self.size, self.offset = keep, half, offset + half
        self.from_source = False

    def quarter(self):
        e = self.env
        q = self.size // 4
        for k in range(1, 4):
            z = (e["z"] + k) % 4
            self.push(
                self.at(self.acc, self.base + z * q, q),
                self.at(self.landing, self.offset + (k - 1) * q, q),
                ((e["dp"] + 4 * k) % 16, e["me"]),
            )

    def finish_quarter(self):
        for copy in self.copies:
            copy.wait()
        self.copies = []
        q = self.size // 4
        here = pl.ds(pl.multiple_of(self.base + self.env["z"] * q, 16), q)
        total = self.acc[here, :].astype(F32)
        for k in range(3):
            total += self.landing[self.offset + k * q : self.offset + (k + 1) * q, :].astype(F32)
        self.full[here, :] = total.astype(BF16)
        region = self.at(self.full, self.base + self.env["z"] * q, q)
        for k in range(1, 4):
            self.push(region, region, ((self.env["dp"] + 4 * k) % 16, self.env["me"]))

    def spread(self):
        for copy in self.copies:
            copy.wait()
        self.copies = []
        keep, half, device = self.kept.pop()
        region = self.at(self.full, keep, half)
        self.push(region, region, device)

    def hand_over(self):
        for copy in self.copies:
            copy.wait()
        self.copies = []
        self.push(self.full, self.full, (self.env["dp"], 1 - self.env["me"]))

    def close(self):
        for copy in self.copies:
            copy.wait()

    def steps(self):
        e = self.env
        first, second = e["axes"]
        line = []
        if self.shared:
            line.append(lambda: self.halve(((e["dp"], 1 - e["me"]), e["me"])))
            line.append(lambda: (self.finish_half(), self.halve(first)))
        else:
            line.append(lambda: self.halve(first))
        line.append(lambda: (self.finish_half(), self.halve(second)))
        line.append(lambda: (self.finish_half(), self.quarter()))
        line.append(self.finish_quarter)
        line += [self.spread] * (3 if self.shared else 2)
        if not self.shared:
            line.append(self.hand_over)
        line.append(self.close)
        return line


def final_kernel(
    ga_ref, gb_ref, up_ref, down_ref, out_ref, qkv_ref, vec_ref,
    back_ref, up_full, down_full, out_full, qkv_full, vec_full,
    ret_ref, gbr_ref, acc_ref, landing_ref, acc_own, landing_own, vec_recv,
    send, recv, asend, arecv, gsend, grecv, vsend, vrecv,
):
    n = 16
    dp, me = lax.axis_index("dp"), lax.axis_index("seq")
    rows = ga_ref.shape[0]
    piece = rows // n
    partner = (dp, 1 - me)
    wa, wb = 1 + me, 2 - me
    bit_a, bit_b = (dp // wa) % 2, (dp // wb) % 2
    env = {
        "dp": dp,
        "me": me,
        "z": dp // 4,
        "axes": (
            ((dp + (1 - 2 * bit_a) * wa, me), bit_a),
            ((dp + (1 - 2 * bit_b) * wb, me), bit_b),
        ),
        "send": send,
        "recv": recv,
    }
    barrier = pltpu.get_barrier_semaphore()
    for k in range(1, n):
        pl.semaphore_signal(barrier, inc=1, device_id=((dp + k) % n, me), device_id_type=MESH)
    pl.semaphore_signal(barrier, inc=1, device_id=partner, device_id_type=MESH)
    pl.semaphore_wait(barrier, n)

    def push(src, dst, s, r, device):
        return pltpu.make_async_remote_copy(
            src_ref=src, dst_ref=dst, send_sem=s, recv_sem=r,
            device_id=device, device_id_type=MESH,
        )

    quarter = rows // 4
    halves = []
    for j in range(4):
        part = pl.ds(j * quarter, quarter)
        copy = push(gb_ref.at[part, :], gbr_ref.at[part, :], gsend.at[j], grecv.at[j], partner)
        copy.start()
        halves.append(copy)

    chunks = []
    for c in range(4):
        lanes = pl.ds(c * D, D)
        chunks.append((up_ref.at[:, lanes], up_full.at[:, lanes], True))
    for c in range(4):
        part = pl.ds(c * D, D)
        chunks.append((down_ref.at[part, :], down_full.at[part, :], True))
    chunks.append((out_ref, out_full, True))
    for c in range(3):
        chunks.append((qkv_ref.at[c], qkv_full.at[me, c], False))
    lines = []
    counts = {True: 0, False: 0}
    for number, (source, full, shared) in enumerate(chunks):
        i = counts[shared]
        counts[shared] += 1
        acc = (acc_ref if shared else acc_own).at[i]
        landing = (landing_ref if shared else landing_own).at[i]
        lines.append(Chunk(env, number, source, full, acc, landing, shared).steps())
    peers = [partner]
    for w, size in ((1, 2), (2, 2), (4, 2), (8, 2)):
        bit = (dp // w) % 2
        peers.append((dp + (1 - 2 * bit) * w, me))
    vec_copies = []

    def vec_step(s):
        if s == 0:
            vec_full[...] = vec_ref[...]
        else:
            vec_copies[-1].wait()
            vec_full[...] += vec_recv[s - 1]
        if s < len(peers):
            sent = vec_recv.at[len(peers) + s]
            sent[...] = vec_full[...]
            copy = push(sent, vec_recv.at[s], vsend.at[s], vrecv.at[s], peers[s])
            copy.start()
            vec_copies.append(copy)

    lines.append([functools.partial(vec_step, s) for s in range(len(peers) + 1)])

    returns = []

    def give_back():
        for j in range(4):
            halves[j].wait()

            def add(i, _, j=j):
                here = pl.ds(pl.multiple_of(j * quarter + i * 64, 64), 64)
                ret_ref[here, :] = (ga_ref[here, :] + gbr_ref[here, :].astype(F32)).astype(BF16)
                return 0

            lax.fori_loop(0, quarter // 64, add, 0)
        mine = pl.ds(pl.multiple_of(dp * piece, piece), piece)
        for k in far_first(n):
            p = (dp + k) % n
            theirs = pl.ds(pl.multiple_of(p * piece, piece), piece)
            copy = push(
                ret_ref.at[theirs, :], back_ref.at[mine, :], asend.at[k], arecv.at[k], (p, me)
            )
            copy.start()
            returns.append(copy)
        back_ref[mine, :] = ret_ref[mine, :]

    ticks = max(len(line) + at for at, line in enumerate(lines))
    for t in range(ticks):
        for at, line in enumerate(lines):
            if 0 <= t - at < len(line):
                line[t - at]()
        if t == 0:
            give_back()
    for copy in returns:
        copy.wait()


def give_back_and_sum(ga, gb, up, down, out, qkv, vec, collective_id):
    vmem = pl.BlockSpec(memory_space=VMEM)
    shape = jax.ShapeDtypeStruct
    dma = pltpu.SemaphoreType.DMA
    return pl.pallas_call(
        final_kernel,
        out_shape=[
            shape(gb.shape, BF16),
            shape(up.shape, BF16),
            shape(down.shape, BF16),
            shape(out.shape, BF16),
            shape((2,) + qkv.shape, BF16),
            shape(vec.shape, F32),
        ],
        in_specs=[vmem] * 7,
        out_specs=[vmem] * 6,
        scratch_shapes=[
            VMEM(gb.shape, BF16),
            VMEM(gb.shape, BF16),
            VMEM((9, D, D), BF16),
            VMEM((9, D, D), BF16),
            VMEM((3, D, C), BF16),
            VMEM((3, D, C), BF16),
            VMEM((10,) + vec.shape, F32),
            dma((12, 12)), dma((12, 12)),
            dma((16,)), dma((16,)),
            dma((4,)), dma((4,)),
            dma((5,)), dma((5,)),
        ],
        compiler_params=pltpu.CompilerParams(
            collective_id=collective_id, has_side_effects=True, vmem_limit_bytes=62 << 20
        ),
        name="give_back_and_sum",
    )(ga, gb, up, down, out, qkv, vec)


def body(
    tokens,
    route,
    lengths,
    query_weight,
    query_bias,
    key_weight,
    value_weight,
    value_bias,
    output_weight,
    output_bias,
    first_gain,
    first_shift,
    up_weight,
    up_bias,
    down_weight,
    down_bias,
    second_gain,
    second_shift,
    cotangent,
):
    groups = lax.axis_size("dp")
    rows = tokens.shape[0]
    piece = rows // groups
    span = rows * lax.axis_size("seq")
    seq = lax.axis_index("seq")
    bounds = jnp.cumsum(lengths[0]).astype(jnp.int32)
    me = seq.reshape(1).astype(jnp.int32)
    kernels = groups == 16 and piece % 16 == 0
    if kernels:
        pieces = 2 * groups
        outgoing, slots_out = arrange(tokens.reshape(groups, piece, D), route)
        x_all, slots_all = dispatch(outgoing, slots_out, 0)
        x_all = x_all.reshape(span, D)
        slots = slots_all[:, :, 0, 0].reshape(pieces)
    else:
        pieces = 0
        target = route // groups // lax.axis_size("seq")
        place = route % groups
        outgoing = jnp.zeros((groups, piece, D), BF16).at[target].set(tokens.reshape(groups, piece, D))
        slots_out = jnp.zeros((groups,), jnp.int32).at[target].set(place)
        incoming, slots = (
            lax.all_to_all(outgoing, "dp", split_axis=0, concat_axis=0, tiled=True),
            lax.all_to_all(slots_out, "dp", split_axis=0, concat_axis=0, tiled=True),
        )
        inputs = jnp.zeros_like(incoming).at[slots].set(incoming).reshape(rows, D)
        x_all = swap(inputs, 0).reshape(span, D)
    q, k, v, mixed_all, attend_out, lse, inputs = attend_forward(
        x_all, pieces, bounds, me, slots,
        query_weight, key_weight, value_weight, query_bias, value_bias,
    )
    mixed_halves = swap(mixed_all.reshape(2, rows, C), 1)
    mixed = jnp.concatenate([mixed_halves[0], mixed_halves[1]], axis=1)
    branch = product(mixed, output_weight) + output_bias
    residual = inputs.astype(F32) + branch
    first, first_back = jax.vjp(
        norm_rows, residual, first_gain.astype(F32), first_shift.astype(F32)
    )
    first_low = first.astype(BF16)
    hidden = product(first_low, up_weight) + up_bias
    active = gelu_exact(hidden).astype(BF16)
    update = product(active, down_weight) + down_bias
    layer_out, second_back = jax.vjp(
        norm_rows, first + update, second_gain.astype(F32), second_shift.astype(F32)
    )
    grad_second, grad_second_gain, grad_second_shift = second_back(cotangent.astype(F32))
    grad_update = grad_second.astype(BF16)
    again = product(first_low, up_weight) + up_bias
    active_again, gelu_back = jax.vjp(gelu_exact, again)
    active_low = active_again.astype(BF16)
    grad_down = product_left(active_low, grad_update)
    grad_down_bias = column_sums(grad_update)
    (grad_active,) = gelu_back(product_right(grad_update, down_weight))
    grad_hidden = grad_active.astype(BF16)
    grad_up = product_left(first_low, grad_hidden)
    grad_up_bias = column_sums(grad_hidden)
    grad_first = grad_second + product_right(grad_hidden, up_weight)
    grad_residual, grad_first_gain, grad_first_shift = first_back(grad_first)
    grad_branch = grad_residual.astype(BF16)
    grad_output = product_left(mixed, grad_branch)
    grad_output_bias = column_sums(grad_branch)
    grad_mixed = product_right(grad_branch, output_weight).astype(BF16)
    grad_halves = jnp.stack([grad_mixed[:, :C], grad_mixed[:, C:]])
    grad_mixed_all = swap(grad_halves, 2).reshape(span, C)
    grad_columns, column_parts, grad_own, grad_other = attend_backward(
        bounds, me, slots, pieces, x_all, q, k, v, grad_mixed_all, attend_out, lse,
        query_weight, key_weight, value_weight, grad_residual,
    )

    def own_columns(part):
        return lax.dynamic_update_slice(jnp.zeros((1, D), F32), part, (0, seq * C))

    vec = jnp.concatenate(
        [
            own_columns(column_parts[:, :C]),
            own_columns(column_parts[:, C:]),
            jnp.stack(
                [
                    grad_output_bias,
                    grad_first_gain,
                    grad_first_shift,
                    grad_down_bias,
                    grad_second_gain,
                    grad_second_shift,
                ]
            ),
            grad_up_bias.reshape(-1, D),
            jnp.zeros((4, D), F32),
        ]
    )
    if kernels:
        back, up_sum, down_sum, out_sum, columns, vec = give_back_and_sum(
            grad_own, grad_other,
            grad_up.astype(BF16), grad_down.astype(BF16), grad_output.astype(BF16),
            grad_columns, vec, 4,
        )
        token_grad = restore(back.reshape(groups, piece, D), route).reshape(rows, D)
        up_sum, down_sum, out_sum = (a.astype(F32) for a in (up_sum, down_sum, out_sum))
        columns = jnp.concatenate([columns[0], columns[1]], axis=2).astype(F32)
    else:
        grad_inputs = grad_own + swap(jnp.stack([grad_other, grad_other]), 3)[1 - seq].astype(F32)
        back_rows = grad_inputs.astype(BF16).reshape(groups, piece, D)[slots]
        returned = lax.all_to_all(back_rows, "dp", split_axis=0, concat_axis=0, tiled=True)
        token_grad = returned[target].reshape(rows, D)
        up_sum, down_sum, out_sum, vec = lax.psum((grad_up, grad_down, grad_output, vec), ("dp", "seq"))
        columns = lax.psum(grad_columns.astype(F32), "dp")
        columns = lax.all_gather(columns, "seq", axis=2, tiled=True)
    query_sum, key_sum, value_sum = columns[0], columns[1], columns[2]
    return (
        layer_out.astype(BF16),
        token_grad,
        query_sum,
        vec[0],
        key_sum,
        value_sum,
        vec[1],
        out_sum,
        vec[2],
        vec[3],
        vec[4],
        up_sum,
        vec[8:12].reshape(-1),
        down_sum,
        vec[5],
        vec[6],
        vec[7],
    )


def solution(mesh):
    both, one = P(("dp", "seq"), None), P()
    return jax.shard_map(
        body,
        mesh=mesh,
        in_specs=(both, P(("dp", "seq")), P("dp", None)) + (one,) * 15 + (both,),
        out_specs=(both, both) + (one,) * 15,
        check_vma=False,
    )
```

time: 369 us -> 314 us (0.85)
  starting transfers between devices: 42.3 us -> 0 us
  Pallas kernels: 201 us -> 235 us
  waiting for transfers between devices: 24.1 us -> 0 us
  local copies, waits for them, and re-layouts: 35.5 us -> 11.7 us
    pallas_call x3 -> x6, Pallas kernels: 182 us -> 227 us  [the longest x1 107 us: give_back_and_sum(): pl.pallas_call(final_kernel, out_shape=[shape(gb.shape, BF16), shape(up.s...]
    all_to_all x3 -> x0, starting transfers between devices: 42.3 us -> none  [the longest x1 29.6 us: body(): lax.all_to_all(back_rows, 'dp', split_axis=0, concat_axis=0, tiled=True)]
    all_to_all x3 -> x0, waiting for transfers between devices: 24.1 us -> none  [the longest x1 21.4 us: body(): lax.all_to_all(outgoing, 'dp', split_axis=0, concat_axis=0, tiled=True)]
    pallas_call x4 -> x2, Pallas kernels: 19.2 us -> 8.31 us  [swap(): pl.pallas_call(swap_kernel, out_shape=jax.ShapeDtypeStruct(shape, x.dtype...]
    unnamed x55 -> x54, local copies, waits for them, and re-layouts: 12.6 us -> 3.22 us
    scatter x3 -> x0, local copies, waits for them, and re-layouts: 6.26 us -> none  [the longest x1 3.37 us: body(): jnp.zeros((groups, piece, D), BF16).at[target]]
    convert_element_type x1 -> x4, other arithmetic: 2.61 us -> 6.68 us  [the longest x3 6.25 us: body(): a.astype(F32)]
  transfers between devices with their start and end apart: 3 -> 0, of which waited for: 2 -> 0; matrix products, arithmetic and copies ran while one was open for 9% -> 0% of each run, Pallas kernels for 26% -> 0%
where the time goes in v2:
time: 314 us; the launch traced here: 313 us
  Pallas kernels  235 us (75%)
  matrix products  48.8 us (16%)
  other arithmetic  16.3 us (5%)
  local copies, waits for them, and re-layouts  11.7 us (4%)
    pallas_call x1, Pallas kernels, give_back_and_sum(): pl.pallas_call(final_kernel, out_shape=[shape(gb.shape, BF16), shape(up.s...  107 us
    pallas_call x1, Pallas kernels, attend_backward(): pl.pallas_call(functools.partial(backward_kernel, pieces), grid_spec=pltp...  47.9 us
    pallas_call x1, Pallas kernels, dispatch(): pl.pallas_call(functools.partial(dispatch_kernel, n), out_shape=[jax.Shap...  34.6 us
    pallas_call x1, Pallas kernels, attend_forward(): pl.pallas_call(functools.partial(forward_kernel, pieces), grid_spec=pltpu...  31.3 us
    dot_general x3, matrix products, product(): return jnp.dot(left, right, preferred_element_type=F32)  25.4 us
    dot_general x3, matrix products, product_right(): lax.dot_general(left, right, (((1,), (1,)), ((), ())), preferred_element_...  11.9 us
    dot_general x3, matrix products, product_left(): lax.dot_general(left, right, (((0,), (0,)), ((), ())), preferred_element_...  11.5 us
    pallas_call x2, Pallas kernels, swap(): pl.pallas_call(swap_kernel, out_shape=jax.ShapeDtypeStruct(shape, x.dtype...  8.31 us

profile of v2, /device:TPU:0, one launch (start us, length us, event | category | flops | bytes accessed | tf_op | source)
XLA Modules:
  0.0 312.9 jit_solution(4572736034230979298)
XLA Ops:
  0.7 0.7 convert_element_type.87
  1.4 0.7 convert_element_type.85
  2.8 1.3 reduce-window.9
  4.1 3.0 arrange.1
  7.1 34.6 %dispatch.1 = (bf16[2,16,64,512]{3,2,1,0:T(8,128)(2,1)}, s32[2,16,8,128]{3,2,1,0:T(8,128)}) custom-call(bf16[16,64,512]{2,1,0:T(8,128)(2,1)} %get-tuple-element.38.x_ref, s32[16,8,128]{2,1,0:T(8,128)} %get-tuple-element.39.slot_ref), custom_call_target="tpu_custom_call" | custom-call | tf_op jit(solution)/shard_map/dispatch/pallas_call | solution.py:515
  41.7 1.6 slice_reduce_fusion
  45.0 31.3 %attend_forward.1 = (bf16[2048,256]{1,0:T(8,128)(2,1)}, bf16[2048,256]{1,0:T(8,128)(2,1)}, bf16[2048,256]{1,0:T(8,128)(2,1)}, bf16[2048,256]{1,0:T(8,128)(2,1)},...) custom-call(s32[6]{0:T(128)} %bitcast.68, s32[1]{0:T(128)} %bitcast.2.me_ref, ...), custom_call_target="tpu_custom_call" | custom-call | tf_op jit(solution)/shard_map/attend_forward/pallas_call | solution.py:226
  76.3 4.2 %shard_map.314 = bf16[2,1024,256]{2,1,0:T(8,128)(2,1)} custom-call(bf16[2,1024,256]{2,1,0:T(8,128)(2,1)} %bitcast.62), custom_call_target="tpu_custom_call" | custom-call | tf_op jit(solution)/shard_map/pallas_call | solution.py:77
  80.5 1.4 slice_bitcast_fusion.8
  82.1 0.8 fusion.24
  83.3 1.1 copy-done.21
  84.4 21.9 %multiply_convert_fusion = (bf16[1024,2048]{1,0:T(8,128)(2,1)S(1)}, f32[1024,2048]{1,0:T(8,128)S(1)}, f32[1024,2048]{1,0:T(8,128)}) fusion(f32[2048]{0:T(1024)S(1)} %convert_element_type.85, bf16[512,2048]{1,0:T(8,128)(2,1)S(1)} %copy-done.21, f32[1024,512]{1,0:T(8,128)S(1)} %get-tuple-element.94, f32[512]{0:T(512)S(1)} %convert_element_type.83, ...), kind=kOutput, calls=%fused_computation.4 | convolution fusion | flops 2288517120 | bytes 25186304 | tf_op jit(solution)/shard_map/dot_general | solution.py:38
  106.4 2.7 fusion.25
  110.3 1.0 fusion.9
  111.3 2.0 fusion.21
  113.6 8.1 %convert_reduce_fusion = (f32[2048]{0:T(1024)S(1)}, bf16[1024,2048]{1,0:T(8,128)(2,1)S(1)}) fusion(f32[1024,2048]{1,0:T(8,128)S(1)} %get-tuple-element.74, bf16[1024,512]{1,0:T(8,128)(2,1)S(1)} %get-tuple-element.66, bf16[2048,512]{1,0:T(8,128)(2,1)S(1)} %copy-done.20, f32[1024,2048]{1,0:T(8,128)} %get-tuple-element.95, f32[2048]{0:T(1024)S(1)} %convert_element_type.85), kind=kOutput, calls=%fused_computation.2 | convolution fusion | flops 2183133184 | bytes 24133632 | tf_op jit(solution)/shard_map/dot_general | solution.py:46
  121.6 3.1 multiply_reduce_fusion
  124.7 0.8 fusion.20
  125.9 0.7 convolution_convert_fusion.2
  127.2 1.1 pad_maximum_fusion.1.x_ref
  128.3 4.2 %shard_map.315 = bf16[2,1024,256]{2,1,0:T(8,128)(2,1)} custom-call(bf16[2,1024,256]{2,1,0:T(8,128)(2,1)} %pad_maximum_fusion.1.x_ref), custom_call_target="tpu_custom_call" | custom-call | tf_op jit(solution)/shard_map/pallas_call | solution.py:77
  132.4 47.9 %attend_backward.1 = (bf16[3,512,256]{2,1,0:T(8,128)(2,1)}, f32[1,512]{1,0:T(1,128)}, f32[1024,512]{1,0:T(8,128)}, bf16[1024,512]{1,0:T(8,128)(2,1)}) custom-call(s32[6]{0:T(128)} %bitcast.69, s32[1]{0:T(128)} %bitcast.2.me_ref, s32[32]{0:T(128)} %reshape_squeeze.3.slot_ref, bf16[2048,512]{1,0:T(8,128)(2,1)} %bitcast.57, ...), custom_call_target="tpu_custom_call" | custom-call | tf_op jit(solution)/shard_map/attend_backward/pallas_call | solution.py:383
  180.4 6.2 %convolution_convert_fusion.1.up_ref = bf16[512,2048]{1,0:T(8,128)(2,1)} fusion(bf16[1024,2048]{1,0:T(8,128)(2,1)} %copy-done.25, f32[1024,512]{1,0:T(8,128)S(1)} %get-tuple-element.94, f32[512]{0:T(512)S(1)} %convert_element_type.83, f32[512]{0:T(512)S(1)} %convert_element_type.82, f32[1024]{0:T(1024)S(1)} %fusion.11, f32[1024]{0:T(1024)S(1)} %broadcast_multiply_fusion.1), kind=kOutput, calls=%fused_computation.24 | convolution fusion | flops 2151153664 | bytes 8400896 | tf_op jit(solution)/shard_map/dot_general | solution.py:42
  186.6 3.8 %convolution_convert_fusion.down_ref = bf16[2048,512]{1,0:T(8,128)(2,1)} fusion(bf16[1024,2048]{1,0:T(8,128)(2,1)S(1)} %copy-done.24, bf16[1024,512]{1,0:T(8,128)(2,1)S(1)} %copy-done.8), kind=kOutput, calls=%fused_computation.23 | convolution fusion | flops 2148532224 | bytes 7340032 | tf_op jit(solution)/shard_map/dot_general | solution.py:42
  190.4 1.6 convolution_convert_fusion.3.out_ref
  192.0 1.3 concatenate.10.vec_ref
  193.2 106.8 %give_back_and_sum.1 = (bf16[1024,512]{1,0:T(8,128)(2,1)}, bf16[512,2048]{1,0:T(8,128)(2,1)}, bf16[2048,512]{1,0:T(8,128)(2,1)}, bf16[512,512]{1,0:T(8,128)(2,1)...) custom-call(f32[1024,512]{1,0:T(8,128)} %get-tuple-element.49.ga_ref, bf16[1024,512]{1,0:T(8,128)(2,1)} %get-tuple-element.50.gb_ref, ...), custom_call_target="tpu_custom_call" | custom-call | tf_op jit(solution)/shard_map/give_back_and_sum/pallas_call | solution.py:762
  300.0 3.1 restore.1
  303.7 1.7 slice_bitcast_fusion
  306.0 1.1 convert_element_type.103
  307.1 2.5 convert_element_type.104
  310.3 2.6 convert_element_type.105
  (83 shorter events, 7.2 us)
Async XLA Ops:
  0.7 81.2 %copy-start = (bf16[512,512]{1,0:T(8,128)(2,1)S(1)}, bf16[512,512]{1,0:T(8,128)(2,1)}, u32[]{:S(2)}) copy-start(bf16[512,512]{1,0:T(8,128)(2,1)} %param.27) | copy-start | bytes 1572868
  0.7 43.2 %copy-start.14 = (bf16[512]{0:T(512)(128)(2,1)S(1)}, bf16[512]{0:T(512)(128)(2,1)}, u32[]{:S(2)}) copy-start(bf16[512]{0:T(512)(128)(2,1)} %param.23) | copy-start | bytes 3076
  0.7 43.7 %copy-start.15 = (bf16[512]{0:T(512)(128)(2,1)S(1)}, bf16[512]{0:T(512)(128)(2,1)}, u32[]{:S(2)}) copy-start(bf16[512]{0:T(512)(128)(2,1)} %param.26) | copy-start | bytes 3076
  80.5 1.5 copy-start.22
  81.9 1.0 copy-start.10
  82.0 0.8 copy-start.16
  82.1 0.8 copy-start.17
  82.8 1.6 copy-start.21
  84.4 21.9 %copy-start.20 = (bf16[2048,512]{1,0:T(8,128)(2,1)S(1)}, bf16[2048,512]{1,0:T(8,128)(2,1)}, u32[]{:S(2)}) copy-start(bf16[2048,512]{1,0:T(8,128)(2,1)} %param.33) | copy-start | bytes 6291460
  106.4 2.7 copy-start.23
  109.1 0.7 copy-start.18
  109.1 1.2 copy-start.3
  109.5 1.8 copy-start.19
  113.5 8.1 %copy-start.7 = (bf16[1024,512]{1,0:T(8,128)(2,1)}, bf16[1024,512]{1,0:T(8,128)(2,1)S(1)}, u32[]{:S(2)}) copy-start(bf16[1024,512]{1,0:T(8,128)(2,1)S(1)} %get-tuple-element.66) | copy-start | bytes 3145732
  121.6 3.1 copy-start.25
  125.9 1.3 copy-start.1
  180.4 6.2 %copy-start.8 = (bf16[1024,512]{1,0:T(8,128)(2,1)S(1)}, bf16[1024,512]{1,0:T(8,128)(2,1)}, u32[]{:S(2)}) copy-start(bf16[1024,512]{1,0:T(8,128)(2,1)} %copy-done.7) | copy-start | bytes 3145732
  180.4 6.2 %copy-start.24 = (bf16[1024,2048]{1,0:T(8,128)(2,1)S(1)}, bf16[1024,2048]{1,0:T(8,128)(2,1)}, u32[]{:S(2)}) copy-start(bf16[1024,2048]{1,0:T(8,128)(2,1)} %copy-done.23) | copy-start | bytes 12582916
  186.6 3.8 %copy-start.2 = (f32[1024,512]{1,0:T(8,128)S(1)}, f32[1024,512]{1,0:T(8,128)}, u32[]{:S(2)}) copy-start(f32[1024,512]{1,0:T(8,128)} %copy-done.1) | copy-start | bytes 6291460
  186.6 3.8 %copy-start.11 = (bf16[1024,256]{1,0:T(8,128)(2,1)S(1)}, bf16[1024,256]{1,0:T(8,128)(2,1)}, u32[]{:S(2)}) copy-start(bf16[1024,256]{1,0:T(8,128)(2,1)} %copy-done.10) | copy-start | bytes 1572868
  190.3 1.6 copy-start.13
  300.0 3.1 copy-start.6
  303.6 1.8 copy-start.12
  303.6 2.4 copy-start.9
  303.7 3.5 %copy-start.5 = (bf16[512,2048]{1,0:T(8,128)(2,1)S(1)}, bf16[512,2048]{1,0:T(8,128)(2,1)}, u32[]{:S(2)}) copy-start(bf16[512,2048]{1,0:T(8,128)(2,1)} %get-tuple-element.57) | copy-start | bytes 6291460
  307.1 3.2 %copy-start.4 = (bf16[2048,512]{1,0:T(8,128)(2,1)S(1)}, bf16[2048,512]{1,0:T(8,128)(2,1)}, u32[]{:S(2)}) copy-start(bf16[2048,512]{1,0:T(8,128)(2,1)} %get-tuple-element.58) | copy-start | bytes 6291460

commit v3 on v2

v3 whole, which is shorter than its diff:
```python
import functools

import jax
import jax.numpy as jnp
from jax import lax
from jax.experimental import pallas as pl
from jax.experimental.pallas import tpu as pltpu
from jax.sharding import PartitionSpec as P

D = 512
HEADS = 8
HEAD = 64
HL = HEADS // 2
C = HL * HEAD
PAIR = 128
NEG = -1e30
LOG2E = 1.4426950408889634
BQ = 256
BK = 256
F32 = jnp.float32
BF16 = jnp.bfloat16
MESH = pl.DeviceIdType.MESH
VMEM = pltpu.VMEM
SMEM = pltpu.SMEM


def norm_rows(value, gain, shift):
    center = value - jnp.mean(value, axis=-1, keepdims=True)
    spread = jnp.mean(center * center, axis=-1, keepdims=True)
    return center * lax.rsqrt(spread + 1e-05) * gain + shift


def gelu_exact(value):
    return jax.nn.gelu(value, approximate=False)


def product(left, right):
    return jnp.dot(left, right, preferred_element_type=F32)


def product_left(left, right):
    return lax.dot_general(left, right, (((0,), (0,)), ((), ())), preferred_element_type=F32)


def product_right(left, right):
    return lax.dot_general(left, right, (((1,), (1,)), ((), ())), preferred_element_type=F32)


def column_sums(value):
    return jnp.sum(value.astype(F32), axis=0)


def swap_kernel(x_ref, o_ref, send, recv, local):
    dp, me = lax.axis_index("dp"), lax.axis_index("seq")
    other = 1 - me
    barrier = pltpu.get_barrier_semaphore()
    pl.semaphore_signal(barrier, inc=1, device_id=(dp, other), device_id_type=MESH)
    pl.semaphore_wait(barrier, 1)
    whole = len(x_ref.shape) == 2
    copy = pltpu.make_async_remote_copy(
        src_ref=x_ref if whole else x_ref.at[other],
        dst_ref=o_ref.at[me],
        send_sem=send,
        recv_sem=recv,
        device_id=(dp, other),
        device_id_type=MESH,
    )
    copy.start()
    own = pltpu.make_async_copy(x_ref if whole else x_ref.at[me], o_ref.at[me], local)
    own.start()
    own.wait()
    copy.wait()


def swap(x, collective_id):
    shape = x.shape if x.ndim == 3 else (2,) + x.shape
    return pl.pallas_call(
        swap_kernel,
        out_shape=jax.ShapeDtypeStruct(shape, x.dtype),
        in_specs=[pl.BlockSpec(memory_space=VMEM)],
        out_specs=pl.BlockSpec(memory_space=VMEM),
        scratch_shapes=[pltpu.SemaphoreType.DMA] * 3,
        compiler_params=pltpu.CompilerParams(collective_id=collective_id, has_side_effects=True),
    )(x)


def rotation(len_ref, span):
    lengths = [len_ref[j] for j in range(len_ref.shape[0])]
    longest = functools.reduce(jnp.maximum, lengths)
    shift, total, ends = jnp.int32(0), jnp.int32(0), []
    for length in lengths:
        shift = jnp.where(length == longest, total, shift)
        total = total + length
        ends.append(total)
    turned = [e - shift for e in ends]
    return shift, [jnp.where(e <= 0, e + span, e) for e in turned]


def rows_from(ref, start, count):
    base = lax.div(start, 8) * 8
    r = start - base
    x = ref[pl.ds(base, count + 8), :]
    width = x.shape[1]
    row = lax.broadcasted_iota(jnp.int32, (1, 8, 1), 1)
    for bit in (1, 2, 4):
        by_eights = x.reshape(x.shape[0] // 8, 8, width)
        turned = pltpu.roll(by_eights, 8 - bit, axis=1)
        following = jnp.concatenate([turned[1:], turned[:1]], axis=0)
        moved = jnp.where(row < 8 - bit, turned, following).reshape(x.shape)
        x = jnp.where(jnp.full(x.shape, r & bit) != 0, moved, x)
    return x[:count]


def table_of(ends, position):
    start, end = jnp.zeros_like(position), jnp.full_like(position, 1 << 30)
    for e in ends:
        start = jnp.where(e <= position, jnp.maximum(start, e), start)
        end = jnp.where(e > position, jnp.minimum(end, e), end)
    return start, end


def tile_mask(ends, i):
    return table_of(ends, i * BQ + lax.broadcasted_iota(jnp.int32, (1, BQ), 1))


def head_masks():
    lane = lax.broadcasted_iota(jnp.int32, (1, PAIR), 1)
    low = (lane < HEAD).astype(F32).astype(BF16)
    return low, (lane >= HEAD).astype(F32).astype(BF16)


def by_eight(value, op):
    return op(value.reshape(value.shape[0] // 8, 8, value.shape[1]), axis=0)


def forward_kernel(
    pieces, len_ref, me_ref, slot_ref, loaded_ref, wq_ref, wk_ref, wv_ref, bq_ref, bv_ref,
    x_ref, q_ref, k_ref, v_ref, mixed_ref, out_ref, lse_ref, own_ref,
    vt_ref, acc_ref, s_ref, packed_ref, turned_ref,
):
    span = loaded_ref.shape[0]
    half, blocks = span // 2, span // BQ
    near = blocks // 2
    shift, ends = rotation(len_ref, span)
    count = pieces if pieces else 32
    piece = span // count

    def place(k, _):
        slot = slot_ref[k] if pieces else k % (count // 2)
        row = (k // (count // 2)) * half + slot * piece
        packed_ref[pl.ds(pl.multiple_of(row, piece), piece), :] = loaded_ref[
            pl.ds(pl.multiple_of(k * piece, piece), piece), :
        ].astype(F32)
        return 0

    lax.fori_loop(0, count, place, 0)
    packed_ref[span:, :] = packed_ref[: BQ + 8, :]
    own_ref[...] = packed_ref[pl.ds(pl.multiple_of(me_ref[0] * half, half), half), :].astype(BF16)

    def project(i, _):
        rows = pl.ds(pl.multiple_of(i * BQ, BQ), BQ)
        x = rows_from(packed_ref, lax.rem(i * BQ + shift, span), BQ).astype(BF16)
        x_ref[rows, :] = x
        q = (product(x, wq_ref[...]) + bq_ref[...].astype(F32)).astype(BF16)
        q_ref[rows, :] = (q.astype(F32) * (HEAD**-0.5)).astype(BF16)
        k_ref[rows, :] = product(x, wk_ref[...]).astype(BF16)
        v = (product(x, wv_ref[...]) + bv_ref[...].astype(F32)).astype(BF16)
        v_ref[rows, :] = v
        vt_ref[:, rows] = v.T
        return 0

    lax.fori_loop(0, blocks, project, 0)
    masks = head_masks()

    def query_block(masked, i, _):
        rows = pl.ds(pl.multiple_of(i * BQ, BQ), BQ)
        base = near if masked else 0
        if masked:
            start, end = tile_mask(ends, i)
        q = q_ref[rows, :]
        heads = [q[:, (h // 2) * PAIR : (h // 2 + 1) * PAIR] * masks[h % 2] for h in range(HL)]
        acc_ref[...] = jnp.zeros_like(acc_ref)

        def score_block(j, tops):
            keys = pl.ds(pl.multiple_of((base + j) * BK, BK), BK)
            if masked:
                kpos = (base + j) * BK + lax.broadcasted_iota(jnp.int32, (BK, BQ), 0)
                mask = (kpos >= start) & (kpos < end)
            new = []
            for h in range(HL):
                kp = k_ref[keys, (h // 2) * PAIR : (h // 2 + 1) * PAIR]
                s = product_right(kp, heads[h]) * LOG2E
                if masked:
                    s = jnp.where(mask, s, NEG)
                s_ref[h, pl.ds(pl.multiple_of(j * BK, BK), BK), :] = s
                new.append(jnp.maximum(tops[h], by_eight(s, jnp.max)))
            return tuple(new)

        tops = lax.fori_loop(
            0, near, score_block, tuple(jnp.full((8, BQ), NEG, F32) for _ in range(HL))
        )
        tops = [jnp.max(t, axis=0, keepdims=True) for t in tops]

        def mix_block(j, totals):
            keys = pl.ds(pl.multiple_of((base + j) * BK, BK), BK)
            new = []
            for h in range(HL):
                p = jnp.exp2(s_ref[h, pl.ds(pl.multiple_of(j * BK, BK), BK), :] - tops[h])
                new.append(totals[h] + by_eight(p, jnp.sum))
                lanes = slice(h * HEAD, (h + 1) * HEAD)
                acc_ref[lanes, :] += product(vt_ref[lanes, keys], p.astype(BF16))
            return tuple(new)

        totals = lax.fori_loop(
            0, near, mix_block, tuple(jnp.zeros((8, BQ), F32) for _ in range(HL))
        )
        for h in range(HL):
            total = jnp.sum(totals[h], axis=0, keepdims=True)
            lanes = slice(h * HEAD, (h + 1) * HEAD)
            acc_ref[lanes, :] = acc_ref[lanes, :] / total
            lse_ref[h : h + 1, rows] = tops[h] + jnp.log2(total)
        out = acc_ref[...]
        out_ref[:, rows] = out
        turned_ref[rows, :] = out.T
        return 0

    lax.fori_loop(0, near, functools.partial(query_block, False), 0)
    lax.fori_loop(near, blocks, functools.partial(query_block, True), 0)
    turned_ref[span:, :] = turned_ref[: BQ + 8, :]

    def turn_back(i, _):
        rows = pl.ds(pl.multiple_of(i * BQ, BQ), BQ)
        mixed_ref[rows, :] = rows_from(turned_ref, lax.rem(i * BQ + span - shift, span), BQ).astype(BF16)
        return 0

    lax.fori_loop(0, blocks, turn_back, 0)


def column_block(shape):
    return pl.BlockSpec(shape, lambda i, lengths, me, slots: (0, me[0]))


def whole_block(shape):
    return pl.BlockSpec(shape, lambda i, lengths, me, slots: (0,) * len(shape))


def attend_forward(x_all, pieces, lengths, me, slots, wq, wk, wv, bq, bv):
    span = x_all.shape[0]
    rows_shape = jax.ShapeDtypeStruct((span, C), BF16)
    return pl.pallas_call(
        functools.partial(forward_kernel, pieces),
        grid_spec=pltpu.PrefetchScalarGridSpec(
            num_scalar_prefetch=3,
            grid=(1,),
            in_specs=[
                whole_block((span, D)),
                column_block((D, C)),
                column_block((D, C)),
                column_block((D, C)),
                column_block((1, C)),
                column_block((1, C)),
            ],
            out_specs=[whole_block((span, D))] + [whole_block((span, C))] * 4
            + [whole_block((C, span)), whole_block((8, span)), whole_block((span // 2, D))],
            scratch_shapes=[
                VMEM((C, span), BF16),
                VMEM((C, BQ), F32),
                VMEM((HL, span // 2, BQ), F32),
                VMEM((span + BQ + 8, D), F32),
                VMEM((span + BQ + 8, C), F32),
            ],
        ),
        out_shape=[jax.ShapeDtypeStruct((span, D), BF16)] + [rows_shape] * 4
        + [jax.ShapeDtypeStruct((C, span), F32), jax.ShapeDtypeStruct((8, span), F32)]
        + [jax.ShapeDtypeStruct((span // 2, D), BF16)],
        name="attend_forward",
    )(lengths, me, slots, x_all, wq, wk, wv, bq.reshape(1, D), bv.reshape(1, D))


def backward_kernel(pieces, sums, *refs):
    len_ref, slot_ref, x_ref, q_ref, k_ref, v_ref, g_ref, out_ref, lse_ref = refs[:9]
    weights, res_ref = refs[9:12], refs[12]
    refs = refs[13:]
    if sums:
        raw, refs = refs[:3], refs[3:]
    gw_ref, sums_ref, ga_ref, gb_ref = refs[:4]
    refs = refs[4:]
    if sums:
        full, refs = refs[:3], refs[3:]
    kt_ref, gq_ref, gk_ref, gv_ref, gqt_ref, qs_ref, gs_ref, w_ref, ds_ref = refs[:9]
    term_ref, turned_ref, gx_ref = refs[9:12]
    me = lax.axis_index("seq")
    span = x_ref.shape[0]
    half, blocks = span // 2, span // BQ
    near = blocks // 2
    scale = HEAD**-0.5
    ticks = []
    if sums:
        acc_ref, landing_ref, send, recv = refs[12:]
        env = chip_links(send, recv)
        meet([env["partner"]] + [peer for peer, _ in env["axes"]] + env["stack"])
        lines = [
            Chunk(env, c, source, target, acc_ref.at[c], landing_ref.at[c], True).steps()
            for c, (source, target) in enumerate(square_blocks(raw, full))
        ]
        for c, line in enumerate(lines):
            for j, step in enumerate(line):
                at = c + 2 * j
                ticks += [[] for _ in range(at + 1 - len(ticks))]
                ticks[at].append(step)

    def tick(now, candidates):
        for t in candidates:
            if t < len(ticks):

                @pl.when(now == t)
                def _(t=t):
                    for step in ticks[t]:
                        step()

    def straight(candidates):
        for t in candidates:
            if t < len(ticks):
                for step in ticks[t]:
                    step()

    straight([0])
    shift, ends = rotation(len_ref, span)

    def prepare(i, _):
        rows = pl.ds(pl.multiple_of(i * BQ, BQ), BQ)
        kt_ref[:, rows] = k_ref[rows, :].T
        gk_ref[rows, :] = jnp.zeros((BQ, C), F32)
        gv_ref[rows, :] = jnp.zeros((BQ, C), F32)
        turned_ref[rows, :] = g_ref[rows, :].astype(F32)
        return 0

    lax.fori_loop(0, blocks, prepare, 0)
    turned_ref[span:, :] = turned_ref[: BQ + 8, :]
    straight([1])
    lane = lax.broadcasted_iota(jnp.int32, (1, C), 1) // HEAD
    masks = [(lane == h).astype(F32).astype(BF16) for h in range(HL)]

    def query_block(masked, i, _):
        rows = pl.ds(pl.multiple_of(i * BQ, BQ), BQ)
        base = near if masked else 0
        if masked:
            start, end = tile_mask(ends, i)
        q = q_ref[rows, :]
        exact = rows_from(turned_ref, lax.rem(i * BQ + shift, span), BQ)
        g = exact.astype(BF16)
        for h in range(HL):
            part = slice(h * BQ, (h + 1) * BQ)
            qs_ref[part, :] = q * masks[h]
            gs_ref[part, :] = g * masks[h]
        weighted = exact.T * out_ref[:, rows]
        inner = [
            jnp.sum(weighted[h * HEAD : (h + 1) * HEAD], axis=0, keepdims=True) for h in range(HL)
        ]
        logsum = [lse_ref[h : h + 1, rows] for h in range(HL)]
        gqt_ref[...] = jnp.zeros_like(gqt_ref)

        def key_block(j, _):
            keys = pl.ds(pl.multiple_of((base + j) * BK, BK), BK)
            here = pl.ds(pl.multiple_of(j * BK, BK), BK)
            if masked:
                kpos = (base + j) * BK + lax.broadcasted_iota(jnp.int32, (BK, BQ), 0)
                mask = (kpos >= start) & (kpos < end)
            for h in range(HL):
                part = slice(h * BQ, (h + 1) * BQ)
                pair = slice((h // 2) * PAIR, (h // 2 + 1) * PAIR)
                s = product_right(k_ref[keys, pair], qs_ref[part, pair])
                w = jnp.exp2(s * LOG2E - logsum[h])
                if masked:
                    w = jnp.where(mask, w, 0.0)
                gw = product_right(v_ref[keys, pair], gs_ref[part, pair])
                gs = (w * (gw - inner[h])).astype(BF16)
                w_ref[here, part] = w.astype(BF16)
                ds_ref[here, part] = gs
            return 0

        def product_block(j, _):
            keys = pl.ds(pl.multiple_of((base + j) * BK, BK), BK)
            here = pl.ds(pl.multiple_of(j * BK, BK), BK)
            for h in range(HL):
                part = slice(h * BQ, (h + 1) * BQ)
                lanes = slice(h * HEAD, (h + 1) * HEAD)
                gqt_ref[lanes, :] += product(kt_ref[lanes, keys], ds_ref[here, part])
            gv_ref[keys, :] += product(w_ref[here, :], gs_ref[...])
            gk_ref[keys, :] += product(ds_ref[here, :], qs_ref[...])
            return 0

        first = 2 + 2 * base
        lax.fori_loop(0, near, key_block, 0)
        tick(2 + 2 * i, range(first, first + 2 * near, 2))
        lax.fori_loop(0, near, product_block, 0)
        gq_ref[rows, :] = (gqt_ref[...].T * scale).astype(BF16)
        tick(3 + 2 * i, range(first + 1, first + 2 * near, 2))
        return 0

    lax.fori_loop(0, near, functools.partial(query_block, False), 0)
    lax.fori_loop(near, blocks, functools.partial(query_block, True), 0)

    columns = pl.ds(pl.multiple_of(me * C, C), C)
    after = 2 + 2 * blocks
    term_ref[...] = jnp.zeros_like(term_ref)
    sums_ref[...] = jnp.zeros_like(sums_ref)

    def gradients(i, _):
        rows = pl.ds(pl.multiple_of(i * BQ, BQ), BQ)
        parts = [gq_ref[rows, :], gk_ref[rows, :].astype(BF16), gv_ref[rows, :].astype(BF16)]
        x = x_ref[rows, :]
        for n, part in enumerate(parts):
            term_ref[n] += product_left(x, part)
        sums_ref[...] += jnp.concatenate(
            [jnp.sum(a.astype(F32), axis=0, keepdims=True) for a in (parts[0], parts[2])], axis=1
        )
        gx_ref[rows, :] = (
            product_right(parts[0], weights[0][:, columns])
            + product_right(parts[1], weights[1][:, columns])
            + product_right(parts[2], weights[2][:, columns])
        )
        tick(after + i, range(after, after + blocks))
        return 0

    lax.fori_loop(0, blocks, gradients, 0)
    gw_ref[...] = term_ref[...].astype(BF16)
    count = pieces if pieces else 32
    each = count // 2
    piece = span // count
    gx_ref[span:, :] = gx_ref[: piece + 8, :]

    def piece_rows(part, k):
        row = (slot_ref[part * each + k] if pieces else k) * piece
        return rows_from(gx_ref, lax.rem(part * half + row + span - shift, span), piece), row

    def own_piece(k, _):
        gx, row = piece_rows(me, k)
        ga_ref[pl.ds(pl.multiple_of(k * piece, piece), piece), :] = (
            gx + res_ref[pl.ds(row, piece), :]
        )
        return 0

    def other_piece(k, _):
        gx, _ = piece_rows(1 - me, k)
        gb_ref[pl.ds(pl.multiple_of(k * piece, piece), piece), :] = gx.astype(BF16)
        return 0

    lax.fori_loop(0, each, own_piece, 0)
    lax.fori_loop(0, each, other_piece, 0)
    straight(range(after + blocks, len(ticks)))


def attend_backward(lengths, slots, pieces, x, q, k, v, g, out, lse, wq, wk, wv, res, raw, collective_id):
    span = x.shape[0]
    vmem, smem = pl.BlockSpec(memory_space=VMEM), pl.BlockSpec(memory_space=SMEM)
    shape = jax.ShapeDtypeStruct
    sums = len(raw) > 0
    chunks = sum(a.size for a in raw) // (D * D)
    dma = pltpu.SemaphoreType.DMA
    comm = [VMEM((chunks, D, D), BF16)] * 2 + [dma((chunks, 12))] * 2 if sums else []
    params = dict(collective_id=collective_id, has_side_effects=True) if sums else {}
    return pl.pallas_call(
        functools.partial(backward_kernel, pieces, sums),
        out_shape=[
            shape((3, D, C), BF16),
            shape((1, 2 * C), F32),
            shape((span // 2, D), F32),
            shape((span // 2, D), BF16),
        ]
        + [shape(a.shape, BF16) for a in raw],
        in_specs=[smem] * 2 + [vmem] * (11 + len(raw)),
        out_specs=[vmem] * (4 + len(raw)),
        scratch_shapes=[
            VMEM((C, span), BF16),
            VMEM((span, C), BF16),
            VMEM((span, C), F32),
            VMEM((span, C), F32),
            VMEM((C, BQ), F32),
            VMEM((HL * BQ, C), BF16),
            VMEM((HL * BQ, C), BF16),
            VMEM((span // 2, HL * BQ), BF16),
            VMEM((span // 2, HL * BQ), BF16),
            VMEM((3, D, C), F32),
            VMEM((span + BQ + 8, C), F32),
            VMEM((span + span // (pieces if pieces else 32) + 8, D), F32),
        ]
        + comm,
        compiler_params=pltpu.CompilerParams(vmem_limit_bytes=63 << 20, **params),
        name="attend_backward",
    )(lengths, slots, x, q, k, v, g, out, lse, wq, wk, wv, res, *raw)


def arrange_kernel(groups, route_ref, x_ref, o_ref, slot_ref):
    for k in range(groups):
        packed = route_ref[k]
        group = packed // (2 * groups)
        o_ref[group] = x_ref[k]
        slot_ref[group] = jnp.full(slot_ref.shape[1:], packed % groups, jnp.int32)


def arrange(pieces, route):
    groups, piece, _ = pieces.shape
    return pl.pallas_call(
        functools.partial(arrange_kernel, groups),
        grid_spec=pltpu.PrefetchScalarGridSpec(
            num_scalar_prefetch=1,
            grid=(1,),
            in_specs=[pl.BlockSpec(pieces.shape, lambda i, r: (0, 0, 0))],
            out_specs=[
                pl.BlockSpec(pieces.shape, lambda i, r: (0, 0, 0)),
                pl.BlockSpec((groups, 8, 128), lambda i, r: (0, 0, 0)),
            ],
        ),
        out_shape=[
            jax.ShapeDtypeStruct(pieces.shape, BF16),
            jax.ShapeDtypeStruct((groups, 8, 128), jnp.int32),
        ],
        name="arrange",
    )(route, pieces)


def restore_kernel(groups, route_ref, x_ref, o_ref):
    for k in range(groups):
        o_ref[k] = x_ref[route_ref[k] // (2 * groups)]


def restore(pieces, route):
    spec = pl.BlockSpec(pieces.shape, lambda i, r: (0, 0, 0))
    return pl.pallas_call(
        functools.partial(restore_kernel, pieces.shape[0]),
        grid_spec=pltpu.PrefetchScalarGridSpec(
            num_scalar_prefetch=1, grid=(1,), in_specs=[spec], out_specs=spec
        ),
        out_shape=jax.ShapeDtypeStruct(pieces.shape, BF16),
        name="restore",
    )(route, pieces)


def far_first(n):
    return sorted(range(1, n), key=lambda k: abs(k - n // 2))


def dispatch_kernel(n, x_ref, slot_ref, o_ref, slots_ref, send, recv, ssend, srecv, fsend, frecv):
    dp, me = lax.axis_index("dp"), lax.axis_index("seq")
    partner = (dp, 1 - me)
    barrier = pltpu.get_barrier_semaphore()
    for k in range(1, n):
        pl.semaphore_signal(barrier, inc=1, device_id=((dp + k) % n, me), device_id_type=MESH)
    pl.semaphore_signal(barrier, inc=1, device_id=partner, device_id_type=MESH)
    pl.semaphore_wait(barrier, n)

    order = far_first(n)
    copies, small = {}, {}
    for k in order:
        p = (dp + k) % n
        copies[k] = push(x_ref.at[p], o_ref.at[me, dp], send.at[k], recv.at[k], (p, me))
        copies[k].start()
        small[k] = push(slot_ref.at[p], slots_ref.at[me, dp], ssend.at[k], srecv.at[k], (p, me))
        small[k].start()
    forwards = [push(x_ref.at[dp], o_ref.at[me, dp], fsend.at[0], frecv.at[0], partner)]
    forwards[0].start()
    o_ref[me, dp] = x_ref[dp]
    slots_ref[me, dp] = slot_ref[dp]
    for k in order:
        s = (dp + n - k) % n
        copies[k].wait_recv()
        forward = push(o_ref.at[me, s], o_ref.at[me, s], fsend.at[k], frecv.at[k], partner)
        forward.start()
        forwards.append(forward)
    for k in order:
        small[k].wait_recv()
    last = push(slots_ref.at[me], slots_ref.at[me], fsend.at[n], frecv.at[n], partner)
    last.start()
    forwards.append(last)
    for k in order:
        copies[k].wait_send()
        small[k].wait_send()
    for forward in forwards:
        forward.wait()


def dispatch(outgoing, slots, collective_id):
    n = outgoing.shape[0]
    vmem = pl.BlockSpec(memory_space=VMEM)
    return pl.pallas_call(
        functools.partial(dispatch_kernel, n),
        out_shape=[
            jax.ShapeDtypeStruct((2,) + outgoing.shape, BF16),
            jax.ShapeDtypeStruct((2,) + slots.shape, jnp.int32),
        ],
        in_specs=[vmem] * 2,
        out_specs=[vmem] * 2,
        scratch_shapes=[pltpu.SemaphoreType.DMA((n,))] * 4 + [pltpu.SemaphoreType.DMA((n + 1,))] * 2,
        compiler_params=pltpu.CompilerParams(collective_id=collective_id, has_side_effects=True),
        name="dispatch",
    )(outgoing, slots)


def push(src, dst, send, recv, device):
    return pltpu.make_async_remote_copy(
        src_ref=src, dst_ref=dst, send_sem=send, recv_sem=recv,
        device_id=device, device_id_type=MESH,
    )


def meet(peers):
    barrier = pltpu.get_barrier_semaphore()
    for peer in peers:
        pl.semaphore_signal(barrier, inc=1, device_id=peer, device_id_type=MESH)
    pl.semaphore_wait(barrier, len(peers))


def chip_links(send, recv):
    dp, me = lax.axis_index("dp"), lax.axis_index("seq")
    axes = []
    for w in (1 + me, 2 - me):
        bit = (dp // w) % 2
        axes.append(((dp + (1 - 2 * bit) * w, me), bit))
    return {
        "dp": dp,
        "me": me,
        "z": dp // 4,
        "partner": (dp, 1 - me),
        "axes": axes,
        "stack": [((dp + 4 * k) % 16, me) for k in range(1, 4)],
        "send": send,
        "recv": recv,
    }


def square_blocks(sources, targets):
    for source, target in zip(sources, targets):
        tall, wide = source.shape
        for r in range(tall // D):
            for c in range(wide // D):
                at = (pl.ds(r * D, D), pl.ds(c * D, D))
                yield source.at[at], target.at[at]


class Chunk:
    def __init__(self, env, number, source, full, acc, landing, shared):
        self.env, self.number, self.shared = env, number, shared
        self.source, self.full, self.acc, self.landing = source, full, acc, landing
        base, size, offset = 0, source.shape[0], 0
        self.levels = []
        for device, bit in ([(env["partner"], env["me"])] if shared else []) + env["axes"]:
            half = size // 2
            keep, give = base + bit * half, base + (1 - bit) * half
            self.levels.append((device, keep, give, half, offset))
            base, size, offset = keep, half, offset + half
        self.base, self.size, self.offset = base, size // 4, offset

    def copy(self, stage, src, dst, device):
        e = self.env
        return push(src, dst, e["send"].at[self.number, stage], e["recv"].at[self.number, stage], device)

    def at(self, ref, start, size):
        return ref.at[pl.ds(start if isinstance(start, int) else pl.multiple_of(start, 16), size), :]

    def halves(self, level):
        device, _, give, half, offset = self.levels[level]
        src = self.acc if level else self.source
        return [self.copy(level, self.at(src, give, half), self.at(self.landing, offset, half), device)]

    def add(self, level):
        _, keep, _, half, offset = self.levels[level]
        src = self.acc if level else self.source
        step = min(half, 64)

        def run(i, _):
            here = pl.ds(pl.multiple_of(keep + i * step, 16), step)
            there = pl.ds(pl.multiple_of(offset + i * step, 16), step)
            total = src[here, :].astype(F32) + self.landing[there, :].astype(F32)
            self.acc[here, :] = total.astype(BF16)
            return 0

        lax.fori_loop(0, half // step, run, 0)

    def quarters(self):
        copies = []
        for k in range(1, 4):
            z = (self.env["z"] + k) % 4
            copies.append(
                self.copy(
                    len(self.levels) + k - 1,
                    self.at(self.acc, self.base + z * self.size, self.size),
                    self.at(self.landing, self.offset + (k - 1) * self.size, self.size),
                    self.env["stack"][k - 1],
                )
            )
        return copies

    def total(self):
        here = pl.ds(pl.multiple_of(self.base + self.env["z"] * self.size, 16), self.size)
        total = self.acc[here, :].astype(F32)
        for k in range(3):
            there = slice(self.offset + k * self.size, self.offset + (k + 1) * self.size)
            total += self.landing[there, :].astype(F32)
        self.full[here, :] = total.astype(BF16)

    def gathers(self):
        region = self.at(self.full, self.base + self.env["z"] * self.size, self.size)
        first = len(self.levels) + 3
        return [self.copy(first + k, region, region, self.env["stack"][k]) for k in range(3)]

    def spread(self, level):
        device, keep, _, half, _ = self.levels[level]
        region = self.at(self.full, keep, half)
        return [self.copy(len(self.levels) + 6 + level, region, region, device)]

    def hand_over(self):
        return [self.copy(2 * len(self.levels) + 6, self.full, self.full, self.env["partner"])]

    def steps(self):
        count = len(self.levels)
        stages = [functools.partial(self.halves, n) for n in range(count)] + [self.quarters, self.gathers]
        stages += [functools.partial(self.spread, n) for n in range(count - 1, -1, -1)]
        between = [functools.partial(self.add, n) for n in range(count)] + [self.total]
        if not self.shared:
            stages.append(self.hand_over)

        def step(n):
            if n > 0:
                for copy in stages[n - 1]():
                    copy.wait()
                if n - 1 < len(between):
                    between[n - 1]()
            if n < len(stages):
                for copy in stages[n]():
                    copy.start()

        return [functools.partial(step, n) for n in range(len(stages) + 1)]


def final_kernel(
    ga_ref, gb_ref, qkv_ref, vec_ref,
    back_ref, qkv_full, vec_full,
    ret_ref, gbr_ref, acc_ref, landing_ref, vec_recv,
    send, recv, asend, arecv, gsend, grecv, vsend, vrecv,
):
    n = 16
    rows = ga_ref.shape[0]
    piece = rows // n
    env = chip_links(send, recv)
    dp, me, partner = env["dp"], env["me"], env["partner"]
    meet([((dp + k) % n, me) for k in range(1, n)] + [partner])

    quarter = rows // 4
    halves = []
    for j in range(4):
        part = pl.ds(j * quarter, quarter)
        copy = push(gb_ref.at[part, :], gbr_ref.at[part, :], gsend.at[j], grecv.at[j], partner)
        copy.start()
        halves.append(copy)

    lines = []
    for c in range(3):
        lines.append(
            Chunk(
                env, c, qkv_ref.at[c], qkv_full.at[me, c], acc_ref.at[c], landing_ref.at[c], False
            ).steps()
        )
    peers = [partner]
    for w in (1, 2, 4, 8):
        bit = (dp // w) % 2
        peers.append((dp + (1 - 2 * bit) * w, me))
    vec_copies = []

    def vec_step(s):
        if s == 0:
            vec_full[...] = vec_ref[...]
        else:
            vec_copies[-1].wait()
            vec_full[...] += vec_recv[s - 1]
        if s < len(peers):
            sent = vec_recv.at[len(peers) + s]
            sent[...] = vec_full[...]
            copy = push(sent, vec_recv.at[s], vsend.at[s], vrecv.at[s], peers[s])
            copy.start()
            vec_copies.append(copy)

    lines.append([functools.partial(vec_step, s) for s in range(len(peers) + 1)])

    returns = []

    def give_back():
        for j in range(4):
            halves[j].wait()

            def add(i, _, j=j):
                here = pl.ds(pl.multiple_of(j * quarter + i * 64, 64), 64)
                ret_ref[here, :] = (ga_ref[here, :] + gbr_ref[here, :].astype(F32)).astype(BF16)
                return 0

            lax.fori_loop(0, quarter // 64, add, 0)
        mine = pl.ds(pl.multiple_of(dp * piece, piece), piece)
        for k in far_first(n):
            p = (dp + k) % n
            theirs = pl.ds(pl.multiple_of(p * piece, piece), piece)
            copy = push(
                ret_ref.at[theirs, :], back_ref.at[mine, :], asend.at[k], arecv.at[k], (p, me)
            )
            copy.start()
            returns.append(copy)
        back_ref[mine, :] = ret_ref[mine, :]

    ticks = max(len(line) for line in lines)
    for t in range(ticks):
        for line in lines:
            if t < len(line):
                line[t]()
        if t == 0:
            give_back()
    for copy in returns:
        copy.wait()


def give_back_and_sum(ga, gb, qkv, vec, collective_id):
    vmem = pl.BlockSpec(memory_space=VMEM)
    shape = jax.ShapeDtypeStruct
    dma = pltpu.SemaphoreType.DMA
    return pl.pallas_call(
        final_kernel,
        out_shape=[shape(gb.shape, BF16), shape((2,) + qkv.shape, BF16), shape(vec.shape, F32)],
        in_specs=[vmem] * 4,
        out_specs=[vmem] * 3,
        scratch_shapes=[
            VMEM(gb.shape, BF16),
            VMEM(gb.shape, BF16),
            VMEM((3, D, C), BF16),
            VMEM((3, D, C), BF16),
            VMEM((10,) + vec.shape, F32),
            dma((3, 12)), dma((3, 12)),
            dma((16,)), dma((16,)),
            dma((4,)), dma((4,)),
            dma((5,)), dma((5,)),
        ],
        compiler_params=pltpu.CompilerParams(collective_id=collective_id, has_side_effects=True),
        name="give_back_and_sum",
    )(ga, gb, qkv, vec)


def body(
    tokens,
    route,
    lengths,
    query_weight,
    query_bias,
    key_weight,
    value_weight,
    value_bias,
    output_weight,
    output_bias,
    first_gain,
    first_shift,
    up_weight,
    up_bias,
    down_weight,
    down_bias,
    second_gain,
    second_shift,
    cotangent,
):
    groups = lax.axis_size("dp")
    rows = tokens.shape[0]
    piece = rows // groups
    span = rows * lax.axis_size("seq")
    seq = lax.axis_index("seq")
    tables = lengths[0]
    me = seq.reshape(1).astype(jnp.int32)
    kernels = groups == 16 and piece % 16 == 0
    if kernels:
        pieces = 2 * groups
        outgoing, slots_out = arrange(tokens.reshape(groups, piece, D), route)
        x_all, slots_all = dispatch(outgoing, slots_out, 0)
        x_all = x_all.reshape(span, D)
        slots = slots_all[:, :, 0, 0].reshape(pieces)
    else:
        pieces = 0
        target = route // groups // lax.axis_size("seq")
        place = route % groups
        outgoing = jnp.zeros((groups, piece, D), BF16).at[target].set(tokens.reshape(groups, piece, D))
        slots_out = jnp.zeros((groups,), jnp.int32).at[target].set(place)
        incoming, slots = (
            lax.all_to_all(outgoing, "dp", split_axis=0, concat_axis=0, tiled=True),
            lax.all_to_all(slots_out, "dp", split_axis=0, concat_axis=0, tiled=True),
        )
        inputs = jnp.zeros_like(incoming).at[slots].set(incoming).reshape(rows, D)
        x_all = swap(inputs, 0).reshape(span, D)
    x_turned, q, k, v, mixed_all, attend_out, lse, inputs = attend_forward(
        x_all, pieces, tables, me, slots,
        query_weight, key_weight, value_weight, query_bias, value_bias,
    )
    mixed_halves = swap(mixed_all.reshape(2, rows, C), 1)
    mixed = jnp.concatenate([mixed_halves[0], mixed_halves[1]], axis=1)
    branch = product(mixed, output_weight) + output_bias
    residual = inputs.astype(F32) + branch
    first, first_back = jax.vjp(
        norm_rows, residual, first_gain.astype(F32), first_shift.astype(F32)
    )
    first_low = first.astype(BF16)
    hidden = product(first_low, up_weight) + up_bias
    active = gelu_exact(hidden).astype(BF16)
    update = product(active, down_weight) + down_bias
    layer_out, second_back = jax.vjp(
        norm_rows, first + update, second_gain.astype(F32), second_shift.astype(F32)
    )
    grad_second, grad_second_gain, grad_second_shift = second_back(cotangent.astype(F32))
    grad_update = grad_second.astype(BF16)
    again = product(first_low, up_weight) + up_bias
    active_again, gelu_back = jax.vjp(gelu_exact, again)
    active_low = active_again.astype(BF16)
    grad_down = product_left(active_low, grad_update)
    grad_down_bias = column_sums(grad_update)
    (grad_active,) = gelu_back(product_right(grad_update, down_weight))
    grad_hidden = grad_active.astype(BF16)
    grad_up = product_left(first_low, grad_hidden)
    grad_up_bias = column_sums(grad_hidden)
    grad_first = grad_second + product_right(grad_hidden, up_weight)
    grad_residual, grad_first_gain, grad_first_shift = first_back(grad_first)
    grad_branch = grad_residual.astype(BF16)
    grad_output = product_left(mixed, grad_branch)
    grad_output_bias = column_sums(grad_branch)
    grad_mixed = product_right(grad_branch, output_weight).astype(BF16)
    grad_halves = jnp.stack([grad_mixed[:, :C], grad_mixed[:, C:]])
    grad_mixed_all = swap(grad_halves, 2).reshape(span, C)
    raw = [a.astype(BF16) for a in (grad_up, grad_down, grad_output)] if kernels else []
    grad_columns, column_parts, grad_own, grad_other, *summed = attend_backward(
        tables, slots, pieces, x_turned, q, k, v, grad_mixed_all, attend_out, lse,
        query_weight, key_weight, value_weight, grad_residual, raw, 3,
    )

    def own_columns(part):
        return lax.dynamic_update_slice(jnp.zeros((1, D), F32), part, (0, seq * C))

    vec = jnp.concatenate(
        [
            own_columns(column_parts[:, :C]),
            own_columns(column_parts[:, C:]),
            jnp.stack(
                [
                    grad_output_bias,
                    grad_first_gain,
                    grad_first_shift,
                    grad_down_bias,
                    grad_second_gain,
                    grad_second_shift,
                ]
            ),
            grad_up_bias.reshape(-1, D),
            jnp.zeros((4, D), F32),
        ]
    )
    if kernels:
        back, columns, vec = give_back_and_sum(grad_own, grad_other, grad_columns, vec, 4)
        token_grad = restore(back.reshape(groups, piece, D), route).reshape(rows, D)
        up_sum, down_sum, out_sum = (a.astype(F32) for a in summed)
        columns = jnp.concatenate([columns[0], columns[1]], axis=2).astype(F32)
    else:
        grad_inputs = grad_own + swap(jnp.stack([grad_other, grad_other]), 5)[1 - seq].astype(F32)
        back_rows = grad_inputs.astype(BF16).reshape(groups, piece, D)[slots]
        returned = lax.all_to_all(back_rows, "dp", split_axis=0, concat_axis=0, tiled=True)
        token_grad = returned[target].reshape(rows, D)
        up_sum, down_sum, out_sum, vec = lax.psum((grad_up, grad_down, grad_output, vec), ("dp", "seq"))
        columns = lax.psum(grad_columns.astype(F32), "dp")
        columns = lax.all_gather(columns, "seq", axis=2, tiled=True)
    query_sum, key_sum, value_sum = columns[0], columns[1], columns[2]
    return (
        layer_out.astype(BF16),
        token_grad,
        query_sum,
        vec[0],
        key_sum,
        value_sum,
        vec[1],
        out_sum,
        vec[2],
        vec[3],
        vec[4],
        up_sum,
        vec[8:12].reshape(-1),
        down_sum,
        vec[5],
        vec[6],
        vec[7],
    )


def solution(mesh):
    both, one = P(("dp", "seq"), None), P()
    return jax.shard_map(
        body,
        mesh=mesh,
        in_specs=(both, P(("dp", "seq")), P("dp", None)) + (one,) * 15 + (both,),
        out_specs=(both, both) + (one,) * 15,
        check_vma=False,
    )
```

time: 314 us -> 286 us (0.911)
  Pallas kernels: 235 us -> 207 us
    pallas_call x2, Pallas kernels: 155 us -> 125 us  [the longest x1 71.9 us: attend_backward(): pl.pallas_call(functools.partial(backward_kernel, pieces, sums), out_shap...]
where the time goes in v3:
time: 286 us
  Pallas kernels  207 us (72%)
  matrix products  49.1 us (17%)
  other arithmetic  15.1 us (5%)
  local copies, waits for them, and re-layouts  13.1 us (5%)
    pallas_call x1, Pallas kernels, attend_backward(): pl.pallas_call(functools.partial(backward_kernel, pieces, sums), out_shap...  71.9 us
    pallas_call x1, Pallas kernels, give_back_and_sum(): pl.pallas_call(final_kernel, out_shape=[shape(gb.shape, BF16), shape((2,)...  53.6 us
    pallas_call x1, Pallas kernels, dispatch(): pl.pallas_call(functools.partial(dispatch_kernel, n), out_shape=[jax.Shap...  34.5 us
    pallas_call x1, Pallas kernels, attend_forward(): pl.pallas_call(functools.partial(forward_kernel, pieces), grid_spec=pltpu...  33.1 us
    dot_general x3, matrix products, product(): return jnp.dot(left, right, preferred_element_type=F32)  25.4 us
    dot_general x3, matrix products, product_left(): lax.dot_general(left, right, (((0,), (0,)), ((), ())), preferred_element_...  12.1 us
    dot_general x3, matrix products, product_right(): lax.dot_general(left, right, (((1,), (1,)), ((), ())), preferred_element_...  11.6 us
    pallas_call x2, Pallas kernels, swap(): pl.pallas_call(swap_kernel, out_shape=jax.ShapeDtypeStruct(shape, x.dtype...  8.36 us

profile of v3, /device:TPU:0, one launch (start us, length us, event | category | flops | bytes accessed | tf_op | source)
XLA Modules:
  0.0 285.7 jit_solution(1325235333051111392)
XLA Ops:
  0.7 0.7 convert_element_type.87
  1.4 0.7 convert_element_type.85
  2.8 3.0 %arrange.1 = (bf16[16,64,512]{2,1,0:T(8,128)(2,1)}, s32[16,8,128]{2,1,0:T(8,128)}) custom-call(s32[16]{0:T(128)} %route_ref.3, bf16[16,64,512]{2,1,0:T(8,128)(2,1)} %bitcast.59), custom_call_target="tpu_custom_call" | custom-call | tf_op jit(solution)/shard_map/arrange/pallas_call | solution.py:504
  5.8 34.5 %dispatch.1 = (bf16[2,16,64,512]{3,2,1,0:T(8,128)(2,1)}, s32[2,16,8,128]{3,2,1,0:T(8,128)}) custom-call(bf16[16,64,512]{2,1,0:T(8,128)(2,1)} %get-tuple-element.39.x_ref, s32[16,8,128]{2,1,0:T(8,128)} %get-tuple-element.40.slot_ref), custom_call_target="tpu_custom_call" | custom-call | tf_op jit(solution)/shard_map/dispatch/pallas_call | solution.py:586
  40.3 1.6 slice_reduce_fusion
  43.6 33.1 %attend_forward.1 = (bf16[2048,512]{1,0:T(8,128)(2,1)}, bf16[2048,256]{1,0:T(8,128)(2,1)}, bf16[2048,256]{1,0:T(8,128)(2,1)}, bf16[2048,256]{1,0:T(8,128)(2,1)},...) custom-call(s32[6]{0:T(128)} %bitcast.66, s32[1]{0:T(128)} %bitcast.1.me_ref, ...), custom_call_target="tpu_custom_call" | custom-call | tf_op jit(solution)/shard_map/attend_forward/pallas_call | solution.py:250
  76.7 4.2 %shard_map.314 = bf16[2,1024,256]{2,1,0:T(8,128)(2,1)} custom-call(bf16[2,1024,256]{2,1,0:T(8,128)(2,1)} %bitcast.60), custom_call_target="tpu_custom_call" | custom-call | tf_op jit(solution)/shard_map/pallas_call | solution.py:77
  80.9 1.3 slice_bitcast_fusion.8
  82.3 0.8 fusion.24
  83.6 1.9 copy-done.20
  85.4 21.9 %multiply_convert_fusion = (bf16[1024,2048]{1,0:T(8,128)(2,1)S(1)}, f32[1024,2048]{1,0:T(8,128)S(1)}, f32[1024,2048]{1,0:T(8,128)}) fusion(f32[2048]{0:T(1024)S(1)} %convert_element_type.85, bf16[512,2048]{1,0:T(8,128)(2,1)S(1)} %copy-done.20, f32[1024,512]{1,0:T(8,128)S(1)} %get-tuple-element.96, f32[512]{0:T(512)S(1)} %convert_element_type.83, ...), kind=kOutput, calls=%fused_computation.4 | convolution fusion | flops 2288517120 | bytes 25186304 | tf_op jit(solution)/shard_map/dot_general | solution.py:38
  107.4 2.7 fusion.25
  111.3 1.0 fusion.9
  112.3 2.0 fusion.21
  114.6 7.8 %convert_reduce_fusion = (f32[2048]{0:T(1024)S(1)}, bf16[1024,2048]{1,0:T(8,128)(2,1)S(1)}) fusion(f32[1024,2048]{1,0:T(8,128)S(1)} %get-tuple-element.76, bf16[1024,512]{1,0:T(8,128)(2,1)S(1)} %get-tuple-element.68, bf16[2048,512]{1,0:T(8,128)(2,1)S(1)} %copy-done.19, f32[1024,2048]{1,0:T(8,128)} %get-tuple-element.97, f32[2048]{0:T(1024)S(1)} %convert_element_type.85), kind=kOutput, calls=%fused_computation.2 | convolution fusion | flops 2183133184 | bytes 24133632 | tf_op jit(solution)/shard_map/dot_general | solution.py:46
  122.4 3.0 %multiply_reduce_fusion = (f32[512]{0:T(512)S(1)}, f32[1024]{0:T(1024)S(1)}, f32[512]{0:T(512)S(1)}, f32[1024,512]{1,0:T(8,128)S(1)}) fusion(f32[1024,512]{1,0:T(8,128)S(1)} %get-tuple-element.96, f32[1024]{0:T(1024)S(1)} %fusion.11, f32[1024]{0:T(1024)S(1)} %broadcast_multiply_fusion.1, f32[512]{0:T(512)S(1)} %convert_element_type.82, ...), kind=kOutput, calls=%fused_computation.30 | convolution fusion | flops 2152724480 | bytes 12605440 | tf_op jit(solution)/shard_map/dot_general | solution.py:46
  125.5 0.8 fusion.20
  126.6 0.7 convolution_convert_fusion.2
  127.4 1.1 pad_maximum_fusion.1.x_ref
  128.5 4.1 %shard_map.315 = bf16[2,1024,256]{2,1,0:T(8,128)(2,1)} custom-call(bf16[2,1024,256]{2,1,0:T(8,128)(2,1)} %pad_maximum_fusion.1.x_ref), custom_call_target="tpu_custom_call" | custom-call | tf_op jit(solution)/shard_map/pallas_call | solution.py:77
  132.6 6.8 %convolution_convert_fusion.1.refs_13_ = bf16[512,2048]{1,0:T(8,128)(2,1)} fusion(bf16[1024,2048]{1,0:T(8,128)(2,1)} %copy-done.24, f32[1024,512]{1,0:T(8,128)} %copy-done.2, f32[512]{0:T(512)S(1)} %convert_element_type.83, f32[512]{0:T(512)S(1)} %convert_element_type.82, f32[1024]{0:T(1024)S(1)} %fusion.11, f32[1024]{0:T(1024)S(1)} %broadcast_multiply_fusion.1), kind=kOutput, calls=%fused_computation.24 | convolution fusion | flops 2151153664 | bytes 8400896 | tf_op jit(solution)/shard_map/dot_general | solution.py:42
  139.5 3.8 %convolution_convert_fusion.refs_14_ = bf16[2048,512]{1,0:T(8,128)(2,1)} fusion(bf16[1024,2048]{1,0:T(8,128)(2,1)S(1)} %copy-done.23, bf16[1024,512]{1,0:T(8,128)(2,1)S(1)} %copy-done.8), kind=kOutput, calls=%fused_computation.23 | convolution fusion | flops 2148532224 | bytes 7340032 | tf_op jit(solution)/shard_map/dot_general | solution.py:42
  143.2 1.5 convolution_convert_fusion.3.refs_15_
  144.8 71.9 %attend_backward.1 = (bf16[3,512,256]{2,1,0:T(8,128)(2,1)}, f32[1,512]{1,0:T(1,128)}, f32[1024,512]{1,0:T(8,128)}, bf16[1024,512]{1,0:T(8,128)(2,1)}, bf16[512,2...) custom-call(s32[6]{0:T(128)} %bitcast.67, s32[32]{0:T(128)} %reshape_squeeze.3.slot_ref.refs_1_, ...), custom_call_target="tpu_custom_call" | custom-call | tf_op jit(solution)/shard_map/attend_backward/pallas_call | solution.py:463
  216.7 0.7 slice_dynamic-update-slice_fusion.1
  218.0 1.3 concatenate.10.vec_ref
  219.3 53.6 %give_back_and_sum.1 = (bf16[1024,512]{1,0:T(8,128)(2,1)}, bf16[2,3,512,256]{3,2,1,0:T(8,128)(2,1)}, f32[16,512]{1,0:T(8,128)}) custom-call(f32[1024,512]{1,0:T(8,128)} %get-tuple-element.51.ga_ref, bf16[1024,512]{1,0:T(8,128)(2,1)} %get-tuple-element.52.gb_ref, bf16[3,512,256]{2,1,0:T(8,128)(2,1)} %get-tuple-element.53.qkv_ref, f32[16,512]{1,0:T(8,128)} %concatenate.10.vec_ref), custom_call_target="tpu_custom_call" | custom-call | tf_op jit(solution)/shard_map/give_back_and_sum/pallas_call | solution.py:823
  272.8 3.1 %restore.1 = bf16[16,64,512]{2,1,0:T(8,128)(2,1)} custom-call(s32[16]{0:T(128)} %route_ref.3, bf16[16,64,512]{2,1,0:T(8,128)(2,1)} %bitcast.58), custom_call_target="tpu_custom_call" | custom-call | tf_op jit(solution)/shard_map/restore/pallas_call | solution.py:530
  276.5 1.7 slice_bitcast_fusion
  278.8 1.1 convert_element_type.103
  279.9 2.5 convert_element_type.104
  283.1 2.6 convert_element_type.105
  (80 shorter events, 7.2 us)
Async XLA Ops:
  0.7 81.6 %copy-start = (bf16[512,512]{1,0:T(8,128)(2,1)S(1)}, bf16[512,512]{1,0:T(8,128)(2,1)}, u32[]{:S(2)}) copy-start(bf16[512,512]{1,0:T(8,128)(2,1)} %param.27) | copy-start | bytes 1572868
  0.7 41.8 %copy-start.13 = (bf16[512]{0:T(512)(128)(2,1)S(1)}, bf16[512]{0:T(512)(128)(2,1)}, u32[]{:S(2)}) copy-start(bf16[512]{0:T(512)(128)(2,1)} %param.23) | copy-start | bytes 3076
  0.7 42.3 %copy-start.14 = (bf16[512]{0:T(512)(128)(2,1)S(1)}, bf16[512]{0:T(512)(128)(2,1)}, u32[]{:S(2)}) copy-start(bf16[512]{0:T(512)(128)(2,1)} %param.26) | copy-start | bytes 3076
  76.7 5.5 %copy-start.21 = (bf16[1024,512]{1,0:T(8,128)(2,1)S(1)}, bf16[1024,512]{1,0:T(8,128)(2,1)}, u32[]{:S(2)}) copy-start(bf16[1024,512]{1,0:T(8,128)(2,1)} %get-tuple-element.43) | copy-start | bytes 3145732
  82.2 0.9 copy-start.10
  82.2 0.9 copy-start.15
  82.3 0.9 copy-start.16
  83.1 42.4 %copy-start.2 = (f32[1024,512]{1,0:T(8,128)}, f32[1024,512]{1,0:T(8,128)S(1)}, u32[]{:S(2)}) copy-start(f32[1024,512]{1,0:T(8,128)S(1)} %get-tuple-element.96) | copy-start | bytes 6291460
  83.1 2.4 copy-start.20
  85.4 21.9 %copy-start.19 = (bf16[2048,512]{1,0:T(8,128)(2,1)S(1)}, bf16[2048,512]{1,0:T(8,128)(2,1)}, u32[]{:S(2)}) copy-start(bf16[2048,512]{1,0:T(8,128)(2,1)} %param.33) | copy-start | bytes 6291460
  107.3 2.7 copy-start.22
  110.1 0.7 copy-start.17
  110.1 1.2 copy-start.3
  110.5 1.8 copy-start.18
  114.6 7.8 %copy-start.7 = (bf16[1024,512]{1,0:T(8,128)(2,1)}, bf16[1024,512]{1,0:T(8,128)(2,1)S(1)}, u32[]{:S(2)}) copy-start(bf16[1024,512]{1,0:T(8,128)(2,1)S(1)} %get-tuple-element.68) | copy-start | bytes 3145732
  122.4 3.0 %copy-start.24 = (bf16[1024,2048]{1,0:T(8,128)(2,1)}, bf16[1024,2048]{1,0:T(8,128)(2,1)S(1)}, u32[]{:S(2)}) copy-start(bf16[1024,2048]{1,0:T(8,128)(2,1)S(1)} %get-tuple-element.102) | copy-start | bytes 12582916
  126.6 16.7 %copy-start.1 = (f32[1024,512]{1,0:T(8,128)}, f32[1024,512]{1,0:T(8,128)S(1)}, u32[]{:S(2)}) copy-start(f32[1024,512]{1,0:T(8,128)S(1)} %get-tuple-element.70.refs_12_) | copy-start | bytes 6291460
  132.6 6.8 %copy-start.8 = (bf16[1024,512]{1,0:T(8,128)(2,1)S(1)}, bf16[1024,512]{1,0:T(8,128)(2,1)}, u32[]{:S(2)}) copy-start(bf16[1024,512]{1,0:T(8,128)(2,1)} %copy-done.7) | copy-start | bytes 3145732
  132.6 6.8 %copy-start.23 = (bf16[1024,2048]{1,0:T(8,128)(2,1)S(1)}, bf16[1024,2048]{1,0:T(8,128)(2,1)}, u32[]{:S(2)}) copy-start(bf16[1024,2048]{1,0:T(8,128)(2,1)} %copy-done.22) | copy-start | bytes 12582916
  139.5 3.8 %copy-start.11 = (bf16[1024,256]{1,0:T(8,128)(2,1)S(1)}, bf16[1024,256]{1,0:T(8,128)(2,1)}, u32[]{:S(2)}) copy-start(bf16[1024,256]{1,0:T(8,128)(2,1)} %copy-done.10) | copy-start | bytes 1572868
  272.8 3.1 %copy-start.6 = (bf16[2,3,512,256]{3,2,1,0:T(8,128)(2,1)S(1)}, bf16[2,3,512,256]{3,2,1,0:T(8,128)(2,1)}, u32[]{:S(2)}) copy-start(bf16[2,3,512,256]{3,2,1,0:T(8,128)(2,1)} %get-tuple-element.56) | copy-start | bytes 4718596
  276.5 1.8 copy-start.12
  276.5 2.4 copy-start.9
  276.5 3.5 %copy-start.5 = (bf16[512,2048]{1,0:T(8,128)(2,1)S(1)}, bf16[512,2048]{1,0:T(8,128)(2,1)}, u32[]{:S(2)}) copy-start(bf16[512,2048]{1,0:T(8,128)(2,1)} %get-tuple-element.59) | copy-start | bytes 6291460
  279.9 3.2 %copy-start.4 = (bf16[2048,512]{1,0:T(8,128)(2,1)S(1)}, bf16[2048,512]{1,0:T(8,128)(2,1)}, u32[]{:S(2)}) copy-start(bf16[2048,512]{1,0:T(8,128)(2,1)} %get-tuple-element.60) | copy-start | bytes 6291460

commit v4 on v3

--- a/solution.py
+++ b/solution.py
@@ -17,6 +17,7 @@
 LOG2E = 1.4426950408889634
 BQ = 256
 BK = 256
+PACE = 1.2
 F32 = jnp.float32
 BF16 = jnp.bfloat16
 MESH = pl.DeviceIdType.MESH
@@ -56,24 +57,25 @@
     barrier = pltpu.get_barrier_semaphore()
     pl.semaphore_signal(barrier, inc=1, device_id=(dp, other), device_id_type=MESH)
     pl.semaphore_wait(barrier, 1)
-    whole = len(x_ref.shape) == 2
-    copy = pltpu.make_async_remote_copy(
-        src_ref=x_ref if whole else x_ref.at[other],
-        dst_ref=o_ref.at[me],
-        send_sem=send,
-        recv_sem=recv,
-        device_id=(dp, other),
-        device_id_type=MESH,
-    )
+    rows, width = o_ref.shape
+    if x_ref.shape == (2 * rows, width // 2):
+        target = o_ref.at[:, pl.ds(pl.multiple_of(me * (width // 2), width // 2), width // 2)]
+        sources = [x_ref.at[pl.ds(pl.multiple_of(d * rows, rows), rows), :] for d in (other, me)]
+    elif x_ref.shape == (rows // 2, 2 * width):
+        target = o_ref.at[pl.ds(pl.multiple_of(me * (rows // 2), rows // 2), rows // 2), :]
+        sources = [x_ref.at[:, pl.ds(pl.multiple_of(d * width, width), width)] for d in (other, me)]
+    else:
+        target = o_ref.at[pl.ds(pl.multiple_of(me * (rows // 2), rows // 2), rows // 2), :]
+        sources = [x_ref, x_ref]
+    copy = push(sources[0], target, send, recv, (dp, other))
     copy.start()
-    own = pltpu.make_async_copy(x_ref if whole else x_ref.at[me], o_ref.at[me], local)
+    own = pltpu.make_async_copy(sources[1], target, local)
     own.start()
     own.wait()
     copy.wait()
 
 
-def swap(x, collective_id):
-    shape = x.shape if x.ndim == 3 else (2,) + x.shape
+def swap(x, shape, collective_id):
     return pl.pallas_call(
         swap_kernel,
         out_shape=jax.ShapeDtypeStruct(shape, x.dtype),
@@ -282,11 +284,11 @@
     weights, res_ref = refs[9:12], refs[12]
     refs = refs[13:]
     if sums:
-        raw, refs = refs[:3], refs[3:]
+        raw, vec_ref = refs[:3], refs[3]
+        full, back_ref, qkv_full, vec_full = refs[4:7], refs[7], refs[8], refs[9]
+        refs = refs[10:]
     gw_ref, sums_ref, ga_ref, gb_ref = refs[:4]
     refs = refs[4:]
-    if sums:
-        full, refs = refs[:3], refs[3:]
     kt_ref, gq_ref, gk_ref, gv_ref, gqt_ref, qs_ref, gs_ref, w_ref, ds_ref = refs[:9]
     term_ref, turned_ref, gx_ref = refs[9:12]
     me = lax.axis_index("seq")
@@ -294,37 +296,43 @@
     half, blocks = span // 2, span // BQ
     near = blocks // 2
     scale = HEAD**-0.5
+    columns = pl.ds(pl.multiple_of(me * C, C), C)
     ticks = []
     if sums:
-        acc_ref, landing_ref, send, recv = refs[12:]
+        acc_ref, landing_ref, acc_own, landing_own, gbr_ref, arrived_ref, vec_recv = refs[12:19]
+        send, recv, asend, arecv, gsend, grecv, vsend, vrecv = refs[19:]
         env = chip_links(send, recv)
-        meet([env["partner"]] + [peer for peer, _ in env["axes"]] + env["stack"])
+        dp, partner = env["dp"], env["partner"]
+        meet([(lax.rem(dp + k, 16), me) for k in range(1, 16)] + [partner])
+        cross = push(
+            g_ref.at[:, pl.ds(pl.multiple_of((1 - me) * C, C), C)], arrived_ref,
+            gsend.at[4], grecv.at[4], partner,
+        )
+        cross.start()
         lines = [
             Chunk(env, c, source, target, acc_ref.at[c], landing_ref.at[c], True).steps()
             for c, (source, target) in enumerate(square_blocks(raw, full))
         ]
         for c, line in enumerate(lines):
             for j, step in enumerate(line):
-                at = c + 2 * j
+                at = int((c + 2 * j) * PACE)
                 ticks += [[] for _ in range(at + 1 - len(ticks))]
                 ticks[at].append(step)
 
     def tick(now, candidates):
         for t in candidates:
-            if t < len(ticks):
+            if t < len(ticks) and ticks[t]:
 
                 @pl.when(now == t)
                 def _(t=t):
                     for step in ticks[t]:
                         step()
 
-    def straight(candidates):
-        for t in candidates:
-            if t < len(ticks):
-                for step in ticks[t]:
-                    step()
-
-    straight([0])
+    def straight(t):
+        for step in ticks[t] if t < len(ticks) else []:
+            step()
+
+    straight(0)
     shift, ends = rotation(len_ref, span)
 
     def prepare(i, _):
@@ -332,12 +340,17 @@
         kt_ref[:, rows] = k_ref[rows, :].T
         gk_ref[rows, :] = jnp.zeros((BQ, C), F32)
         gv_ref[rows, :] = jnp.zeros((BQ, C), F32)
-        turned_ref[rows, :] = g_ref[rows, :].astype(F32)
+        if not sums:
+            turned_ref[rows, :] = g_ref[rows, :].astype(F32)
         return 0
 
     lax.fori_loop(0, blocks, prepare, 0)
+    if sums:
+        turned_ref[pl.ds(pl.multiple_of(me * half, half), half), :] = g_ref[:, columns].astype(F32)
+        cross.wait()
+        turned_ref[pl.ds(pl.multiple_of((1 - me) * half, half), half), :] = arrived_ref[...].astype(F32)
     turned_ref[span:, :] = turned_ref[: BQ + 8, :]
-    straight([1])
+    straight(1)
     lane = lax.broadcasted_iota(jnp.int32, (1, C), 1) // HEAD
     masks = [(lane == h).astype(F32).astype(BF16) for h in range(HL)]
 
@@ -401,7 +414,6 @@
     lax.fori_loop(0, near, functools.partial(query_block, False), 0)
     lax.fori_loop(near, blocks, functools.partial(query_block, True), 0)
 
-    columns = pl.ds(pl.multiple_of(me * C, C), C)
     after = 2 + 2 * blocks
     term_ref[...] = jnp.zeros_like(term_ref)
     sums_ref[...] = jnp.zeros_like(sums_ref)
@@ -436,9 +448,12 @@
 
     def own_piece(k, _):
         gx, row = piece_rows(me, k)
-        ga_ref[pl.ds(pl.multiple_of(k * piece, piece), piece), :] = (
-            gx + res_ref[pl.ds(row, piece), :]
-        )
+        here = pl.ds(pl.multiple_of(k * piece, piece), piece)
+        gx = gx + res_ref[pl.ds(row, piece), :]
+        if sums:
+            ga_ref[here, :] = (gx + gbr_ref[here, :].astype(F32)).astype(BF16)
+        else:
+            ga_ref[here, :] = gx
         return 0
 
     def other_piece(k, _):
@@ -446,32 +461,118 @@
         gb_ref[pl.ds(pl.multiple_of(k * piece, piece), piece), :] = gx.astype(BF16)
         return 0
 
-    lax.fori_loop(0, each, own_piece, 0)
-    lax.fori_loop(0, each, other_piece, 0)
-    straight(range(after + blocks, len(ticks)))
-
-
-def attend_backward(lengths, slots, pieces, x, q, k, v, g, out, lse, wq, wk, wv, res, raw, collective_id):
+    if not sums:
+        lax.fori_loop(0, each, own_piece, 0)
+        lax.fori_loop(0, each, other_piece, 0)
+        return
+
+    lines = [
+        Chunk(
+            env, 9 + c, gw_ref.at[c], qkv_full.at[me, c], acc_own.at[c], landing_own.at[c], False
+        ).steps()
+        for c in range(3)
+    ]
+    peers = [partner]
+    for w in (1, 2, 4, 8):
+        bit = (dp // w) % 2
+        peers.append((dp + (1 - 2 * bit) * w, me))
+
+    def vec_copy(s):
+        return push(vec_recv.at[len(peers) + s], vec_recv.at[s], vsend.at[s], vrecv.at[s], peers[s])
+
+    def vec_step(s):
+        if s == 0:
+            vec_full[...] = vec_ref[...]
+            vec_full[0:1, columns] = sums_ref[:, :C]
+            vec_full[1:2, columns] = sums_ref[:, C:]
+        else:
+            vec_copy(s - 1).wait()
+            vec_full[...] += vec_recv[s - 1]
+        if s < len(peers):
+            vec_recv[len(peers) + s] = vec_full[...]
+            vec_copy(s).start()
+
+    lines.append([functools.partial(vec_step, s) for s in range(len(peers) + 1)])
+    left = [ticks[t] for t in range(after + blocks, len(ticks))]
+    queue = [
+        (left[n] if n < len(left) else []) + [line[n] for line in lines if n < len(line)]
+        for n in range(max([len(left)] + [len(line) for line in lines]))
+    ]
+
+    def advance():
+        for step in queue.pop(0) if queue else []:
+            step()
+
+    floor, place = env["z"], lax.rem(dp, 4)
+    order = (2, 1, 3, 0)
+    plane = 4 * piece
+
+    def across(k):
+        here = pl.ds(pl.multiple_of(lax.rem(floor + k, 4) * plane, plane), plane)
+        return push(gb_ref.at[here, :], gbr_ref.at[here, :], gsend.at[k], grecv.at[k], partner)
+
+    advance()
+    for k in order:
+        first = lax.rem(floor + k, 4) * 4
+        lax.fori_loop(first, first + 4, other_piece, 0)
+        across(k).start()
+    advance()
+    mine = pl.ds(pl.multiple_of(dp * piece, piece), piece)
+    returns = []
+    for k in order:
+        first = lax.rem(floor + k, 4) * 4
+        across(k).wait()
+        lax.fori_loop(first, first + 4, own_piece, 0)
+        for i in range(4):
+            if k == 0 and i == 0:
+                back_ref[mine, :] = ga_ref[mine, :]
+                continue
+            p = first + lax.rem(place + i, 4)
+            theirs = pl.ds(pl.multiple_of(p * piece, piece), piece)
+            n = 4 * k + i
+            copy = push(ga_ref.at[theirs, :], back_ref.at[mine, :], asend.at[n], arecv.at[n], (p, me))
+            copy.start()
+            returns.append(copy)
+        advance()
+    while queue:
+        advance()
+    for copy in returns:
+        copy.wait()
+
+
+def attend_backward(lengths, slots, pieces, x, q, k, v, g, out, lse, wq, wk, wv, res, raw, vec, collective_id):
     span = x.shape[0]
+    half = span // 2
     vmem, smem = pl.BlockSpec(memory_space=VMEM), pl.BlockSpec(memory_space=SMEM)
     shape = jax.ShapeDtypeStruct
     sums = len(raw) > 0
-    chunks = sum(a.size for a in raw) // (D * D)
     dma = pltpu.SemaphoreType.DMA
-    comm = [VMEM((chunks, D, D), BF16)] * 2 + [dma((chunks, 12))] * 2 if sums else []
-    params = dict(collective_id=collective_id, has_side_effects=True) if sums else {}
+    results = [
+        ((3, D, C), BF16),
+        ((1, 2 * C), F32),
+        ((half, D), BF16 if sums else F32),
+        ((half, D), BF16),
+    ]
+    outs = [shape(*r) for r in results]
+    operands = (lengths, slots, x, q, k, v, g, out, lse, wq, wk, wv, res)
+    before, comm, params = [], [], {}
+    if sums:
+        chunks = sum(a.size for a in raw) // (D * D)
+        outs = [shape(a.shape, BF16) for a in raw]
+        outs += [shape((half, D), BF16), shape((2, 3, D, C), BF16), shape(vec.shape, F32)]
+        before = [VMEM(*r) for r in results]
+        comm = [VMEM((chunks, D, D), BF16)] * 2 + [VMEM((3, D, C), BF16)] * 2
+        comm += [VMEM((half, D), BF16), VMEM((half, C), BF16), VMEM((10,) + vec.shape, F32)]
+        comm += [dma((chunks + 3, 13))] * 2 + [dma((16,))] * 2 + [dma((5,))] * 4
+        params = dict(collective_id=collective_id, has_side_effects=True)
+        operands += (*raw, vec)
     return pl.pallas_call(
         functools.partial(backward_kernel, pieces, sums),
-        out_shape=[
-            shape((3, D, C), BF16),
-            shape((1, 2 * C), F32),
-            shape((span // 2, D), F32),
-            shape((span // 2, D), BF16),
-        ]
-        + [shape(a.shape, BF16) for a in raw],
-        in_specs=[smem] * 2 + [vmem] * (11 + len(raw)),
-        out_specs=[vmem] * (4 + len(raw)),
-        scratch_shapes=[
+        out_shape=outs,
+        in_specs=[smem] * 2 + [vmem] * (len(operands) - 2),
+        out_specs=[vmem] * len(outs),
+        scratch_shapes=before
+        + [
             VMEM((C, span), BF16),
             VMEM((span, C), BF16),
             VMEM((span, C), F32),
@@ -479,8 +580,8 @@
             VMEM((C, BQ), F32),
             VMEM((HL * BQ, C), BF16),
             VMEM((HL * BQ, C), BF16),
-            VMEM((span // 2, HL * BQ), BF16),
-            VMEM((span // 2, HL * BQ), BF16),
+            VMEM((half, HL * BQ), BF16),
+            VMEM((half, HL * BQ), BF16),
             VMEM((3, D, C), F32),
             VMEM((span + BQ + 8, C), F32),
             VMEM((span + span // (pieces if pieces else 32) + 8, D), F32),
@@ -488,7 +589,7 @@
         + comm,
         compiler_params=pltpu.CompilerParams(vmem_limit_bytes=63 << 20, **params),
         name="attend_backward",
-    )(lengths, slots, x, q, k, v, g, out, lse, wq, wk, wv, res, *raw)
+    )(*operands)
 
 
 def arrange_kernel(groups, route_ref, x_ref, o_ref, slot_ref):
@@ -731,114 +832,6 @@
                     copy.start()
 
         return [functools.partial(step, n) for n in range(len(stages) + 1)]
-
-
-def final_kernel(
-    ga_ref, gb_ref, qkv_ref, vec_ref,
-    back_ref, qkv_full, vec_full,
-    ret_ref, gbr_ref, acc_ref, landing_ref, vec_recv,
-    send, recv, asend, arecv, gsend, grecv, vsend, vrecv,
-):
-    n = 16
-    rows = ga_ref.shape[0]
-    piece = rows // n
-    env = chip_links(send, recv)
-    dp, me, partner = env["dp"], env["me"], env["partner"]
-    meet([((dp + k) % n, me) for k in range(1, n)] + [partner])
-
-    quarter = rows // 4
-    halves = []
-    for j in range(4):
-        part = pl.ds(j * quarter, quarter)
-        copy = push(gb_ref.at[part, :], gbr_ref.at[part, :], gsend.at[j], grecv.at[j], partner)
-        copy.start()
-        halves.append(copy)
-
-    lines = []
-    for c in range(3):
-        lines.append(
-            Chunk(
-                env, c, qkv_ref.at[c], qkv_full.at[me, c], acc_ref.at[c], landing_ref.at[c], False
-            ).steps()
-        )
-    peers = [partner]
-    for w in (1, 2, 4, 8):
-        bit = (dp // w) % 2
-        peers.append((dp + (1 - 2 * bit) * w, me))
-    vec_copies = []
-
-    def vec_step(s):
-        if s == 0:
-            vec_full[...] = vec_ref[...]
-        else:
-            vec_copies[-1].wait()
-            vec_full[...] += vec_recv[s - 1]
-        if s < len(peers):
-            sent = vec_recv.at[len(peers) + s]
-            sent[...] = vec_full[...]
-            copy = push(sent, vec_recv.at[s], vsend.at[s], vrecv.at[s], peers[s])
-            copy.start()
-            vec_copies.append(copy)
-
-    lines.append([functools.partial(vec_step, s) for s in range(len(peers) + 1)])
-
-    returns = []
-
-    def give_back():
-        for j in range(4):
-            halves[j].wait()
-
-            def add(i, _, j=j):
-                here = pl.ds(pl.multiple_of(j * quarter + i * 64, 64), 64)
-                ret_ref[here, :] = (ga_ref[here, :] + gbr_ref[here, :].astype(F32)).astype(BF16)
-                return 0
-
-            lax.fori_loop(0, quarter // 64, add, 0)
-        mine = pl.ds(pl.multiple_of(dp * piece, piece), piece)
-        for k in far_first(n):
-            p = (dp + k) % n
-            theirs = pl.ds(pl.multiple_of(p * piece, piece), piece)
-            copy = push(
-                ret_ref.at[theirs, :], back_ref.at[mine, :], asend.at[k], arecv.at[k], (p, me)
-            )
-            copy.start()
-            returns.append(copy)
-        back_ref[mine, :] = ret_ref[mine, :]
-
-    ticks = max(len(line) for line in lines)
-    for t in range(ticks):
-        for line in lines:
-            if t < len(line):
-                line[t]()
-        if t == 0:
-            give_back()
-    for copy in returns:
-        copy.wait()
-
-
-def give_back_and_sum(ga, gb, qkv, vec, collective_id):
-    vmem = pl.BlockSpec(memory_space=VMEM)
-    shape = jax.ShapeDtypeStruct
-    dma = pltpu.SemaphoreType.DMA
-    return pl.pallas_call(
-        final_kernel,
-        out_shape=[shape(gb.shape, BF16), shape((2,) + qkv.shape, BF16), shape(vec.shape, F32)],
-        in_specs=[vmem] * 4,
-        out_specs=[vmem] * 3,
-        scratch_shapes=[
-            VMEM(gb.shape, BF16),
-            VMEM(gb.shape, BF16),
-            VMEM((3, D, C), BF16),
-            VMEM((3, D, C), BF16),
-            VMEM((10,) + vec.shape, F32),
-            dma((3, 12)), dma((3, 12)),
-            dma((16,)), dma((16,)),
-            dma((4,)), dma((4,)),
-            dma((5,)), dma((5,)),
-        ],
-        compiler_params=pltpu.CompilerParams(collective_id=collective_id, has_side_effects=True),
-        name="give_back_and_sum",
-    )(ga, gb, qkv, vec)
 
 
 def body(
@@ -887,13 +880,12 @@
             lax.all_to_all(slots_out, "dp", split_axis=0, concat_axis=0, tiled=True),
         )
         inputs = jnp.zeros_like(incoming).at[slots].set(incoming).reshape(rows, D)
-        x_all = swap(inputs, 0).reshape(span, D)
+        x_all = swap(inputs, (span, D), 0)
     x_turned, q, k, v, mixed_all, attend_out, lse, inputs = attend_forward(
         x_all, pieces, tables, me, slots,
         query_weight, key_weight, value_weight, query_bias, value_bias,
     )
-    mixed_halves = swap(mixed_all.reshape(2, rows, C), 1)
-    mixed = jnp.concatenate([mixed_halves[0], mixed_halves[1]], axis=1)
+    mixed = swap(mixed_all, (rows, D), 1)
     branch = product(mixed, output_weight) + output_bias
     residual = inputs.astype(F32) + branch
     first, first_back = jax.vjp(
@@ -923,21 +915,9 @@
     grad_output = product_left(mixed, grad_branch)
     grad_output_bias = column_sums(grad_branch)
     grad_mixed = product_right(grad_branch, output_weight).astype(BF16)
-    grad_halves = jnp.stack([grad_mixed[:, :C], grad_mixed[:, C:]])
-    grad_mixed_all = swap(grad_halves, 2).reshape(span, C)
-    raw = [a.astype(BF16) for a in (grad_up, grad_down, grad_output)] if kernels else []
-    grad_columns, column_parts, grad_own, grad_other, *summed = attend_backward(
-        tables, slots, pieces, x_turned, q, k, v, grad_mixed_all, attend_out, lse,
-        query_weight, key_weight, value_weight, grad_residual, raw, 3,
-    )
-
-    def own_columns(part):
-        return lax.dynamic_update_slice(jnp.zeros((1, D), F32), part, (0, seq * C))
-
     vec = jnp.concatenate(
         [
-            own_columns(column_parts[:, :C]),
-            own_columns(column_parts[:, C:]),
+            jnp.zeros((2, D), F32),
             jnp.stack(
                 [
                     grad_output_bias,
@@ -952,13 +932,25 @@
             jnp.zeros((4, D), F32),
         ]
     )
+    shared = (tables, slots, pieces, x_turned, q, k, v)
+    rest = (attend_out, lse, query_weight, key_weight, value_weight, grad_residual)
     if kernels:
-        back, columns, vec = give_back_and_sum(grad_own, grad_other, grad_columns, vec, 4)
+        raw = [a.astype(BF16) for a in (grad_up, grad_down, grad_output)]
+        up_sum, down_sum, out_sum, back, columns, vec = attend_backward(
+            *shared, grad_mixed, *rest, raw, vec, 3
+        )
         token_grad = restore(back.reshape(groups, piece, D), route).reshape(rows, D)
-        up_sum, down_sum, out_sum = (a.astype(F32) for a in summed)
+        up_sum, down_sum, out_sum = (a.astype(F32) for a in (up_sum, down_sum, out_sum))
         columns = jnp.concatenate([columns[0], columns[1]], axis=2).astype(F32)
     else:
-        grad_inputs = grad_own + swap(jnp.stack([grad_other, grad_other]), 5)[1 - seq].astype(F32)
+        grad_mixed_all = swap(grad_mixed, (span, C), 2)
+        grad_columns, parts, grad_own, grad_other = attend_backward(
+            *shared, grad_mixed_all, *rest, [], vec, 3
+        )
+        parts = parts.reshape(2, C)
+        vec = vec + lax.dynamic_update_slice(jnp.zeros_like(vec), parts, (0, seq * C))
+        both = swap(grad_other, (span, D), 5).reshape(2, rows, D)
+        grad_inputs = grad_own + both[1 - seq].astype(F32)
         back_rows = grad_inputs.astype(BF16).reshape(groups, piece, D)[slots]
         returned = lax.all_to_all(back_rows, "dp", split_axis=0, concat_axis=0, tiled=True)
         token_grad = returned[target].reshape(rows, D)

time: 286 us -> 274 us (0.958)
  Pallas kernels: 207 us -> 199 us
  local copies, waits for them, and re-layouts: 13.1 us -> 9.58 us
    pallas_call x1 -> x0, Pallas kernels: 53.6 us -> none  [give_back_and_sum(): pl.pallas_call(final_kernel, out_shape=[shape(gb.shape, BF16), shape((2,)...]
    pallas_call x1, Pallas kernels: 71.9 us -> 121 us  [attend_backward(): pl.pallas_call(functools.partial(backward_kernel, pieces, sums), out_shap...]
    pallas_call x2 -> x1, Pallas kernels: 8.36 us -> 4.24 us  [swap(): pl.pallas_call(swap_kernel, out_shape=jax.ShapeDtypeStruct(shape, x.dtype...]
where the time goes in v4:
time: 274 us
  Pallas kernels  199 us (73%)
  matrix products  49.9 us (18%)
  other arithmetic  14 us (5%)
  local copies, waits for them, and re-layouts  9.58 us (3%)
    pallas_call x1, Pallas kernels, attend_backward(): pl.pallas_call(functools.partial(backward_kernel, pieces, sums), out_shap...  121 us
    pallas_call x1, Pallas kernels, dispatch(): pl.pallas_call(functools.partial(dispatch_kernel, n), out_shape=[jax.Shap...  34.5 us
    pallas_call x1, Pallas kernels, attend_forward(): pl.pallas_call(functools.partial(forward_kernel, pieces), grid_spec=pltpu...  33.1 us
    dot_general x3, matrix products, product(): return jnp.dot(left, right, preferred_element_type=F32)  26.9 us
    dot_general x3, matrix products, product_right(): lax.dot_general(left, right, (((1,), (1,)), ((), ())), preferred_element_...  13.8 us
    dot_general x3, matrix products, product_left(): lax.dot_general(left, right, (((0,), (0,)), ((), ())), preferred_element_...  9.29 us
    convert_element_type x3, other arithmetic, body(): a.astype(F32)  6.25 us

profile of v4, /device:TPU:0, one launch (start us, length us, event | category | flops | bytes accessed | tf_op | source)
XLA Modules:
  0.0 273.7 jit_solution(1279489426704006558)
XLA Ops:
  0.7 0.7 convert_element_type.87
  1.4 0.7 convert_element_type.85
  2.1 0.7 convert_element_type.81
  2.8 3.0 %arrange.1 = (bf16[16,64,512]{2,1,0:T(8,128)(2,1)}, s32[16,8,128]{2,1,0:T(8,128)}) custom-call(s32[16]{0:T(128)} %route_ref.3, bf16[16,64,512]{2,1,0:T(8,128)(2,1)} %bitcast.50), custom_call_target="tpu_custom_call" | custom-call | tf_op jit(solution)/shard_map/arrange/pallas_call | solution.py:605
  5.8 34.5 %dispatch.1 = (bf16[2,16,64,512]{3,2,1,0:T(8,128)(2,1)}, s32[2,16,8,128]{3,2,1,0:T(8,128)}) custom-call(bf16[16,64,512]{2,1,0:T(8,128)(2,1)} %get-tuple-element.35.x_ref, s32[16,8,128]{2,1,0:T(8,128)} %get-tuple-element.36.slot_ref), custom_call_target="tpu_custom_call" | custom-call | tf_op jit(solution)/shard_map/dispatch/pallas_call | solution.py:687
  40.3 1.6 slice_reduce_fusion
  41.9 0.6 reshape_squeeze.3.slot_ref.refs_1_
  42.5 0.6 reshape.139.bq_ref
  43.7 33.1 %attend_forward.1 = (bf16[2048,512]{1,0:T(8,128)(2,1)}, bf16[2048,256]{1,0:T(8,128)(2,1)}, bf16[2048,256]{1,0:T(8,128)(2,1)}, bf16[2048,256]{1,0:T(8,128)(2,1)},...) custom-call(s32[6]{0:T(128)} %bitcast.56, s32[1]{0:T(128)} %bitcast.1.me_ref, ...), custom_call_target="tpu_custom_call" | custom-call | tf_op jit(solution)/shard_map/attend_forward/pallas_call | solution.py:252
  76.8 4.2 %shard_map.314 = bf16[1024,512]{1,0:T(8,128)(2,1)} custom-call(bf16[2048,256]{1,0:T(8,128)(2,1)} %get-tuple-element.40.x_ref), custom_call_target="tpu_custom_call" | custom-call | tf_op jit(solution)/shard_map/pallas_call | solution.py:79
  81.1 2.0 fusion.22
  83.6 1.1 copy-done.16
  84.7 22.2 %multiply_convert_fusion = (bf16[1024,2048]{1,0:T(8,128)(2,1)S(1)}, f32[1024,2048]{1,0:T(8,128)}, f32[1024,2048]{1,0:T(8,128)}) fusion(f32[2048]{0:T(1024)S(1)} %convert_element_type.85, bf16[512,2048]{1,0:T(8,128)(2,1)S(1)} %copy-done.16, f32[1024,512]{1,0:T(8,128)S(1)} %get-tuple-element.84, f32[512]{0:T(512)S(1)} %convert_element_type.83, ...), kind=kOutput, calls=%fused_computation.4 | convolution fusion | flops 2288517120 | bytes 25186304 | tf_op jit(solution)/shard_map/dot_general | solution.py:39
  106.8 2.7 fusion.23
  110.8 1.0 fusion.9
  111.8 2.0 fusion.19
  114.0 8.9 %convert_reduce_fusion = (f32[2048]{0:T(1024)S(1)}, bf16[1024,2048]{1,0:T(8,128)(2,1)S(1)}) fusion(f32[1024,2048]{1,0:T(8,128)} %get-tuple-element.68, bf16[1024,512]{1,0:T(8,128)(2,1)S(1)} %get-tuple-element.60, bf16[2048,512]{1,0:T(8,128)(2,1)S(1)} %copy-done.15, f32[1024,2048]{1,0:T(8,128)} %get-tuple-element.85, f32[2048]{0:T(1024)S(1)} %convert_element_type.85), kind=kOutput, calls=%fused_computation.2 | convolution fusion | flops 2183133184 | bytes 24133632 | tf_op jit(solution)/shard_map/dot_general | solution.py:47
  123.0 3.1 %multiply_reduce_fusion = (f32[512]{0:T(512)S(1)}, f32[1024]{0:T(1024)S(1)}, f32[512]{0:T(512)S(1)}, f32[1024,512]{1,0:T(8,128)S(1)}) fusion(f32[1024,512]{1,0:T(8,128)S(1)} %get-tuple-element.84, f32[1024]{0:T(1024)S(1)} %fusion.11, f32[1024]{0:T(1024)S(1)} %broadcast_multiply_fusion.1, f32[512]{0:T(512)S(1)} %convert_element_type.82, ...), kind=kOutput, calls=%fused_computation.30 | convolution fusion | flops 2152724480 | bytes 12605440 | tf_op jit(solution)/shard_map/dot_general | solution.py:47
  126.1 0.9 fusion.18
  127.2 1.7 convolution_convert_fusion.2.refs_6_
  129.0 4.0 %convolution_convert_fusion.1.refs_13_ = bf16[512,2048]{1,0:T(8,128)(2,1)} fusion(bf16[1024,2048]{1,0:T(8,128)(2,1)S(1)} %get-tuple-element.90, f32[1024,512]{1,0:T(8,128)S(1)} %get-tuple-element.84, f32[512]{0:T(512)S(1)} %convert_element_type.83, f32[512]{0:T(512)S(1)} %convert_element_type.82, f32[1024]{0:T(1024)S(1)} %fusion.11, ...), kind=kOutput, calls=%fused_computation.24 | convolution fusion | flops 2151153664 | bytes 8400896 | tf_op jit(solution)/shard_map/dot_general | solution.py:43
  132.9 3.8 %convolution_convert_fusion.refs_14_ = bf16[2048,512]{1,0:T(8,128)(2,1)} fusion(bf16[1024,2048]{1,0:T(8,128)(2,1)S(1)} %get-tuple-element.67, bf16[1024,512]{1,0:T(8,128)(2,1)S(1)} %get-tuple-element.60), kind=kOutput, calls=%fused_computation.23 | convolution fusion | flops 2148532224 | bytes 7340032 | tf_op jit(solution)/shard_map/dot_general | solution.py:43
  136.7 1.5 convolution_convert_fusion.3.refs_15_
  138.3 1.2 concatenate.6.refs_16_
  139.5 121.3 %attend_backward.1 = (bf16[512,2048]{1,0:T(8,128)(2,1)}, bf16[2048,512]{1,0:T(8,128)(2,1)}, bf16[512,512]{1,0:T(8,128)(2,1)}, bf16[1024,512]{1,0:T(8,128)(2,1)},...) custom-call(s32[6]{0:T(128)} %bitcast.57, s32[32]{0:T(128)} %reshape_squeeze.3.slot_ref.refs_1_, ...), custom_call_target="tpu_custom_call" | custom-call | tf_op jit(solution)/shard_map/attend_backward/pallas_call | solution.py:569
  260.8 3.1 %restore.1 = bf16[16,64,512]{2,1,0:T(8,128)(2,1)} custom-call(s32[16]{0:T(128)} %route_ref.3, bf16[16,64,512]{2,1,0:T(8,128)(2,1)} %bitcast.49), custom_call_target="tpu_custom_call" | custom-call | tf_op jit(solution)/shard_map/restore/pallas_call | solution.py:631
  264.5 1.7 slice_bitcast_fusion
  266.2 0.6 fusion.21
  266.8 1.1 convert_element_type.103
  267.9 2.5 convert_element_type.104
  270.5 0.6 copy.42
  271.1 2.6 convert_element_type.105
  (58 shorter events, 3.4 us)
Async XLA Ops:
  0.7 80.4 %copy-start = (bf16[512,512]{1,0:T(8,128)(2,1)S(1)}, bf16[512,512]{1,0:T(8,128)(2,1)}, u32[]{:S(2)}) copy-start(bf16[512,512]{1,0:T(8,128)(2,1)} %param.27) | copy-start | bytes 1572868
  0.7 41.8 %copy-start.9 = (bf16[512]{0:T(512)(128)(2,1)S(1)}, bf16[512]{0:T(512)(128)(2,1)}, u32[]{:S(2)}) copy-start(bf16[512]{0:T(512)(128)(2,1)} %param.23) | copy-start | bytes 3076
  0.7 42.4 %copy-start.10 = (bf16[512]{0:T(512)(128)(2,1)S(1)}, bf16[512]{0:T(512)(128)(2,1)}, u32[]{:S(2)}) copy-start(bf16[512]{0:T(512)(128)(2,1)} %param.26) | copy-start | bytes 3076
  76.8 4.3 %copy-start.17 = (bf16[1024,512]{1,0:T(8,128)(2,1)S(1)}, bf16[1024,512]{1,0:T(8,128)(2,1)}, u32[]{:S(2)}) copy-start(bf16[1024,512]{1,0:T(8,128)(2,1)} %get-tuple-element.39) | copy-start | bytes 3145732
  81.0 2.1 copy-start.11
  81.0 2.1 copy-start.12
  83.1 1.6 copy-start.16
  84.7 22.2 %copy-start.15 = (bf16[2048,512]{1,0:T(8,128)(2,1)S(1)}, bf16[2048,512]{1,0:T(8,128)(2,1)}, u32[]{:S(2)}) copy-start(bf16[2048,512]{1,0:T(8,128)(2,1)} %param.33) | copy-start | bytes 6291460
  109.5 0.7 copy-start.13
  109.6 1.2 copy-start.3
  110.0 1.8 copy-start.14
  127.2 9.5 %copy-start.1 = (f32[1024,512]{1,0:T(8,128)}, f32[1024,512]{1,0:T(8,128)S(1)}, u32[]{:S(2)}) copy-start(f32[1024,512]{1,0:T(8,128)S(1)} %get-tuple-element.62.refs_12_) | copy-start | bytes 6291460
  132.9 3.8 %copy-start.2 = (bf16[1024,512]{1,0:T(8,128)(2,1)S(1)}, bf16[1024,512]{1,0:T(8,128)(2,1)}, u32[]{:S(2)}) copy-start(bf16[1024,512]{1,0:T(8,128)(2,1)} %shard_map.314) | copy-start | bytes 3145732
  260.8 3.1 %copy-start.6 = (bf16[2,3,512,256]{3,2,1,0:T(8,128)(2,1)S(1)}, bf16[2,3,512,256]{3,2,1,0:T(8,128)(2,1)}, u32[]{:S(2)}) copy-start(bf16[2,3,512,256]{3,2,1,0:T(8,128)(2,1)} %get-tuple-element.48) | copy-start | bytes 4718596
  264.4 1.8 copy-start.8
  264.5 2.4 copy-start.7
  264.5 3.5 %copy-start.5 = (bf16[512,2048]{1,0:T(8,128)(2,1)S(1)}, bf16[512,2048]{1,0:T(8,128)(2,1)}, u32[]{:S(2)}) copy-start(bf16[512,2048]{1,0:T(8,128)(2,1)} %get-tuple-element.51) | copy-start | bytes 6291460
  267.9 3.2 %copy-start.4 = (bf16[2048,512]{1,0:T(8,128)(2,1)S(1)}, bf16[2048,512]{1,0:T(8,128)(2,1)}, u32[]{:S(2)}) copy-start(bf16[2048,512]{1,0:T(8,128)(2,1)} %get-tuple-element.52) | copy-start | bytes 6291460

commit v5 on v4

--- a/solution.py
+++ b/solution.py
@@ -17,6 +17,7 @@
 LOG2E = 1.4426950408889634
 BQ = 256
 BK = 256
+BR = 128
 PACE = 1.2
 F32 = jnp.float32
 BF16 = jnp.bfloat16
@@ -25,14 +26,29 @@
 SMEM = pltpu.SMEM
 
 
-def norm_rows(value, gain, shift):
-    center = value - jnp.mean(value, axis=-1, keepdims=True)
-    spread = jnp.mean(center * center, axis=-1, keepdims=True)
-    return center * lax.rsqrt(spread + 1e-05) * gain + shift
-
-
-def gelu_exact(value):
-    return jax.nn.gelu(value, approximate=False)
+ERFC_RATE = 0.38
+ERFC = (
+    0.214409851453,
+    0.213944088337,
+    0.203688192149,
+    0.139667636356,
+    0.227252140359,
+    -0.1568920127,
+    0.359389202242,
+    -0.259886715084,
+    0.0584276049124,
+)
+
+
+def gelu_and_slope(value):
+    bell = jnp.exp(-0.5 * value * value)
+    t = 1.0 / (1.0 + (ERFC_RATE * 0.5**0.5) * jnp.abs(value))
+    tail = ERFC[-1]
+    for c in ERFC[-2::-1]:
+        tail = tail * t + c
+    tail = (0.5 * bell) * (tail * t)
+    share = jnp.where(value < 0, tail, 1.0 - tail)
+    return value * share, share + value * bell * 0.3989422804014327
 
 
 def product(left, right):
@@ -45,10 +61,6 @@
 
 def product_right(left, right):
     return lax.dot_general(left, right, (((1,), (1,)), ((), ())), preferred_element_type=F32)
-
-
-def column_sums(value):
-    return jnp.sum(value.astype(F32), axis=0)
 
 
 def swap_kernel(x_ref, o_ref, send, recv, local):
@@ -592,6 +604,171 @@
     )(*operands)
 
 
+def norm_forward(value):
+    center = value - jnp.mean(value, axis=-1, keepdims=True)
+    spread = jnp.mean(center * center, axis=-1, keepdims=True)
+    rate = lax.rsqrt(spread + 1e-05)
+    return center * rate, rate
+
+
+def norm_backward(grad, unit, rate, gain):
+    grad = grad * gain
+    mean = jnp.mean(grad, axis=-1, keepdims=True)
+    along = jnp.mean(grad * unit, axis=-1, keepdims=True)
+    return rate * (grad - mean - unit * along)
+
+
+def feed_kernel(
+    mixed_ref, own_ref, cotangent_ref, wo_ref, wu_ref, wd_ref, bu_ref, bo_ref, g1_ref, s1_ref, bd_ref, g2_ref, s2_ref,
+    out_ref, res_ref, gm_ref, up_ref, down_ref, outw_ref, vec_ref,
+    first_ref, unit1_ref, rate1_ref, low_ref, act_ref, slope_ref, gu_ref, gs_ref, gh_ref, gb_ref,
+    up_acc, down_acc, outw_acc,
+):
+    step, last = pl.program_id(0), pl.num_programs(0) - 1
+    rows = mixed_ref.shape[0]
+    wide = bu_ref.shape[1] // D
+    bo, g1, s1, bd, g2, s2 = (
+        r[...].astype(F32) for r in (bo_ref, g1_ref, s1_ref, bd_ref, g2_ref, s2_ref)
+    )
+
+    @pl.when(step == 0)
+    def _():
+        up_acc[...] = jnp.zeros_like(up_acc)
+        down_acc[...] = jnp.zeros_like(down_acc)
+        outw_acc[...] = jnp.zeros_like(outw_acc)
+        vec_ref[...] = jnp.zeros_like(vec_ref)
+
+    def total(value):
+        return jnp.sum(value, axis=0, keepdims=True)
+
+    def part(r):
+        return pl.ds(pl.multiple_of(r * BR, BR), BR)
+
+    def block(c):
+        return pl.ds(pl.multiple_of(c * D, D), D)
+
+    def project(r, _):
+        here = part(r)
+        branch = product(mixed_ref[here, :], wo_ref[...]) + bo
+        unit, rate = norm_forward(own_ref[here, :].astype(F32) + branch)
+        unit1_ref[here, :] = unit
+        rate1_ref[here, :] = rate
+        first = unit * g1 + s1
+        first_ref[here, :] = first
+        low_ref[here, :] = first.astype(BF16)
+        return 0
+
+    lax.fori_loop(0, rows // BR, project, 0)
+
+    def widen(n, _):
+        here, c = part(n // wide), block(n % wide)
+        hidden = product(low_ref[here, :], wu_ref[:, c]) + bu_ref[:, c].astype(F32)
+        active, slope = gelu_and_slope(hidden)
+        act_ref[here, c] = active.astype(BF16)
+        slope_ref[here, c] = slope
+        return 0
+
+    lax.fori_loop(0, rows // BR * wide, widen, 0)
+
+    def narrow(r, sums):
+        here = part(r)
+        update = product(act_ref[here, :], wd_ref[...]) + bd
+        unit, rate = norm_forward(first_ref[here, :] + update)
+        out_ref[here, :] = (unit * g2 + s2).astype(BF16)
+        cotangent = cotangent_ref[here, :].astype(F32)
+        grad = norm_backward(cotangent, unit, rate, g2)
+        gs_ref[here, :] = grad
+        low = grad.astype(BF16)
+        gu_ref[here, :] = low
+        new = (total(low.astype(F32)), total(cotangent * unit), total(cotangent))
+        return tuple(a + b for a, b in zip(sums, new))
+
+    zero = jnp.zeros((1, D), F32)
+    sums = lax.fori_loop(0, rows // BR, narrow, (zero,) * 3)
+    for n, value in enumerate(sums):
+        vec_ref[5 + n : 6 + n, :] += value
+
+    def widen_back(n, _):
+        here, c = part(n // wide), block(n % wide)
+        grad = product_right(gu_ref[here, :], wd_ref[c, :]) * slope_ref[here, c]
+        gh_ref[here, c] = grad.astype(BF16)
+        return 0
+
+    lax.fori_loop(0, rows // BR * wide, widen_back, 0)
+
+    for c in range(wide):
+        lanes = slice(c * D, (c + 1) * D)
+        vec_ref[8 + c : 9 + c, :] += total(gh_ref[:, lanes].astype(F32))
+
+    def weights(c, _):
+        lanes = block(c)
+        up_acc[:, lanes] += product_left(low_ref[...], gh_ref[:, lanes])
+        down_acc[lanes, :] += product_left(act_ref[:, lanes], gu_ref[...])
+        return 0
+
+    lax.fori_loop(0, wide, weights, 0)
+
+    def narrow_back(r, sums):
+        here = part(r)
+        grad = gs_ref[here, :] + product_right(gh_ref[here, :], wu_ref[...])
+        unit = unit1_ref[here, :]
+        residual = norm_backward(grad, unit, rate1_ref[here, :], g1)
+        res_ref[here, :] = residual
+        low = residual.astype(BF16)
+        gb_ref[here, :] = low
+        gm_ref[here, :] = product_right(low, wo_ref[...]).astype(BF16)
+        new = (total(low.astype(F32)), total(grad * unit), total(grad))
+        return tuple(a + b for a, b in zip(sums, new))
+
+    sums = lax.fori_loop(0, rows // BR, narrow_back, (zero,) * 3)
+    for n, value in enumerate(sums):
+        vec_ref[2 + n : 3 + n, :] += value
+    outw_acc[...] += product_left(mixed_ref[...], gb_ref[...])
+
+    @pl.when(step == last)
+    def _():
+        up_ref[...] = up_acc[...].astype(BF16)
+        down_ref[...] = down_acc[...].astype(BF16)
+        outw_ref[...] = outw_acc[...].astype(BF16)
+
+
+def feed(mixed, own, cotangent, wo, wu, wd, bu, *vectors):
+    count = 2
+    rows = mixed.shape[0] // count
+    ff = wu.shape[1]
+    shape = jax.ShapeDtypeStruct
+    block = pl.BlockSpec((rows, D), lambda i: (i, 0))
+
+    def whole(a):
+        return pl.BlockSpec(a, lambda i: (0, 0))
+
+    return pl.pallas_call(
+        feed_kernel,
+        grid=(count,),
+        in_specs=[block] * 3 + [whole(a.shape) for a in (wo, wu, wd)] + [whole((1, ff))] + [whole((1, D))] * 6,
+        out_specs=[block] * 3 + [whole(wu.shape), whole(wd.shape), whole(wo.shape), whole((16, D))],
+        out_shape=[shape(mixed.shape, BF16), shape(mixed.shape, F32), shape(mixed.shape, BF16)]
+        + [shape(a.shape, BF16) for a in (wu, wd, wo)]
+        + [shape((16, D), F32)],
+        scratch_shapes=[
+            VMEM((rows, D), F32),
+            VMEM((rows, D), F32),
+            VMEM((rows, 1), F32),
+            VMEM((rows, D), BF16),
+            VMEM((rows, ff), BF16),
+            VMEM((rows, ff), F32),
+            VMEM((rows, D), BF16),
+            VMEM((rows, D), F32),
+            VMEM((rows, ff), BF16),
+            VMEM((rows, D), BF16),
+            VMEM(wu.shape, F32),
+            VMEM(wd.shape, F32),
+            VMEM(wo.shape, F32),
+        ],
+        name="feed",
+    )(mixed, own, cotangent, wo, wu, wd, bu.reshape(1, ff), *(v.reshape(1, D) for v in vectors))
+
+
 def arrange_kernel(groups, route_ref, x_ref, o_ref, slot_ref):
     for k in range(groups):
         packed = route_ref[k]
@@ -621,21 +798,44 @@
     )(route, pieces)
 
 
-def restore_kernel(groups, route_ref, x_ref, o_ref):
-    for k in range(groups):
-        o_ref[k] = x_ref[route_ref[k] // (2 * groups)]
-
-
-def restore(pieces, route):
-    spec = pl.BlockSpec(pieces.shape, lambda i, r: (0, 0, 0))
+def finish_kernel(route_ref, up, down, out, columns, back, up_o, down_o, out_o, q_o, k_o, v_o, back_o):
+    up_o[...] = up[...].astype(F32)
+    down_o[...] = down[...].astype(F32)
+    out_o[...] = out[...].astype(F32)
+    for n, ref in enumerate((q_o, k_o, v_o)):
+        ref[:, :C] = columns[0, n].astype(F32)
+        ref[:, C:] = columns[1, n].astype(F32)
+    back_o[...] = back[...]
+
+
+def finish(up, down, out, columns, back, route):
+    groups, piece, _ = back.shape
+
+    def rows(shape):
+        return pl.BlockSpec((shape[0] // groups, shape[1]), lambda i, r: (i, 0))
+
+    square = jax.ShapeDtypeStruct((D, D), F32)
     return pl.pallas_call(
-        functools.partial(restore_kernel, pieces.shape[0]),
+        finish_kernel,
         grid_spec=pltpu.PrefetchScalarGridSpec(
-            num_scalar_prefetch=1, grid=(1,), in_specs=[spec], out_specs=spec
+            num_scalar_prefetch=1,
+            grid=(groups,),
+            in_specs=[
+                rows(up.shape),
+                rows(down.shape),
+                rows(out.shape),
+                pl.BlockSpec((2, 3, D // groups, C), lambda i, r: (0, 0, i, 0)),
+                pl.BlockSpec((1, piece, D), lambda i, r: (r[i] // (2 * groups), 0, 0)),
+            ],
+            out_specs=[rows(up.shape), rows(down.shape)]
+            + [rows(square.shape)] * 4
+            + [pl.BlockSpec((1, piece, D), lambda i, r: (i, 0, 0))],
         ),
-        out_shape=jax.ShapeDtypeStruct(pieces.shape, BF16),
-        name="restore",
-    )(route, pieces)
+        out_shape=[jax.ShapeDtypeStruct(up.shape, F32), jax.ShapeDtypeStruct(down.shape, F32)]
+        + [square] * 4
+        + [jax.ShapeDtypeStruct(back.shape, BF16)],
+        name="finish",
+    )(route, up, down, out, columns, back)
 
 
 def far_first(n):
@@ -886,62 +1086,21 @@
         query_weight, key_weight, value_weight, query_bias, value_bias,
     )
     mixed = swap(mixed_all, (rows, D), 1)
-    branch = product(mixed, output_weight) + output_bias
-    residual = inputs.astype(F32) + branch
-    first, first_back = jax.vjp(
-        norm_rows, residual, first_gain.astype(F32), first_shift.astype(F32)
-    )
-    first_low = first.astype(BF16)
-    hidden = product(first_low, up_weight) + up_bias
-    active = gelu_exact(hidden).astype(BF16)
-    update = product(active, down_weight) + down_bias
-    layer_out, second_back = jax.vjp(
-        norm_rows, first + update, second_gain.astype(F32), second_shift.astype(F32)
-    )
-    grad_second, grad_second_gain, grad_second_shift = second_back(cotangent.astype(F32))
-    grad_update = grad_second.astype(BF16)
-    again = product(first_low, up_weight) + up_bias
-    active_again, gelu_back = jax.vjp(gelu_exact, again)
-    active_low = active_again.astype(BF16)
-    grad_down = product_left(active_low, grad_update)
-    grad_down_bias = column_sums(grad_update)
-    (grad_active,) = gelu_back(product_right(grad_update, down_weight))
-    grad_hidden = grad_active.astype(BF16)
-    grad_up = product_left(first_low, grad_hidden)
-    grad_up_bias = column_sums(grad_hidden)
-    grad_first = grad_second + product_right(grad_hidden, up_weight)
-    grad_residual, grad_first_gain, grad_first_shift = first_back(grad_first)
-    grad_branch = grad_residual.astype(BF16)
-    grad_output = product_left(mixed, grad_branch)
-    grad_output_bias = column_sums(grad_branch)
-    grad_mixed = product_right(grad_branch, output_weight).astype(BF16)
-    vec = jnp.concatenate(
-        [
-            jnp.zeros((2, D), F32),
-            jnp.stack(
-                [
-                    grad_output_bias,
-                    grad_first_gain,
-                    grad_first_shift,
-                    grad_down_bias,
-                    grad_second_gain,
-                    grad_second_shift,
-                ]
-            ),
-            grad_up_bias.reshape(-1, D),
-            jnp.zeros((4, D), F32),
-        ]
+    layer_out, grad_residual, grad_mixed, grad_up, grad_down, grad_output, vec = feed(
+        mixed, inputs, cotangent, output_weight, up_weight, down_weight, up_bias,
+        output_bias, first_gain, first_shift, down_bias, second_gain, second_shift,
     )
     shared = (tables, slots, pieces, x_turned, q, k, v)
     rest = (attend_out, lse, query_weight, key_weight, value_weight, grad_residual)
     if kernels:
-        raw = [a.astype(BF16) for a in (grad_up, grad_down, grad_output)]
+        raw = [grad_up, grad_down, grad_output]
         up_sum, down_sum, out_sum, back, columns, vec = attend_backward(
             *shared, grad_mixed, *rest, raw, vec, 3
         )
-        token_grad = restore(back.reshape(groups, piece, D), route).reshape(rows, D)
-        up_sum, down_sum, out_sum = (a.astype(F32) for a in (up_sum, down_sum, out_sum))
-        columns = jnp.concatenate([columns[0], columns[1]], axis=2).astype(F32)
+        up_sum, down_sum, out_sum, query_sum, key_sum, value_sum, token_grad = finish(
+            up_sum, down_sum, out_sum, columns, back.reshape(groups, piece, D), route
+        )
+        token_grad = token_grad.reshape(rows, D)
     else:
         grad_mixed_all = swap(grad_mixed, (span, C), 2)
         grad_columns, parts, grad_own, grad_other = attend_backward(
@@ -954,12 +1113,14 @@
         back_rows = grad_inputs.astype(BF16).reshape(groups, piece, D)[slots]
         returned = lax.all_to_all(back_rows, "dp", split_axis=0, concat_axis=0, tiled=True)
         token_grad = returned[target].reshape(rows, D)
-        up_sum, down_sum, out_sum, vec = lax.psum((grad_up, grad_down, grad_output, vec), ("dp", "seq"))
+        up_sum, down_sum, out_sum, vec = lax.psum(
+            tuple(a.astype(F32) for a in (grad_up, grad_down, grad_output, vec)), ("dp", "seq")
+        )
         columns = lax.psum(grad_columns.astype(F32), "dp")
         columns = lax.all_gather(columns, "seq", axis=2, tiled=True)
-    query_sum, key_sum, value_sum = columns[0], columns[1], columns[2]
+        query_sum, key_sum, value_sum = columns[0], columns[1], columns[2]
     return (
-        layer_out.astype(BF16),
+        layer_out,
         token_grad,
         query_sum,
         vec[0],

time: 274 us -> 279 us (1.018)
  Pallas kernels: 199 us -> 269 us
  matrix products: 49.9 us -> 0 us
  other arithmetic: 14 us -> 0 us
    pallas_call x1 -> x2, Pallas kernels: 3.06 us -> 72.8 us  [the longest x1 59.6 us: feed(): pl.pallas_call(feed_kernel, grid=(count,), in_specs=[block] * 3 + [whole(...]
    dot_general x9 -> x0, matrix products: 49.9 us -> none  [the longest x3 26.9 us: product(): return jnp.dot(left, right, preferred_element_type=F32)]
    convert_element_type x11 -> x0, other arithmetic: 8.8 us -> none  [the longest x3 6.25 us: body(): a.astype(F32)]
    reduce_sum x7 -> x0, other arithmetic: 5.12 us -> none  [the longest x2 2.82 us: norm_rows(): center = value - jnp.mean(value, axis=-1, keepdims=True)]
    reshape x1 -> x7, local copies, waits for them, and re-layouts: 0.01 us -> 4.09 us  [the longest x6 3.49 us: feed(): v.reshape(1, D)]
where the time goes in v5:
time: 279 us; the launch traced here: 278 us
  Pallas kernels  269 us (96%)
  local copies, waits for them, and re-layouts  8.69 us (3%)
    pallas_call x1, Pallas kernels, attend_backward(): pl.pallas_call(functools.partial(backward_kernel, pieces, sums), out_shap...  121 us
    pallas_call x1, Pallas kernels, feed(): pl.pallas_call(feed_kernel, grid=(count,), in_specs=[block] * 3 + [whole(...  59.6 us
    pallas_call x1, Pallas kernels, dispatch(): pl.pallas_call(functools.partial(dispatch_kernel, n), out_shape=[jax.Shap...  34.5 us
    pallas_call x1, Pallas kernels, attend_forward(): pl.pallas_call(functools.partial(forward_kernel, pieces), grid_spec=pltpu...  33.2 us
    pallas_call x1, Pallas kernels, finish(): pl.pallas_call(finish_kernel, grid_spec=pltpu.PrefetchScalarGridSpec(num_...  13.2 us

profile of v5, /device:TPU:0, one launch (start us, length us, event | category | flops | bytes accessed | tf_op | source)
XLA Modules:
  0.0 278.4 jit_solution(11351762353544940728)
XLA Ops:
  0.7 0.0 copy-start.2
  0.7 0.0 copy-start.3
  0.7 3.1 %arrange.1 = (bf16[16,64,512]{2,1,0:T(8,128)(2,1)}, s32[16,8,128]{2,1,0:T(8,128)}) custom-call(s32[16]{0:T(128)} %route_ref.3, bf16[16,64,512]{2,1,0:T(8,128)(2,1)} %bitcast.18), custom_call_target="tpu_custom_call" | custom-call | tf_op jit(solution)/shard_map/arrange/pallas_call | solution.py:782
  3.8 34.5 %dispatch.1 = (bf16[2,16,64,512]{3,2,1,0:T(8,128)(2,1)}, s32[2,16,8,128]{3,2,1,0:T(8,128)}) custom-call(bf16[16,64,512]{2,1,0:T(8,128)(2,1)} %get-tuple-element.49.x_ref, s32[16,8,128]{2,1,0:T(8,128)} %get-tuple-element.50.slot_ref), custom_call_target="tpu_custom_call" | custom-call | tf_op jit(solution)/shard_map/dispatch/pallas_call | solution.py:887
  38.3 1.6 slice_reduce_fusion
  39.9 0.6 reshape_squeeze.3.slot_ref.refs_1_
  40.5 0.0 copy-done.2
  40.5 0.6 reshape.82.bq_ref
  41.1 0.0 copy-done.3
  41.1 0.6 reshape.83.bv_ref
  41.7 0.0 copy-start.7
  41.7 0.0 copy-start.8
  41.7 0.0 copy-start.9
  41.7 33.2 %attend_forward.1 = (bf16[2048,512]{1,0:T(8,128)(2,1)}, bf16[2048,256]{1,0:T(8,128)(2,1)}, bf16[2048,256]{1,0:T(8,128)(2,1)}, bf16[2048,256]{1,0:T(8,128)(2,1)},...) custom-call(s32[6]{0:T(128)} %bitcast.21, s32[1]{0:T(128)} %bitcast.1.me_ref, ...), custom_call_target="tpu_custom_call" | custom-call | tf_op jit(solution)/shard_map/attend_forward/pallas_call | solution.py:264
  74.9 4.2 %shard_map.314.mixed_ref = bf16[1024,512]{1,0:T(8,128)(2,1)} custom-call(bf16[2048,256]{1,0:T(8,128)(2,1)} %get-tuple-element.53.x_ref), custom_call_target="tpu_custom_call" | custom-call | tf_op jit(solution)/shard_map/pallas_call | solution.py:91
  79.1 0.0 copy-done.1
  79.1 0.6 reshape.84.bu_ref
  79.7 0.0 copy-done.4
  79.7 0.6 reshape.85.bo_ref
  80.3 0.0 copy-done.5
  80.3 0.6 reshape.86.g1_ref
  80.9 0.0 copy-done.6
  80.9 0.6 reshape.87.s1_ref
  81.5 0.0 copy-done.7
  81.5 0.6 reshape.88.bd_ref
  82.1 0.6 reshape.89.g2_ref
  82.7 0.6 reshape.90.s2_ref
  83.2 59.6 %feed.1 = (bf16[1024,512]{1,0:T(8,128)(2,1)}, f32[1024,512]{1,0:T(8,128)}, bf16[1024,512]{1,0:T(8,128)(2,1)}, bf16[512,2048]{1,0:T(8,128)(2,1)}, bf16[2048,512]{...) custom-call(bf16[1024,512]{1,0:T(8,128)(2,1)} %shard_map.314.mixed_ref, ...), custom_call_target="tpu_custom_call" | custom-call | tf_op jit(solution)/shard_map/feed/pallas_call | solution.py:745
  142.8 121.1 %attend_backward.1 = (bf16[512,2048]{1,0:T(8,128)(2,1)}, bf16[2048,512]{1,0:T(8,128)(2,1)}, bf16[512,512]{1,0:T(8,128)(2,1)}, bf16[1024,512]{1,0:T(8,128)(2,1)},...) custom-call(s32[6]{0:T(128)} %bitcast.22, s32[32]{0:T(128)} %reshape_squeeze.3.slot_ref.refs_1_, ...), custom_call_target="tpu_custom_call" | custom-call | tf_op jit(solution)/shard_map/attend_backward/pallas_call | solution.py:581
  264.0 13.2 %finish.1 = (f32[512,2048]{1,0:T(8,128)}, f32[2048,512]{1,0:T(8,128)}, f32[512,512]{1,0:T(8,128)}, f32[512,512]{1,0:T(8,128)}, f32[512,512]{1,0:T(8,128)}, /*ind...) custom-call(s32[16]{0:T(128)} %route_ref.3, bf16[512,2048]{1,0:T(8,128)(2,1)} %get-tuple-element.68.up, ...), custom_call_target="tpu_custom_call" | custom-call | tf_op jit(solution)/shard_map/finish/pallas_call | solution.py:818
  277.2 0.6 fusion
  277.8 0.6 copy.36
  (9 shorter events, 0.0 us)
Async XLA Ops:
  0.7 39.8 %copy-start.2 = (bf16[512]{0:T(512)(128)(2,1)S(1)}, bf16[512]{0:T(512)(128)(2,1)}, u32[]{:S(2)}) copy-start(bf16[512]{0:T(512)(128)(2,1)} %param.23) | copy-start | bytes 3076
  0.7 40.4 %copy-start.3 = (bf16[512]{0:T(512)(128)(2,1)S(1)}, bf16[512]{0:T(512)(128)(2,1)}, u32[]{:S(2)}) copy-start(bf16[512]{0:T(512)(128)(2,1)} %param.26) | copy-start | bytes 3076
  41.7 37.5 %copy-start.1 = (bf16[2048]{0:T(1024)(128)(2,1)S(1)}, bf16[2048]{0:T(1024)(128)(2,1)}, u32[]{:S(2)}) copy-start(bf16[2048]{0:T(1024)(128)(2,1)} %param.32) | copy-start | bytes 12292
  41.7 38.1 %copy-start.4 = (bf16[512]{0:T(512)(128)(2,1)S(1)}, bf16[512]{0:T(512)(128)(2,1)}, u32[]{:S(2)}) copy-start(bf16[512]{0:T(512)(128)(2,1)} %param.28) | copy-start | bytes 3076
  41.7 38.7 %copy-start.5 = (bf16[512]{0:T(512)(128)(2,1)S(1)}, bf16[512]{0:T(512)(128)(2,1)}, u32[]{:S(2)}) copy-start(bf16[512]{0:T(512)(128)(2,1)} %param.29) | copy-start | bytes 3076
  41.7 39.2 %copy-start.6 = (bf16[512]{0:T(512)(128)(2,1)S(1)}, bf16[512]{0:T(512)(128)(2,1)}, u32[]{:S(2)}) copy-start(bf16[512]{0:T(512)(128)(2,1)} %param.30) | copy-start | bytes 3076
  41.7 39.8 %copy-start.7 = (bf16[512]{0:T(512)(128)(2,1)S(1)}, bf16[512]{0:T(512)(128)(2,1)}, u32[]{:S(2)}) copy-start(bf16[512]{0:T(512)(128)(2,1)} %param.34) | copy-start | bytes 3076
  41.7 40.4 %copy-start.8 = (bf16[512]{0:T(512)(128)(2,1)S(1)}, bf16[512]{0:T(512)(128)(2,1)}, u32[]{:S(2)}) copy-start(bf16[512]{0:T(512)(128)(2,1)} %param.35) | copy-start | bytes 3076
  41.7 41.0 %copy-start.9 = (bf16[512]{0:T(512)(128)(2,1)S(1)}, bf16[512]{0:T(512)(128)(2,1)}, u32[]{:S(2)}) copy-start(bf16[512]{0:T(512)(128)(2,1)} %param.36) | copy-start | bytes 3076
  263.9 13.2 %copy-start = (f32[16,512]{1,0:T(8,128)S(1)}, f32[16,512]{1,0:T(8,128)}, u32[]{:S(2)}) copy-start(f32[16,512]{1,0:T(8,128)} %get-tuple-element.75) | copy-start | bytes 98308
